TPU v7x, 32 devices: a whole 2x2x4 slice. The times are simulated.
32 devices in a mesh: dp: 16 (over z, x, core), seq: 2 (over y).
Axes of the slice: x: 2, y: 2, z: 4, core: 2. Of those that a mesh axis runs over, the one named last changes fastest.
Arguments:
- tokens: bfloat16 [16, 1024, 1280], P('dp', 'seq'), may hold values from -6 to 6
- adapter_index: int32 [16], P('dp'), may hold values from 0 to 7
- norm1_gain: bfloat16 [1280], P(('dp', 'seq')), may hold values from 0.5 to 1.5
- norm1_bias: bfloat16 [1280], P(('dp', 'seq')), may hold values from -1.5 to 1.5
- qkv_weight: bfloat16 [1280, 3840], P(('dp', 'seq')), may hold values from -0.15625 to 0.15625
- qkv_bias: bfloat16 [3840], P(('dp', 'seq')), may hold values from -1.5 to 1.5
- proj_weight: bfloat16 [1280, 1280], P(('dp', 'seq')), may hold values from -0.625 to 0.625
- proj_bias: bfloat16 [1280], P(('dp', 'seq')), may hold values from -1.5 to 1.5
- norm2_gain: bfloat16 [1280], P(('dp', 'seq')), may hold values from 0.5 to 1.5
- norm2_bias: bfloat16 [1280], P(('dp', 'seq')), may hold values from -1.5 to 1.5
- fc1_weight: bfloat16 [1280, 5120], P(('dp', 'seq')), may hold values from -0.15625 to 0.15625
- fc1_bias: bfloat16 [5120], P(('dp', 'seq')), may hold values from -1.5 to 1.5
- fc2_weight: bfloat16 [5120, 1280], P(('dp', 'seq')), may hold values from -0.078125 to 0.078125
- fc2_bias: bfloat16 [1280], P(('dp', 'seq')), may hold values from -1.5 to 1.5
- rel_pos_h: bfloat16 [63, 80], replicated, may hold values from -0.8984375 to 0.8984375
- rel_pos_w: bfloat16 [63, 80], replicated, may hold values from -0.8984375 to 0.8984375
- qkv_down: bfloat16 [1280, 128], P(('dp', 'seq')), may hold values from -0.15625 to 0.15625
- qkv_up: bfloat16 [128, 3840], P(None, ('dp', 'seq')), may hold values from -1.5 to 1.5
- proj_down: bfloat16 [1280, 128], P(('dp', 'seq')), may hold values from -0.625 to 0.625
- proj_up: bfloat16 [128, 1280], P(None, ('dp', 'seq')), may hold values from -1.5 to 1.5
- fc1_down: bfloat16 [1280, 128], P(('dp', 'seq')), may hold values from -0.15625 to 0.15625
- fc1_up: bfloat16 [128, 5120], P(None, ('dp', 'seq')), may hold values from -1.5 to 1.5
- fc2_down: bfloat16 [5120, 128], P(('dp', 'seq')), may hold values from -0.078125 to 0.078125
- fc2_up: bfloat16 [128, 1280], P(None, ('dp', 'seq')), may hold values from -1.5 to 1.5
- out_grad: bfloat16 [16, 1024, 1280], P('dp', 'seq'), may hold values from -6 to 6
Outputs:
- block_out: bfloat16 [16, 1024, 1280], P('dp', 'seq')
- input_grad: float32 [16, 1024, 1280], P('dp', 'seq')
- qkv_down_grad: float32 [1280, 128], P(('dp', 'seq'))
- qkv_up_grad: float32 [128, 3840], P(None, ('dp', 'seq'))
- proj_down_grad: float32 [1280, 128], P(('dp', 'seq'))
- proj_up_grad: float32 [128, 1280], P(None, ('dp', 'seq'))
- fc1_down_grad: float32 [1280, 128], P(('dp', 'seq'))
- fc1_up_grad: float32 [128, 5120], P(None, ('dp', 'seq'))
- fc2_down_grad: float32 [5120, 128], P(('dp', 'seq'))
- fc2_up_grad: float32 [128, 1280], P(None, ('dp', 'seq'))
All inputs are finite; a program needn't handle non-finite values.
Results may differ from a plain program's by a relative error of at most 0.015.
Values may be sent and summed in bfloat16 or wider, within the bound.
A program may use at most 512 MiB of HBM per device.

v0:
```python
import jax
import jax.numpy as jnp
from jax import lax
from jax.sharding import PartitionSpec as P

HEADS = 16
HEAD_DIM = 80
ADAPTERS = 8
RANK = 16
G = 32


epsilon = 1e-06
adapter_scale = 0.5
highest = lax.Precision.HIGHEST


def matmul(left, right):
    return jnp.dot(left, right, preferred_element_type=jnp.float32)


def times_transposed(left, right):
    return lax.dot_general(
        left, right, (((1,), (1,)), ((), ())), preferred_element_type=jnp.float32
    )


def column_sums(left, right):
    return lax.dot_general(
        left, right, (((0,), (0,)), ((), ())), preferred_element_type=jnp.float32
    )


def layer_norm(values, gain, shift):
    average = jnp.mean(values, axis=-1, keepdims=True)
    centered = values - average
    variance = jnp.mean(centered * centered, axis=-1, keepdims=True)
    inverse = lax.rsqrt(variance + epsilon)
    normed = centered * inverse
    return (normed * gain + shift, normed, inverse)


def norm_back(upstream, gain, normed, inverse):
    scaled = upstream * gain
    return inverse * (
        scaled
        - jnp.mean(scaled, axis=-1, keepdims=True)
        - normed * jnp.mean(scaled * normed, axis=-1, keepdims=True)
    )


def adapter_forward(source, downward, upward, row_mask):
    middle = (matmul(source, downward) * row_mask).astype(jnp.bfloat16)
    return (middle, adapter_scale * matmul(middle, upward))


def adapter_backward(upstream, source, middle, downward, upward, row_mask):
    grad_middle = (adapter_scale * times_transposed(upstream, upward) * row_mask).astype(
        jnp.bfloat16
    )
    grad_down = column_sums(source, grad_middle)
    grad_upward = adapter_scale * column_sums(middle, upstream)
    return (times_transposed(grad_middle, downward), grad_down, grad_upward)


def rel_rows(lookup, query_places, key_places):
    offsets = query_places[:, None] - key_places[None, :] + G - 1
    onehot = (offsets[:, :, None] == jnp.arange(2 * G - 1, dtype=jnp.int32)[None, None, :]).astype(
        jnp.bfloat16
    )
    return jnp.einsum("qkr,rc->qkc", onehot, lookup, preferred_element_type=jnp.float32).astype(
        jnp.bfloat16
    )


def score_block(queries, key_rows, rel_local, rel_wide):
    query_count = queries.shape[0]
    grid_rows = query_count // G
    length = key_rows.shape[0]
    key_grid = length // G
    heads_query = queries.reshape(query_count, HEADS, HEAD_DIM)
    heads_key = key_rows.reshape(length, HEADS, HEAD_DIM)
    scores = jnp.einsum(
        "qnc,knc->nqk", heads_query, heads_key, preferred_element_type=jnp.float32
    ) * HEAD_DIM ** (-0.5)
    grid_query = queries.reshape(grid_rows, G, HEADS, HEAD_DIM)
    along_h = jnp.einsum(
        "xwnc,xkc->nxwk", grid_query, rel_local, preferred_element_type=jnp.float32
    )
    along_w = jnp.einsum("xwnc,wkc->nxwk", grid_query, rel_wide, preferred_element_type=jnp.float32)
    scores = (
        scores.reshape(HEADS, grid_rows, G, key_grid, G)
        + along_h[..., None]
        + along_w[:, :, :, None, :]
    )
    return scores.reshape(HEADS, query_count, length)


def attend_forward(queries, key_value, rel_local, rel_wide):
    features = queries.shape[1]
    scores = score_block(queries, key_value[:, :features], rel_local, rel_wide)
    top_score = jnp.max(scores, axis=-1, keepdims=True)
    totals = top_score + jnp.log(jnp.sum(jnp.exp(scores - top_score), axis=-1, keepdims=True))
    shares = jnp.exp(scores - totals).astype(jnp.bfloat16)
    value_rows = key_value[:, features:].reshape(key_value.shape[0], HEADS, HEAD_DIM)
    attended = jnp.einsum("nqk,knc->qnc", shares, value_rows, preferred_element_type=jnp.float32)
    return (attended.reshape(queries.shape[0], features).astype(jnp.bfloat16), totals)


def score_grads(queries, key_value, grad_attended, totals, inner, rel_local, rel_wide):
    features = queries.shape[1]
    query_count = queries.shape[0]
    length = key_value.shape[0]
    scores = score_block(queries, key_value[:, :features], rel_local, rel_wide)
    shares_full = jnp.exp(scores - totals)
    heads_value = key_value[:, features:].reshape(length, HEADS, HEAD_DIM)
    heads_grad = grad_attended.reshape(query_count, HEADS, HEAD_DIM)
    grad_shares = jnp.einsum(
        "qnc,knc->nqk", heads_grad, heads_value, preferred_element_type=jnp.float32
    )
    inner = jnp.sum(shares_full * grad_shares, axis=-1, keepdims=True)
    grad_scores = (shares_full * (grad_shares - inner)).astype(jnp.bfloat16)
    return (shares_full, grad_scores, inner)


def query_part(key_value, grad_scores, query_count, rel_local, rel_wide):
    features = key_value.shape[1] // 2
    grid_rows = query_count // G
    length = key_value.shape[0]
    heads_key = key_value[:, :features].reshape(length, HEADS, HEAD_DIM)
    grad_query = jnp.einsum(
        "nqk,knc->qnc", grad_scores, heads_key, preferred_element_type=jnp.float32
    ) * HEAD_DIM ** (-0.5)
    grid_scores = grad_scores.reshape(HEADS, grid_rows, G, G, G)
    sum_rows = jnp.sum(grid_scores, axis=4, dtype=jnp.float32)
    sum_columns = jnp.sum(grid_scores, axis=3, dtype=jnp.float32)
    rel_part = jnp.einsum(
        "nxwk,xkc->xwnc", sum_rows, rel_local.astype(jnp.float32), precision=highest
    )
    rel_part = rel_part + jnp.einsum(
        "nxwk,wkc->xwnc", sum_columns, rel_wide.astype(jnp.float32), precision=highest
    )
    grad_query = grad_query + rel_part.reshape(query_count, HEADS, HEAD_DIM)
    return grad_query.reshape(query_count, features)


def key_part(queries, grad_attended, shares_full, grad_scores, length):
    features = queries.shape[1]
    query_count = queries.shape[0]
    heads_query = queries.reshape(query_count, HEADS, HEAD_DIM)
    heads_grad = grad_attended.reshape(query_count, HEADS, HEAD_DIM)
    shares = shares_full.astype(jnp.bfloat16)
    grad_key = jnp.einsum(
        "nqk,qnc->knc", grad_scores, heads_query, preferred_element_type=jnp.float32
    ) * HEAD_DIM ** (-0.5)
    grad_value = jnp.einsum("nqk,qnc->knc", shares, heads_grad, preferred_element_type=jnp.float32)
    return jnp.concatenate(
        [grad_key.reshape(length, features), grad_value.reshape(length, features)], axis=-1
    )


def attend_backward(queries, key_value, grad_attended, totals, rel_local, rel_wide):
    shares_full, grad_scores, inner = score_grads(
        queries, key_value, grad_attended, totals, None, rel_local, rel_wide
    )
    grad_query = query_part(key_value, grad_scores, queries.shape[0], rel_local, rel_wide)
    grad_pairs = key_part(queries, grad_attended, shares_full, grad_scores, key_value.shape[0])
    return (grad_query, grad_pairs)


def per_device(
    tokens,
    adapter_index,
    norm1_gain,
    norm1_bias,
    qkv_weight,
    qkv_bias,
    proj_weight,
    proj_bias,
    norm2_gain,
    norm2_bias,
    fc1_weight,
    fc1_bias,
    fc2_weight,
    fc2_bias,
    rel_pos_h,
    rel_pos_w,
    qkv_down,
    qkv_up,
    proj_down,
    proj_up,
    fc1_down,
    fc1_up,
    fc2_down,
    fc2_up,
    out_grad,
):
    gathered = (
        lax.all_gather(norm1_gain, ("dp", "seq"), axis=0, tiled=True),
        lax.all_gather(norm1_bias, ("dp", "seq"), axis=0, tiled=True),
        lax.all_gather(qkv_weight, ("dp", "seq"), axis=0, tiled=True),
        lax.all_gather(qkv_bias, ("dp", "seq"), axis=0, tiled=True),
        lax.all_gather(proj_weight, ("dp", "seq"), axis=0, tiled=True),
        lax.all_gather(proj_bias, ("dp", "seq"), axis=0, tiled=True),
        lax.all_gather(norm2_gain, ("dp", "seq"), axis=0, tiled=True),
        lax.all_gather(norm2_bias, ("dp", "seq"), axis=0, tiled=True),
        lax.all_gather(fc1_weight, ("dp", "seq"), axis=0, tiled=True),
        lax.all_gather(fc1_bias, ("dp", "seq"), axis=0, tiled=True),
        lax.all_gather(fc2_weight, ("dp", "seq"), axis=0, tiled=True),
        lax.all_gather(fc2_bias, ("dp", "seq"), axis=0, tiled=True),
        lax.all_gather(qkv_down, ("dp", "seq"), axis=0, tiled=True),
        lax.all_gather(qkv_up, ("dp", "seq"), axis=1, tiled=True),
        lax.all_gather(proj_down, ("dp", "seq"), axis=0, tiled=True),
        lax.all_gather(proj_up, ("dp", "seq"), axis=1, tiled=True),
        lax.all_gather(fc1_down, ("dp", "seq"), axis=0, tiled=True),
        lax.all_gather(fc1_up, ("dp", "seq"), axis=1, tiled=True),
        lax.all_gather(fc2_down, ("dp", "seq"), axis=0, tiled=True),
        lax.all_gather(fc2_up, ("dp", "seq"), axis=1, tiled=True),
    )
    images, part_len, features = tokens.shape
    row_count = images * part_len
    ranks = ADAPTERS * RANK
    columns = jnp.arange(ranks, dtype=jnp.int32) // RANK
    picked = (columns[None, :] == adapter_index[:, None]).astype(jnp.float32)
    row_mask = jnp.broadcast_to(picked[:, None, :], (images, part_len, ranks)).reshape(
        row_count, ranks
    )
    inputs = tokens.reshape(row_count, features).astype(jnp.float32)
    out_one, normed_one, inverse_one = layer_norm(
        inputs, gathered[0].astype(jnp.float32), gathered[1].astype(jnp.float32)
    )
    act_one = out_one.astype(jnp.bfloat16)
    mid_qkv, delta_qkv = adapter_forward(act_one, gathered[12], gathered[13], row_mask)
    qkv_rows = (matmul(act_one, gathered[2]) + gathered[3].astype(jnp.float32) + delta_qkv).astype(
        jnp.bfloat16
    )
    queries = qkv_rows[:, :features].reshape(images, part_len, features)
    kv_local = qkv_rows[:, features:].reshape(images, part_len, 2 * features)
    kv_full = lax.all_gather(kv_local, "seq", axis=1, tiled=True)
    grid_rows = part_len // G
    first_row = lax.axis_index("seq") * grid_rows
    own_rows = first_row + jnp.arange(grid_rows, dtype=jnp.int32)
    every_row = jnp.arange(G, dtype=jnp.int32)
    rel_local = rel_rows(rel_pos_h, own_rows, every_row)
    rel_wide = rel_rows(rel_pos_w, every_row, every_row)
    attended, totals = lax.map(
        lambda members: attend_forward(members[0], members[1], rel_local, rel_wide),
        (queries, kv_full),
    )
    att_rows = attended.reshape(row_count, features)
    mid_proj, delta_proj = adapter_forward(att_rows, gathered[14], gathered[15], row_mask)
    branch = matmul(att_rows, gathered[4]) + gathered[5].astype(jnp.float32) + delta_proj
    residual = inputs + branch
    out_two, normed_two, inverse_two = layer_norm(
        residual, gathered[6].astype(jnp.float32), gathered[7].astype(jnp.float32)
    )
    act_two = out_two.astype(jnp.bfloat16)
    mid_fc1, delta_fc1 = adapter_forward(act_two, gathered[16], gathered[17], row_mask)
    hidden = matmul(act_two, gathered[8]) + gathered[9].astype(jnp.float32) + delta_fc1
    activated = jax.nn.gelu(hidden, approximate=False).astype(jnp.bfloat16)
    mid_fc2, delta_fc2 = adapter_forward(activated, gathered[18], gathered[19], row_mask)
    final = (
        residual + matmul(activated, gathered[10]) + gathered[11].astype(jnp.float32) + delta_fc2
    )
    block_out = final.astype(jnp.bfloat16).reshape(images, part_len, features)
    weights_back = (
        lax.all_gather(norm1_gain, ("dp", "seq"), axis=0, tiled=True),
        lax.all_gather(norm1_bias, ("dp", "seq"), axis=0, tiled=True),
        lax.all_gather(qkv_weight, ("dp", "seq"), axis=0, tiled=True),
        lax.all_gather(qkv_bias, ("dp", "seq"), axis=0, tiled=True),
        lax.all_gather(proj_weight, ("dp", "seq"), axis=0, tiled=True),
        lax.all_gather(proj_bias, ("dp", "seq"), axis=0, tiled=True),
        lax.all_gather(norm2_gain, ("dp", "seq"), axis=0, tiled=True),
        lax.all_gather(norm2_bias, ("dp", "seq"), axis=0, tiled=True),
        lax.all_gather(fc1_weight, ("dp", "seq"), axis=0, tiled=True),
        lax.all_gather(fc1_bias, ("dp", "seq"), axis=0, tiled=True),
        lax.all_gather(fc2_weight, ("dp", "seq"), axis=0, tiled=True),
        lax.all_gather(fc2_bias, ("dp", "seq"), axis=0, tiled=True),
        lax.all_gather(qkv_down, ("dp", "seq"), axis=0, tiled=True),
        lax.all_gather(qkv_up, ("dp", "seq"), axis=1, tiled=True),
        lax.all_gather(proj_down, ("dp", "seq"), axis=0, tiled=True),
        lax.all_gather(proj_up, ("dp", "seq"), axis=1, tiled=True),
        lax.all_gather(fc1_down, ("dp", "seq"), axis=0, tiled=True),
        lax.all_gather(fc1_up, ("dp", "seq"), axis=1, tiled=True),
        lax.all_gather(fc2_down, ("dp", "seq"), axis=0, tiled=True),
        lax.all_gather(fc2_up, ("dp", "seq"), axis=1, tiled=True),
    )
    grad_out = out_grad.reshape(row_count, features)
    back_fc2, down_fc2, upper_fc2 = adapter_backward(
        grad_out, activated, mid_fc2, weights_back[18], weights_back[19], row_mask
    )
    grad_act = times_transposed(grad_out, weights_back[10]) + back_fc2
    cumulative = 0.5 * (1.0 + lax.erf(hidden * 2.0 ** (-0.5)))
    density = jnp.exp(-0.5 * hidden * hidden) * (2.0 * jnp.pi) ** (-0.5)
    grad_hidden = (grad_act * (cumulative + hidden * density)).astype(jnp.bfloat16)
    back_fc1, down_fc1, upper_fc1 = adapter_backward(
        grad_hidden, act_two, mid_fc1, weights_back[16], weights_back[17], row_mask
    )
    grad_norm_two = times_transposed(grad_hidden, weights_back[8]) + back_fc1
    grad_resid = grad_out.astype(jnp.float32) + norm_back(
        grad_norm_two, weights_back[6].astype(jnp.float32), normed_two, inverse_two
    )
    grad_branch = grad_resid.astype(jnp.bfloat16)
    back_proj, down_proj, upper_proj = adapter_backward(
        grad_branch, att_rows, mid_proj, weights_back[14], weights_back[15], row_mask
    )
    grad_att = (times_transposed(grad_branch, weights_back[4]) + back_proj).astype(jnp.bfloat16)
    grad_att = grad_att.reshape(images, part_len, features)
    grad_query, grad_pairs = lax.map(
        lambda members: attend_backward(
            members[0], members[1], members[2], members[3], rel_local, rel_wide
        ),
        (queries, kv_full, grad_att, totals),
    )
    grad_kv = lax.psum_scatter(
        grad_pairs.astype(jnp.bfloat16), "seq", scatter_dimension=1, tiled=True
    ).astype(jnp.float32)
    grad_qkv = (
        jnp.concatenate([grad_query, grad_kv], axis=-1)
        .reshape(row_count, 3 * features)
        .astype(jnp.bfloat16)
    )
    back_qkv, down_qkv, upper_qkv = adapter_backward(
        grad_qkv, act_one, mid_qkv, weights_back[12], weights_back[13], row_mask
    )
    grad_norm_one = times_transposed(grad_qkv, weights_back[2]) + back_qkv
    input_grad = grad_resid + norm_back(
        grad_norm_one, weights_back[0].astype(jnp.float32), normed_one, inverse_one
    )
    summed = (
        lax.psum_scatter(down_qkv, ("dp", "seq"), scatter_dimension=0, tiled=True),
        lax.psum_scatter(upper_qkv, ("dp", "seq"), scatter_dimension=1, tiled=True),
        lax.psum_scatter(down_proj, ("dp", "seq"), scatter_dimension=0, tiled=True),
        lax.psum_scatter(upper_proj, ("dp", "seq"), scatter_dimension=1, tiled=True),
        lax.psum_scatter(down_fc1, ("dp", "seq"), scatter_dimension=0, tiled=True),
        lax.psum_scatter(upper_fc1, ("dp", "seq"), scatter_dimension=1, tiled=True),
        lax.psum_scatter(down_fc2, ("dp", "seq"), scatter_dimension=0, tiled=True),
        lax.psum_scatter(upper_fc2, ("dp", "seq"), scatter_dimension=1, tiled=True),
    )
    return (
        block_out,
        input_grad.reshape(images, part_len, features),
        summed[0],
        summed[1],
        summed[2],
        summed[3],
        summed[4],
        summed[5],
        summed[6],
        summed[7],
    )


def solution(mesh):
    return jax.shard_map(
        per_device,
        mesh=mesh,
        in_specs=(
            P("dp", "seq", None),
            P("dp"),
            P(("dp", "seq")),
            P(("dp", "seq")),
            P(("dp", "seq"), None),
            P(("dp", "seq")),
            P(("dp", "seq"), None),
            P(("dp", "seq")),
            P(("dp", "seq")),
            P(("dp", "seq")),
            P(("dp", "seq"), None),
            P(("dp", "seq")),
            P(("dp", "seq"), None),
            P(("dp", "seq")),
            P(),
            P(),
            P(("dp", "seq"), None),
            P(None, ("dp", "seq")),
            P(("dp", "seq"), None),
            P(None, ("dp", "seq")),
            P(("dp", "seq"), None),
            P(None, ("dp", "seq")),
            P(("dp", "seq"), None),
            P(None, ("dp", "seq")),
            P("dp", "seq", None),
        ),
        out_specs=(
            P("dp", "seq", None),
            P("dp", "seq", None),
            P(("dp", "seq"), None),
            P(None, ("dp", "seq")),
            P(("dp", "seq"), None),
            P(None, ("dp", "seq")),
            P(("dp", "seq"), None),
            P(None, ("dp", "seq")),
            P(("dp", "seq"), None),
            P(None, ("dp", "seq")),
        ),
        check_vma=False,
    )
```

profile of v0, /device:TPU:15, one launch (start us, length us, event | category | flops | bytes accessed | tf_op | source)
XLA Modules:
  0.0 2179.4 jit_solution(1386474633665715667)
XLA Ops:
  14.8 41.0 %all-reduce.14 = (bf16[1280]{0:T(1024)(128)(2,1)S(1)}, bf16[1280]{0:T(1024)(128)(2,1)S(1)}, bf16[3840]{0:T(1024)(128)(2,1)S(1)}, bf16[1280]{0:T(1024)(128)(2,1)S...) all-reduce(bf16[1280]{0:T(1024)(128)(2,1)S(1)} %dynamic-update-slic, ...), channel_id=1, replica_groups=mesh['dp'=16,'seq'=2] {'dp','seq'}, use_global_device_ids=true, to_apply=%add.1 | all-reduce | flops 16640 | bytes 66560
  56.5 55.2 %all_gather.81 = bf16[1280,128]{1,0:T(8,128)(2,1)S(1)} all-gather(bf16[40,128]{1,0:T(8,128)(2,1)} %param.41), channel_id=1, replica_groups=mesh['dp'=16,'seq'=2] {'dp','seq'}, dimensions={0}, use_global_device_ids=true | all-gather | bytes 337920 | tf_op jit(solution)/shard_map/all_gather | solution.py:211
  116.4 61.1 %all_gather.82 = bf16[128,3840]{0,1:T(8,128)(2,1)S(1)} all-gather(bf16[128,120]{0,1:T(8,128)(2,1)S(1)} %copy-done.56), channel_id=1, replica_groups=mesh['dp'=16,'seq'=2] {'dp','seq'}, dimensions={1}, use_global_device_ids=true | all-gather | bytes 1013760 | tf_op jit(solution)/shard_map/all_gather | solution.py:212
  194.4 74.3 %all_gather.86 = bf16[1280,128]{1,0:T(8,128)(2,1)} all-gather(bf16[40,128]{1,0:T(8,128)(2,1)S(1)} %copy-done.59), channel_id=1, replica_groups=mesh['dp'=16,'seq'=2] {'dp','seq'}, dimensions={0}, use_global_device_ids=true | all-gather | bytes 337920 | tf_op jit(solution)/shard_map/all_gather | solution.py:213
  268.7 70.2 %all_gather.87 = bf16[128,1280]{0,1:T(8,128)(2,1)} all-gather(bf16[128,40]{0,1:T(8,128)(2,1)S(1)} %copy-done.60), channel_id=1, replica_groups=mesh['dp'=16,'seq'=2] {'dp','seq'}, dimensions={1}, use_global_device_ids=true | all-gather | bytes 337920 | tf_op jit(solution)/shard_map/all_gather | solution.py:214
  340.2 71.2 %all_gather.92 = bf16[1280,128]{1,0:T(8,128)(2,1)} all-gather(bf16[40,128]{1,0:T(8,128)(2,1)S(1)} %copy-done.61), channel_id=1, replica_groups=mesh['dp'=16,'seq'=2] {'dp','seq'}, dimensions={0}, use_global_device_ids=true | all-gather | bytes 337920 | tf_op jit(solution)/shard_map/all_gather | solution.py:215
  412.0 67.8 %all_gather.97 = bf16[128,1280]{0,1:T(8,128)(2,1)S(1)} all-gather(bf16[128,40]{0,1:T(8,128)(2,1)S(1)} %copy-done.62), channel_id=1, replica_groups=mesh['dp'=16,'seq'=2] {'dp','seq'}, dimensions={1}, use_global_device_ids=true | all-gather | bytes 337920 | tf_op jit(solution)/shard_map/all_gather | solution.py:218
  492.9 41.8 %add.238 = f32[16,16,32,32,32]{4,3,2,1,0:T(8,128)} broadcast(f32[16,16,32,32]{3,2,1,0:T(8,128)S(1)} %copy.66), dimensions={0,1,2,4} | broadcast | bytes 34603008 | tf_op jit(solution)/shard_map/while/body/eval_jaxpr/add | solution.py:92
  534.7 101.7 %add.239 = f32[16,512,1024]{2,1,0:T(8,128)} reshape(f32[16,16,32,32,32]{4,3,2,1,0:T(8,128)} %add.238) | data formatting | bytes 67108864 | tf_op jit(solution)/shard_map/while/body/eval_jaxpr/add | solution.py:92
  646.9 44.6 %add.235 = f32[16,16,32,32,32]{4,3,2,1,0:T(8,128)} broadcast(f32[16,16,32,32]{3,2,1,0:T(8,128)} %copy.64), dimensions={0,1,2,3} | broadcast | bytes 34603008 | tf_op jit(solution)/shard_map/while/body/eval_jaxpr/add | solution.py:92
  691.5 100.5 %add.236 = f32[16,512,1024]{2,1,0:T(8,128)} reshape(f32[16,16,32,32,32]{4,3,2,1,0:T(8,128)} %add.235) | data formatting | bytes 67108864 | tf_op jit(solution)/shard_map/while/body/eval_jaxpr/add | solution.py:92
  802.3 36.0 %fusion.93 = (f32[16,512]{1,0:T(8,128)S(1)}, f32[16,512,1024]{2,1,0:T(8,128)}) fusion(f32[16,512,1024]{2,1,0:T(8,128)} %add.239, f32[16,512,1024]{2,1,0:T(8,128)} %add.236, bf16[512,16,80]{0,2,1:T(8,128)(2,1)} %bitcast.179, bf16[1024,16,80]{0,2,1:T(8,128)(2,1)S(1)} %bitcast.175), kind=kOutput, calls=%fused_computation.152 | convolution fusion | flops 1375723520 | bytes 104628224 | tf_op jit(solution)/shard_map/while/body/eval_jaxpr/qnc,knc->nqk/dot_general | solution.py:83
  838.3 14.4 exponential_reduce_fusion
  852.8 14.4 fusion.54
  876.9 14.7 fusion.96
  891.6 27.6 %fusion.3 = (bf16[512,5120]{1,0:T(8,128)(2,1)}, f32[512,5120]{1,0:T(8,128)}) fusion(bf16[512,128]{1,0:T(8,128)(2,1)S(1)} %fusion.70, bf16[128,5120]{0,1:T(8,128)(2,1)} %all-gather.15.cloned.1.call-done, f32[512,5120]{1,0:T(8,128)} %fusion.96, f32[5120]{0:T(1024)S(1)} %copy-done.57), kind=kOutput, calls=%fused_computation.10 | convolution fusion | flops 849346560 | bytes 27676672 | tf_op jit(solution)/shard_map/dot_general | solution.py:19
  919.3 14.4 fusion.60
  943.6 12.4 fusion.97
  966.3 15.0 fusion.51
  981.3 22.3 %multiply_reduce_fusion = (f32[16,512]{1,0:T(8,128)S(1)}, f32[16,512,1024]{2,1,0:T(8,128)}) fusion(f32[16,512,1024]{2,1,0:T(8,128)} %get-tuple-element.75, f32[16,512]{1,0:T(8,128)S(1)} %log_add_fusion, bf16[512,16,80]{0,2,1:T(8,128)(2,1)S(1)} %bitcast.185, bf16[1024,16,80]{0,2,1:T(8,128)(2,1)S(1)} %bitcast.178), kind=kOutput, calls=%fused_computation.1 | convolution fusion | flops 1367334912 | bytes 71106560 | tf_op jit(solution)/shard_map/while/body/eval_jaxpr/qnc,knc->nqk/dot_general | solution.py:118
  1003.6 28.1 %multiply_convert_fusion = bf16[16,512,1024]{2,1,0:T(8,128)(2,1)} fusion(f32[16,512,1024]{2,1,0:T(8,128)} %get-tuple-element.82, f32[16,512,1024]{2,1,0:T(8,128)} %get-tuple-element.75, f32[16,512]{1,0:T(8,128)S(1)} %get-tuple-element.81, f32[16,512]{1,0:T(8,128)S(1)} %log_add_fusion), kind=kLoop, calls=%fused_computation | loop fusion | flops 33554432 | bytes 83951616 | tf_op jit(solution)/shard_map/while/body/eval_jaxpr/convert_element_type | solution.py:122
  1063.3 79.9 %reshape.276 = f32[16,16,32,32,32]{4,3,2,1,0:T(8,128)} reshape(bf16[16,512,1024]{2,1,0:T(8,128)(2,1)} %multiply_convert_fusion) | data formatting | bytes 50331648 | tf_op jit(solution)/shard_map/while/body/eval_jaxpr/convert_element_type | solution.py:135
  1148.9 45.5 %fusion.89 = (f32[16,16,32,32]{3,2,1,0:T(8,128)}, f32[16,16,32,32]{3,2,1,0:T(8,128)}) fusion(f32[16,16,32,32,32]{4,3,2,1,0:T(8,128)} %reshape.276), kind=kLoop, calls=%fused_computation.148 | loop fusion | flops 16252928 | bytes 35651584 | tf_op jit(solution)/shard_map/while/body/eval_jaxpr/reduce_sum | solution.py:135
  1216.4 12.8 fusion.46
  1234.5 11.6 fusion.28
  1265.4 107.8 %reduce-scatter.39.cloned.1.call-done = f32[128,40]{0,1:T(8,128)} async-done(((f32[128,1280]{0,1:T(8,128)}), f32[128,40]{0,1:T(8,128)}) %reduce-scatter.39.cloned.1.call-update) | async-done | bytes 20496
  1373.3 133.2 %reduce-scatter.41.cloned.1.call-done = f32[40,128]{1,0:T(8,128)} async-done(((f32[1280,128]{1,0:T(8,128)}), f32[40,128]{1,0:T(8,128)}) %reduce-scatter.41.cloned.1.call-update) | async-done | bytes 20496
  1506.5 132.9 %reduce-scatter.43.cloned.1.call-done = f32[128,40]{0,1:T(8,128)} async-done(((f32[128,1280]{0,1:T(8,128)}), f32[128,40]{0,1:T(8,128)}) %reduce-scatter.43.cloned.1.call-update) | async-done | bytes 20496
  1639.5 138.4 %reduce-scatter.29.cloned.1.call-done = f32[128,160]{0,1:T(8,128)} async-done(((f32[128,5120]{0,1:T(8,128)}), f32[128,160]{0,1:T(8,128)}) %reduce-scatter.29.cloned.1.call-update) | async-done | bytes 81936 | tf_op jit(solution)/shard_map/reduce_scatter | solution.py:336
  1777.8 137.4 %reduce-scatter.31.cloned.1.call-done = f32[160,128]{1,0:T(8,128)} async-done(((f32[5120,128]{1,0:T(8,128)}), f32[160,128]{1,0:T(8,128)}) %reduce-scatter.31.cloned.1.call-update) | async-done | bytes 81936 | tf_op jit(solution)/shard_map/reduce_scatter | solution.py:337
  1915.3 132.8 %reduce-scatter.33.cloned.1.call-done = f32[40,128]{1,0:T(8,128)} async-done(((f32[1280,128]{1,0:T(8,128)}), f32[40,128]{1,0:T(8,128)}) %reduce-scatter.33.cloned.1.call-update) | async-done | bytes 20496
  2048.1 124.5 %reduce-scatter.35.cloned.1.call-done = f32[128,120]{0,1:T(8,128)} async-done(((f32[128,3840]{0,1:T(8,128)}), f32[128,120]{0,1:T(8,128)}) %reduce-scatter.35.cloned.1.call-update) | async-done | bytes 61456
  (281 shorter events, 177.5 us)
Async XLA Ops:
  7.2 472.6 %copy-start = (bf16[63,80]{1,0:T(8,128)(2,1)S(1)}, bf16[63,80]{1,0:T(8,128)(2,1)}, u32[]{:S(2)}) copy-start(bf16[63,80]{1,0:T(8,128)(2,1)} %param.40) | copy-start | bytes 30244
  7.2 108.0 %copy-start.4 = (bf16[1,512,1280]{2,1,0:T(8,128)(2,1)S(1)}, bf16[1,512,1280]{2,1,0:T(8,128)(2,1)}, u32[]{:S(2)}) copy-start(bf16[1,512,1280]{2,1,0:T(8,128)(2,1)} %param.25) | copy-start | bytes 3932164
  7.2 109.2 %copy-start.56 = (bf16[128,120]{0,1:T(8,128)(2,1)S(1)}, bf16[128,120]{0,1:T(8,128)(2,1)}, u32[]{:S(2)}) copy-start(bf16[128,120]{0,1:T(8,128)(2,1)} %param.42) | copy-start | bytes 92164
  7.2 170.3 %all-gather.9.cloned.1.call-start = ((), (), s32[]{:S(2)}) async-start(), calls=%async_computation.9 | async-start | bytes 10137600 | tf_op jit(solution)/shard_map/all_gather | solution.py:201
  7.9 784.1 %all-gather.21.cloned.1.call-start = ((), (), s32[]{:S(2)}) async-start(), calls=%async_computation.18 | async-start | bytes 7864320 | tf_op jit(solution)/shard_map/all_gather | solution.py:239
  55.8 60.5 %copy-start.48 = (f32[1280]{0:T(1024)}, f32[1280]{0:T(1024)S(1)}, u32[]{:S(2)}) copy-start(f32[1280]{0:T(1024)S(1)} %convert_element_type.148) | copy-start | bytes 15364
  56.5 59.8 %copy-start.64 = (f32[128]{0:T(128)}, f32[128]{0:T(128)S(1)}, u32[]{:S(2)}) copy-start(f32[128]{0:T(128)S(1)} %compare_convert_fusion) | copy-start | bytes 1540
  115.8 69.7 %copy-start.17 = (bf16[512,1280]{1,0:T(8,128)(2,1)}, bf16[512,1280]{1,0:T(8,128)(2,1)S(1)}, u32[]{:S(2)}) copy-start(bf16[512,1280]{1,0:T(8,128)(2,1)S(1)} %fusion.39) | copy-start | bytes 3932164
  116.4 69.2 %copy-start.42 = (bf16[512,128]{1,0:T(8,128)(2,1)}, bf16[512,128]{1,0:T(8,128)(2,1)S(1)}, u32[]{:S(2)}) copy-start(bf16[512,128]{1,0:T(8,128)(2,1)S(1)} %fusion.68) | copy-start | bytes 393220
  188.7 80.0 %copy-start.60 = (bf16[128,40]{0,1:T(8,128)(2,1)S(1)}, bf16[128,40]{0,1:T(8,128)(2,1)}, u32[]{:S(2)}) copy-start(bf16[128,40]{0,1:T(8,128)(2,1)} %param.44) | copy-start | bytes 30724
  188.7 151.5 %copy-start.61 = (bf16[40,128]{1,0:T(8,128)(2,1)S(1)}, bf16[40,128]{1,0:T(8,128)(2,1)}, u32[]{:S(2)}) copy-start(bf16[40,128]{1,0:T(8,128)(2,1)} %param.45) | copy-start | bytes 30724
  188.7 223.3 %copy-start.62 = (bf16[128,40]{0,1:T(8,128)(2,1)S(1)}, bf16[128,40]{0,1:T(8,128)(2,1)}, u32[]{:S(2)}) copy-start(bf16[128,40]{0,1:T(8,128)(2,1)} %param.48) | copy-start | bytes 30724
  190.4 290.5 %copy-start.58 = (bf16[63,80]{1,0:T(8,128)(2,1)S(1)}, bf16[63,80]{1,0:T(8,128)(2,1)}, u32[]{:S(2)}) copy-start(bf16[63,80]{1,0:T(8,128)(2,1)} %param.39) | copy-start | bytes 30244
  190.4 290.7 %copy-start.20 = (bf16[1,512,1280]{2,1,0:T(8,128)(2,1)S(1)}, bf16[1,512,1280]{2,1,0:T(8,128)(2,1)}, u32[]{:S(2)}) copy-start(bf16[1,512,1280]{2,1,0:T(8,128)(2,1)} %param.49) | copy-start | bytes 3932164
  190.4 678.7 %all-gather.11.cloned.1.call-start = ((), (), s32[]{:S(2)}) async-start(), calls=%async_computation.10 | async-start | bytes 3379200 | tf_op jit(solution)/shard_map/all_gather | solution.py:203
  191.2 685.8 %all-gather.13.cloned.1.call-start = ((), (), s32[]{:S(2)}) async-start(), calls=%async_computation.11 | async-start | bytes 13516800 | tf_op jit(solution)/shard_map/all_gather | solution.py:207
  191.7 699.9 %all-gather.15.cloned.1.call-start = ((), (), s32[]{:S(2)}) async-start(), calls=%async_computation.12 | async-start | bytes 1351680 | tf_op jit(solution)/shard_map/all_gather | solution.py:216
  192.3 726.9 %all-gather.17.cloned.1.call-start = ((), (), s32[]{:S(2)}) async-start(), calls=%async_computation.13 | async-start | bytes 13516800 | tf_op jit(solution)/shard_map/all_gather | solution.py:209
  192.9 740.8 %all-gather.19.cloned.1.call-start = ((), (), s32[]{:S(2)}) async-start(), calls=%async_computation.14 | async-start | bytes 1351680 | tf_op jit(solution)/shard_map/all_gather | solution.py:217
  193.6 1035.6 %reduce-scatter.27.cloned.1.call-start = ((), (), s32[]{:S(2)}) async-start(), calls=%async_computation.15 | async-start | bytes 7864320 | tf_op jit(solution)/shard_map/reduce_scatter | solution.py:315
  481.1 155.2 %copy-start.36 = (bf16[16,32,80,1]{2,1,3,0:T(8,128)(2,1)}, bf16[16,32,80,1]{2,1,3,0:T(8,128)(2,1)S(1)}, u32[]{:S(2)}) copy-start(bf16[16,32,80,1]{2,1,3,0:T(8,128)(2,1)S(1)} %fusion.75) | copy-start | bytes 245764
  874.3 84.3 %copy-start.2 = (f32[512,1280]{1,0:T(8,128)}, f32[512,1280]{1,0:T(8,128)S(1)}, u32[]{:S(2)}) copy-start(f32[512,1280]{1,0:T(8,128)S(1)} %get-tuple-element.77) | copy-start | bytes 7864324
  1043.7 221.8 %reduce-scatter.37.cloned.1.call-start = ((), (), s32[]{:S(2)}) async-start(), calls=%async_computation.21 | async-start | bytes 675840
  1046.6 326.7 %reduce-scatter.39.cloned.1.call-start = ((), (), s32[]{:S(2)}) async-start(), calls=%async_computation.22 | async-start | bytes 675840
  1048.1 458.4 %reduce-scatter.41.cloned.1.call-start = ((), (), s32[]{:S(2)}) async-start(), calls=%async_computation.23 | async-start | bytes 675840
  1050.9 588.6 %reduce-scatter.43.cloned.1.call-start = ((), (), s32[]{:S(2)}) async-start(), calls=%async_computation.24 | async-start | bytes 675840
  1057.0 720.9 %reduce-scatter.29.cloned.1.call-start = ((), (), s32[]{:S(2)}) async-start(), calls=%async_computation.16 | async-start | bytes 2703360 | tf_op jit(solution)/shard_map/reduce_scatter | solution.py:336
  1063.2 852.1 %reduce-scatter.31.cloned.1.call-start = ((), (), s32[]{:S(2)}) async-start(), calls=%async_computation.17 | async-start | bytes 2703360 | tf_op jit(solution)/shard_map/reduce_scatter | solution.py:337
  1063.3 79.9 %copy-start.45 = (bf16[512,128]{1,0:T(8,128)(2,1)S(1)}, bf16[512,128]{1,0:T(8,128)(2,1)}, u32[]{:S(2)}) copy-start(bf16[512,128]{1,0:T(8,128)(2,1)} %fusion.72) | copy-start | bytes 393220
  1148.8 899.3 %reduce-scatter.33.cloned.1.call-start = ((), (), s32[]{:S(2)}) async-start(), calls=%async_computation.19 | async-start | bytes 675840
  1234.5 938.2 %reduce-scatter.35.cloned.1.call-start = ((), (), s32[]{:S(2)}) async-start(), calls=%async_computation.20 | async-start | bytes 2027520
  1262.5 910.1 %copy-start.1 = (bf16[63,80]{1,0:T(8,128)(2,1)S(1)}, bf16[63,80]{1,0:T(8,128)(2,1)}, u32[]{:S(2)}) copy-start(bf16[63,80]{1,0:T(8,128)(2,1)} %param.40) | copy-start | bytes 30244
  (58 other events, 422.2 us)
Sparse Core Ops, SparseCore 0:
  11.0 86.7 all-gather.8
  190.5 93.6 all-gather.20
  287.1 60.4 all-gather.10
  350.3 100.3 all-gather.12
  453.5 53.2 all-gather.14
  509.5 96.9 all-gather.16
  609.3 53.1 all-gather.18
  1043.8 85.2 reduce-scatter.26
  1132.0 108.2 reduce-scatter.36
  1243.0 130.2 reduce-scatter.38
  1376.2 130.2 reduce-scatter.40
  1509.2 130.2 reduce-scatter.42
  1642.4 135.4 reduce-scatter.28
  1780.7 134.5 reduce-scatter.30
  1918.0 130.0 reduce-scatter.32
  2053.8 118.7 reduce-scatter.34
where the time goes:
time: 2200 us; the launch traced here: 2180 us
  waiting for transfers between devices  911 us (41%)
  blocking collectives  441 us (20%)
  local copies, waits for them, and re-layouts  424 us (19%)
  matrix products  285 us (13%)
  other arithmetic  102 us (5%)
    unnamed x22, waiting for transfers between devices  635 us
    add x4, local copies, waits for them, and re-layouts, score_block(): scores.reshape(HEADS, grid_rows, G, key_grid, G) + along_h[..., None]  289 us
    reduce_scatter x1, waiting for transfers between devices, per_device(): lax.psum_scatter(upper_fc1, ('dp', 'seq'), scatter_dimension=1, tiled=True)  138 us
    reduce_scatter x1, waiting for transfers between devices, per_device(): lax.psum_scatter(down_fc2, ('dp', 'seq'), scatter_dimension=0, tiled=True)  137 us
    convert_element_type x1, local copies, waits for them, and re-layouts, query_part(): sum_rows = jnp.sum(grid_scores, axis=4, dtype=jnp.float32)  79.9 us
    dot_general x12, matrix products, matmul(): return jnp.dot(left, right, preferred_element_type=jnp.float32)  77.2 us
    all_gather x1, blocking collectives, per_device(): lax.all_gather(proj_down, ('dp', 'seq'), axis=0, tiled=True)  74.3 us
    all_gather x1, blocking collectives, per_device(): lax.all_gather(fc1_down, ('dp', 'seq'), axis=0, tiled=True)  71.2 us
  transfers between devices with their start and end apart: 16, of which 7 were waited for; matrix products, arithmetic and copies ran while one was open for 31% of the time, Pallas kernels for 0%

commit v1 on v0

v1 whole, which is shorter than its diff:
```python
import functools

import jax
import jax.numpy as jnp
from jax import lax
from jax.experimental import pallas as pl
from jax.experimental.pallas import tpu as pltpu
from jax.sharding import PartitionSpec as P

HEADS = 16
HEAD_DIM = 80
ADAPTERS = 8
RANK = 16
G = 32
LANES = 128
HALF = HEADS // 2

epsilon = 1e-06
adapter_scale = 0.5
log2e = 1.4426950408889634
score_scale = HEAD_DIM ** (-0.5)
exponent_scale = score_scale * log2e
f32 = jnp.float32
bf16 = jnp.bfloat16


def dot_nn(left, right):
    return lax.dot_general(left, right, (((1,), (0,)), ((), ())), preferred_element_type=f32)


def dot_nt(left, right):
    return lax.dot_general(left, right, (((1,), (1,)), ((), ())), preferred_element_type=f32)


def dot_tn(left, right):
    return lax.dot_general(left, right, (((0,), (0,)), ((), ())), preferred_element_type=f32)


def normalize(values):
    average = jnp.mean(values, axis=-1, keepdims=True)
    centered = values - average
    variance = jnp.mean(centered * centered, axis=-1, keepdims=True)
    inverse = lax.rsqrt(variance + epsilon)
    return centered * inverse, inverse


def norm_back(scaled, normed, inverse):
    return inverse * (
        scaled
        - jnp.mean(scaled, axis=-1, keepdims=True)
        - normed * jnp.mean(scaled * normed, axis=-1, keepdims=True)
    )


def params(semantics, megabytes):
    return pltpu.CompilerParams(
        dimension_semantics=semantics, vmem_limit_bytes=megabytes * 1024 * 1024
    )


def whole(shape):
    zeros = (0,) * len(shape)
    return pl.BlockSpec(shape, lambda *_: zeros)


def qkv_kernel(
    x_ref, gain_ref, shift_ref, weight_ref, bias_ref, down_ref, up_ref, mask_ref,
    heads_ref, mid_ref, act_ref,
):
    part = pl.program_id(0)
    length = x_ref.shape[0]

    @pl.when(part == 0)
    def _():
        normed, _ = normalize(x_ref[...].astype(f32))
        act_ref[...] = (normed * gain_ref[...].astype(f32) + shift_ref[...].astype(f32)).astype(bf16)
        mid_ref[...] = (dot_nn(act_ref[...], down_ref[...]) * mask_ref[...]).astype(bf16)

    rows = min(256, length)
    lane = lax.broadcasted_iota(jnp.int32, (rows, LANES - HEAD_DIM), 1)
    pad = jnp.where((lane == 0) & (part == 2), 1.0, 0.0).astype(bf16)
    for start in range(0, length, rows):
        here = pl.ds(start, rows)
        block = dot_nn(act_ref[here, :], weight_ref[...])
        block = block + bias_ref[...].astype(f32)
        block = block + adapter_scale * dot_nt(mid_ref[here, :], up_ref[...])
        block = block.astype(bf16)
        for head in range(HEADS):
            heads_ref[0, head, here, 0:HEAD_DIM] = block[:, head * HEAD_DIM : (head + 1) * HEAD_DIM]
            heads_ref[0, head, here, HEAD_DIM:LANES] = pad


def qkv_call(tokens, gain, shift, weight, bias, down, up, mask):
    length, features = tokens.shape
    return pl.pallas_call(
        qkv_kernel,
        name="qkv",
        grid=(3,),
        in_specs=[
            whole((length, features)),
            whole((1, features)),
            whole((1, features)),
            pl.BlockSpec((features, features), lambda j: (0, j)),
            pl.BlockSpec((1, features), lambda j: (0, j)),
            whole((features, LANES)),
            pl.BlockSpec((features, LANES), lambda j: (j, 0)),
            whole((1, LANES)),
        ],
        out_specs=[
            pl.BlockSpec((1, HEADS, length, LANES), lambda j: (j, 0, 0, 0)),
            whole((length, LANES)),
        ],
        out_shape=[
            jax.ShapeDtypeStruct((3, HEADS, length, LANES), bf16),
            jax.ShapeDtypeStruct((length, LANES), bf16),
        ],
        scratch_shapes=[pltpu.VMEM((length, features), bf16)],
        compiler_params=params(("arbitrary",), 50),
        cost_estimate=pl.CostEstimate(
            flops=6 * length * features * features,
            bytes_accessed=2 * (3 * features * features + 4 * length * features),
            transcendentals=0,
        ),
    )(tokens, gain, shift, weight, bias, down, up, mask)


def forward_kernel(place_ref, q_ref, k_ref, v_ref, table_ref, spots_ref, att_ref, lse_ref, aux_ref):
    head = pl.program_id(0)
    length = q_ref.shape[2]
    part_len = att_ref.shape[0]
    lane = lax.broadcasted_iota(jnp.int32, (G, LANES), 1)
    first = lane < LANES // 2
    even = (lane // G) % 2 == 0
    raw = dot_nn(q_ref[0, 0], table_ref[...]) * (HEAD_DIM**0.5)
    for row in range(length // G):
        block = raw[row * G : (row + 1) * G, :]
        high = block.astype(bf16).astype(f32)
        mixed_h = jnp.where(first, high[:, :LANES], block[:, :LANES] - high[:, :LANES])
        mixed_w = jnp.where(first, high[:, LANES:], block[:, LANES:] - high[:, LANES:])
        along_h = pltpu.roll(mixed_h, LANES - G + 1 + row, 1)
        along_w = pltpu.roll(mixed_w, 1, 1, stride=1, stride_axis=0)
        aux_ref[0, pl.ds(row * G, G), :] = jnp.where(even, along_h, along_w).astype(bf16)
    here = pl.ds(pl.multiple_of(place_ref[0] * part_len, G), part_len)
    left = jnp.concatenate([q_ref[0, 0, here, :], aux_ref[0, here, :]], axis=1)
    right = jnp.concatenate([k_ref[0, 0], spots_ref[...]], axis=1)
    scores = dot_nt(left, right)
    top = jnp.max(scores, axis=1, keepdims=True)
    shares = jnp.exp2((scores - top) * exponent_scale).astype(bf16)
    mixed = dot_nn(shares, v_ref[0, 0])
    total = mixed[:, HEAD_DIM : HEAD_DIM + 1]
    att = (mixed[:, :HEAD_DIM] / total).astype(bf16)
    logs = top * exponent_scale + jnp.log2(total)
    lse_ref[0] = jnp.transpose(jnp.broadcast_to(logs, (part_len, LANES)))[0:1, :]
    for slot in range(HALF):

        @pl.when(head % HALF == slot)
        def _():
            att_ref[:, slot * HEAD_DIM : (slot + 1) * HEAD_DIM] = att


def forward_call(place, heads, table, spots, part_len):
    length = heads.shape[2]
    features = HEADS * HEAD_DIM

    def part(index):
        return pl.BlockSpec((1, 1, length, LANES), lambda n, s: (index, n, 0, 0))

    return pl.pallas_call(
        forward_kernel,
        name="attend",
        grid_spec=pltpu.PrefetchScalarGridSpec(
            num_scalar_prefetch=1,
            grid=(HEADS,),
            in_specs=[
                part(0),
                part(1),
                part(2),
                whole((LANES, 2 * LANES)),
                whole((length, LANES)),
            ],
            out_specs=[
                pl.BlockSpec((part_len, features // 2), lambda n, s: (0, n // HALF)),
                pl.BlockSpec((1, 1, part_len), lambda n, s: (n, 0, 0)),
                pl.BlockSpec((1, length, LANES), lambda n, s: (n, 0, 0)),
            ],
        ),
        out_shape=[
            jax.ShapeDtypeStruct((part_len, features), bf16),
            jax.ShapeDtypeStruct((HEADS, 1, part_len), f32),
            jax.ShapeDtypeStruct((HEADS, length, LANES), bf16),
        ],
        compiler_params=params(("arbitrary",), 40),
        cost_estimate=pl.CostEstimate(
            flops=4 * HEADS * part_len * length * LANES * 2,
            bytes_accessed=8 * HEADS * length * LANES,
            transcendentals=HEADS * part_len * length,
        ),
    )(place, heads, heads, heads, table, spots)


def head_lanes(source, head, padded):
    padded[:, HEAD_DIM:LANES] = jnp.zeros((padded.shape[0], LANES - HEAD_DIM), bf16)
    for slot in range(HALF):

        @pl.when(head % HALF == slot)
        def _():
            padded[:, 0:HEAD_DIM] = source[:, slot * HEAD_DIM : (slot + 1) * HEAD_DIM]


def own_kernel(
    place_ref, q_ref, aux_ref, k_ref, v_ref, spots_ref, turned_spots_ref, table_ref, grad_ref,
    lse_ref, inner_ref, dq_ref, dk_ref, dv_ref, shares_ref, dscores_ref, padded,
):
    head = pl.program_id(0)
    part_len = q_ref.shape[2]
    head_lanes(grad_ref, head, padded)
    queries = q_ref[0, 0]
    keys = k_ref[0, 0]
    left = jnp.concatenate([keys, spots_ref[...]], axis=1)
    right = jnp.concatenate([queries, aux_ref[0]], axis=1)
    shares = jnp.exp2(dot_nt(left, right) * exponent_scale - lse_ref[0])
    grad_shares = dot_nt(v_ref[0, 0], padded[...])
    shares_ref[...] = shares.astype(bf16)
    dscores_ref[...] = (shares * (grad_shares - inner_ref[0])).astype(bf16)
    flat = dot_tn(jnp.concatenate([keys, turned_spots_ref[...]], axis=1), dscores_ref[...])
    turned = jnp.transpose(flat)
    lane = lax.broadcasted_iota(jnp.int32, (G, LANES), 1)
    first = lane < LANES // 2
    even = (lane // G) % 2 == 0
    start = place_ref[0] * (part_len // G)
    pieces_h, pieces_w = [], []
    for row in range(part_len // G):
        sums = turned[row * G : (row + 1) * G, LANES:]
        high = sums.astype(bf16).astype(f32)
        mixed = jnp.where(first, high, sums - high)
        pieces_h.append(pltpu.roll(jnp.where(even, mixed, 0.0), start + row, 1))
        pieces_w.append(
            pltpu.roll(jnp.where(even, 0.0, mixed), LANES - G, 1, stride=1, stride_axis=0)
        )
    spread = jnp.concatenate(
        [jnp.concatenate(pieces_h, axis=0), jnp.concatenate(pieces_w, axis=0)], axis=1
    ).astype(bf16)
    grad_query = turned[:, :LANES] * score_scale + dot_nn(spread, table_ref[...])
    grad_query = grad_query[:, :HEAD_DIM].astype(bf16)
    for slot in range(HALF):

        @pl.when(head % HALF == slot)
        def _():
            dq_ref[:, slot * HEAD_DIM : (slot + 1) * HEAD_DIM] = grad_query

    here = pl.ds(pl.multiple_of(place_ref[0] * part_len, G), part_len)
    dk_ref[0] = dot_nn(dscores_ref[here, :], queries)
    dv_ref[0] = dot_nn(shares_ref[here, :], padded[...])


def own_call(place, heads, aux, spots, turned_spots, table, grad, lse, inner):
    length = heads.shape[2]
    part_len, features = grad.shape

    def part(index):
        return pl.BlockSpec((1, 1, length, LANES), lambda n, s: (index, n, 0, 0))

    return pl.pallas_call(
        own_kernel,
        name="back_own",
        grid_spec=pltpu.PrefetchScalarGridSpec(
            num_scalar_prefetch=1,
            grid=(HEADS,),
            in_specs=[
                pl.BlockSpec((1, 1, part_len, LANES), lambda n, s: (0, n, s[0], 0)),
                pl.BlockSpec((1, part_len, LANES), lambda n, s: (n, s[0], 0)),
                part(1),
                part(2),
                whole((length, LANES)),
                whole((length, LANES)),
                whole((2 * LANES, LANES)),
                pl.BlockSpec((part_len, features // 2), lambda n, s: (0, n // HALF)),
                pl.BlockSpec((1, 1, part_len), lambda n, s: (n, 0, 0)),
                pl.BlockSpec((1, 1, part_len), lambda n, s: (n, 0, 0)),
            ],
            out_specs=[
                pl.BlockSpec((part_len, features // 2), lambda n, s: (0, n // HALF)),
                pl.BlockSpec((1, part_len, LANES), lambda n, s: (n, 0, 0)),
                pl.BlockSpec((1, part_len, LANES), lambda n, s: (n, 0, 0)),
            ],
            scratch_shapes=[
                pltpu.VMEM((length, part_len), bf16),
                pltpu.VMEM((length, part_len), bf16),
                pltpu.VMEM((part_len, LANES), bf16),
            ],
        ),
        out_shape=[
            jax.ShapeDtypeStruct((part_len, features), bf16),
            jax.ShapeDtypeStruct((HEADS, part_len, LANES), f32),
            jax.ShapeDtypeStruct((HEADS, part_len, LANES), f32),
        ],
        compiler_params=params(("arbitrary",), 40),
        cost_estimate=pl.CostEstimate(
            flops=8 * HEADS * part_len * length * LANES * 2,
            bytes_accessed=12 * HEADS * length * LANES,
            transcendentals=HEADS * part_len * length,
        ),
    )(place, heads, aux, heads, heads, spots, turned_spots, table, grad, lse, inner)


def other_kernel(
    place_ref, q_ref, aux_ref, k_ref, v_ref, spots_ref, grad_ref, lse_ref, inner_ref, dk_in, dv_in,
    dk_ref, dv_ref, dk_sum, dv_sum, padded,
):
    head = pl.program_id(0)
    step = pl.program_id(1)
    head_lanes(grad_ref.at[0], head, padded)
    queries = q_ref[0, 0]
    left = jnp.concatenate([k_ref[0, 0], spots_ref[...]], axis=1)
    right = jnp.concatenate([queries, aux_ref[0]], axis=1)
    shares = jnp.exp2(dot_nt(left, right) * exponent_scale - lse_ref[0, 0])
    grad_shares = dot_nt(v_ref[0, 0], padded[...])
    dscores = (shares * (grad_shares - inner_ref[0, 0])).astype(bf16)

    @pl.when(step == 0)
    def _():
        dk_sum[...] = dk_in[0]
        dv_sum[...] = dv_in[0]

    dk_sum[...] += dot_nn(dscores, queries)
    dv_sum[...] += dot_nn(shares.astype(bf16), padded[...])

    @pl.when(step == pl.num_programs(1) - 1)
    def _():
        grad_key = (dk_sum[:, :HEAD_DIM] * score_scale).astype(bf16)
        grad_value = dv_sum[:, :HEAD_DIM].astype(bf16)
        for slot in range(HALF):

            @pl.when(head % HALF == slot)
            def _():
                dk_ref[:, slot * HEAD_DIM : (slot + 1) * HEAD_DIM] = grad_key
                dv_ref[:, slot * HEAD_DIM : (slot + 1) * HEAD_DIM] = grad_value


def other_call(place, heads, aux, spots, grads, lses, inners, dk, dv):
    length = heads.shape[2]
    blocks, part_len, features = grads.shape
    count = length // part_len

    def theirs(i, s):
        return lax.rem(s[0] + 1 + i, count)

    def given(i, s):
        return theirs(i, s) if blocks > 1 else 0

    def own(index):
        return pl.BlockSpec((1, 1, part_len, LANES), lambda n, i, s: (index, n, s[0], 0))

    stats = pl.BlockSpec((1, 1, 1, part_len), lambda n, i, s: (given(i, s), n, 0, 0))
    sums = pl.BlockSpec((1, part_len, LANES), lambda n, i, s: (n, 0, 0))
    dense = pl.BlockSpec((part_len, features // 2), lambda n, i, s: (0, n // HALF))
    return pl.pallas_call(
        other_kernel,
        name="back_other",
        grid_spec=pltpu.PrefetchScalarGridSpec(
            num_scalar_prefetch=1,
            grid=(HEADS, count - 1),
            in_specs=[
                pl.BlockSpec((1, 1, part_len, LANES), lambda n, i, s: (0, n, theirs(i, s), 0)),
                pl.BlockSpec((1, part_len, LANES), lambda n, i, s: (n, theirs(i, s), 0)),
                own(1),
                own(2),
                pl.BlockSpec((part_len, LANES), lambda n, i, s: (s[0], 0)),
                pl.BlockSpec(
                    (1, part_len, features // 2), lambda n, i, s: (given(i, s), 0, n // HALF)
                ),
                stats,
                stats,
                sums,
                sums,
            ],
            out_specs=[dense, dense],
            scratch_shapes=[
                pltpu.VMEM((part_len, LANES), f32),
                pltpu.VMEM((part_len, LANES), f32),
                pltpu.VMEM((part_len, LANES), bf16),
            ],
        ),
        out_shape=[
            jax.ShapeDtypeStruct((part_len, features), bf16),
            jax.ShapeDtypeStruct((part_len, features), bf16),
        ],
        compiler_params=params(("arbitrary", "arbitrary"), 40),
        cost_estimate=pl.CostEstimate(
            flops=4 * HEADS * part_len * (length - part_len) * LANES * 2,
            bytes_accessed=12 * HEADS * length * LANES,
            transcendentals=HEADS * part_len * (length - part_len),
        ),
    )(place, heads, aux, heads, heads, spots, grads, lses, inners, dk, dv)


def project_kernel(
    att_ref, x_ref, weight_ref, bias_ref, down_ref, up_ref, mask_ref, gain_ref, shift_ref,
    fc1_down_ref, resid_ref, act_ref, mid_ref, mid1_ref,
):
    att = att_ref[...]
    mid_ref[...] = (dot_nn(att, down_ref[...]) * mask_ref[...]).astype(bf16)
    branch = dot_nn(att, weight_ref[...]) + bias_ref[...].astype(f32)
    branch = branch + adapter_scale * dot_nt(mid_ref[...], up_ref[...])
    resid = x_ref[...].astype(f32) + branch
    resid_ref[...] = resid
    normed, _ = normalize(resid)
    act_ref[...] = (normed * gain_ref[...].astype(f32) + shift_ref[...].astype(f32)).astype(bf16)
    mid1_ref[...] = (dot_nn(act_ref[...], fc1_down_ref[...]) * mask_ref[...]).astype(bf16)


def project_call(att, x, weight, bias, down, up, mask, gain, shift, fc1_down):
    rows, features = att.shape
    return pl.pallas_call(
        project_kernel,
        name="project",
        out_shape=[
            jax.ShapeDtypeStruct((rows, features), f32),
            jax.ShapeDtypeStruct((rows, features), bf16),
            jax.ShapeDtypeStruct((rows, LANES), bf16),
            jax.ShapeDtypeStruct((rows, LANES), bf16),
        ],
        compiler_params=params(None, 50),
        cost_estimate=pl.CostEstimate(
            flops=2 * rows * features * features,
            bytes_accessed=2 * features * features + 12 * rows * features,
            transcendentals=0,
        ),
    )(att, x, weight, bias, down, up, mask, gain, shift, fc1_down)


def gelu_parts(hidden):
    size = jnp.abs(hidden) * (0.5**0.5)
    bell = jnp.exp2(hidden * hidden * (-0.5 * log2e))
    t = 1.0 / (1.0 + 0.3275911 * size)
    poly = t * (
        0.254829592
        + t * (-0.284496736 + t * (1.421413741 + t * (-1.453152027 + t * 1.061405429)))
    )
    tail = 0.5 * poly * bell
    cumulative = jnp.where(hidden < 0.0, tail, 1.0 - tail)
    return hidden * cumulative, cumulative + hidden * bell * 0.3989422804014327


def feed_kernel(
    pick_ref, act_ref, resid_ref, og_ref, w1_ref, b1_ref, w2_ref, b2_ref, down1_ref, up1_ref,
    down2_ref, up2_ref, mid1_ref, mask_ref, gain_ref,
    out_ref, grad_ref, branch_ref, gd1_ref, gu1_ref, gd2_ref, gu2_ref,
    total, back, mid2_sum, gm1_sum, gm2, gm2_t, mid1_t,
):
    step = pl.program_id(0)
    picked = pl.ds(pl.multiple_of(pick_ref[0] * RANK, RANK), RANK)
    mask = mask_ref[...]

    @pl.when(step == 0)
    def _():
        total[...] = jnp.zeros_like(total)
        back[...] = jnp.zeros_like(back)
        mid2_sum[...] = jnp.zeros_like(mid2_sum)
        gm1_sum[...] = jnp.zeros_like(gm1_sum)
        middle = adapter_scale * dot_nn(og_ref[...], up2_ref[...]) * mask
        gm2[...] = middle.astype(bf16)
        gm2_t[...] = jnp.transpose(gm2[...].astype(f32)).astype(bf16)
        mid1_t[...] = jnp.transpose(mid1_ref[...].astype(f32)).astype(bf16)

    hidden = dot_nn(act_ref[...], w1_ref[...]) + b1_ref[...].astype(f32)
    hidden = hidden + adapter_scale * dot_nt(mid1_ref[...], up1_ref[...])
    grad_act = dot_nt(og_ref[...], w2_ref[...]) + dot_nt(gm2[...], down2_ref[...])
    value, slope = gelu_parts(hidden)
    activated = value.astype(bf16)
    grad_hidden = (grad_act * slope).astype(bf16)
    total[...] += dot_nn(activated, w2_ref[...])
    mid2_sum[...] += dot_nn(activated, down2_ref[...])
    back[...] += dot_nt(grad_hidden, w1_ref[...])
    gm1_sum[...] += dot_nn(grad_hidden, up1_ref[...])
    gd2_ref[...] = dot_nn(gm2_t[picked, :], activated).astype(bf16)
    gu1_ref[...] = (adapter_scale * dot_nn(mid1_t[picked, :], grad_hidden)).astype(bf16)

    @pl.when(step == pl.num_programs(0) - 1)
    def _():
        mid2 = mid2_sum[...] * mask
        mid2_low = mid2.astype(bf16)
        resid = resid_ref[...]
        final = resid + total[...] + b2_ref[...].astype(f32)
        final = final + adapter_scale * dot_nt(mid2_low, up2_ref[...])
        out_ref[...] = final.astype(bf16)
        gm1 = adapter_scale * gm1_sum[...] * mask
        gm1_low = gm1.astype(bf16)
        upstream = back[...] + dot_nt(gm1_low, down1_ref[...])
        normed, inverse = normalize(resid)
        grad = og_ref[...].astype(f32) + norm_back(
            upstream * gain_ref[...].astype(f32), normed, inverse
        )
        grad_ref[...] = grad
        branch_ref[...] = grad.astype(bf16)
        gm2_t[...] = jnp.transpose(gm1_low.astype(f32)).astype(bf16)
        gd1_ref[...] = dot_nn(gm2_t[picked, :], act_ref[...]).astype(bf16)
        mid1_t[...] = jnp.transpose(mid2_low.astype(f32)).astype(bf16)
        gu2_ref[...] = (adapter_scale * dot_nn(mid1_t[picked, :], og_ref[...])).astype(bf16)


def feed_call(pick, act, resid, og, w1, b1, w2, b2, down1, up1, down2, up2, mid1, mask, gain):
    rows, features = act.shape
    wide = w1.shape[1]
    block = 512
    row_block = pl.BlockSpec((block, LANES), lambda j, s: (j, 0))
    return pl.pallas_call(
        feed_kernel,
        name="feed",
        grid_spec=pltpu.PrefetchScalarGridSpec(
            num_scalar_prefetch=1,
            grid=(wide // block,),
            in_specs=[
                whole((rows, features)),
                whole((rows, features)),
                whole((rows, features)),
                pl.BlockSpec((features, block), lambda j, s: (0, j)),
                pl.BlockSpec((1, block), lambda j, s: (0, j)),
                pl.BlockSpec((block, features), lambda j, s: (j, 0)),
                whole((1, features)),
                whole((features, LANES)),
                row_block,
                row_block,
                whole((features, LANES)),
                whole((rows, LANES)),
                whole((1, LANES)),
                whole((1, features)),
            ],
            out_specs=[
                whole((rows, features)),
                whole((rows, features)),
                whole((rows, features)),
                whole((RANK, features)),
                pl.BlockSpec((RANK, block), lambda j, s: (0, j)),
                pl.BlockSpec((RANK, block), lambda j, s: (0, j)),
                whole((RANK, features)),
            ],
            scratch_shapes=[
                pltpu.VMEM((rows, features), f32),
                pltpu.VMEM((rows, features), f32),
                pltpu.VMEM((rows, LANES), f32),
                pltpu.VMEM((rows, LANES), f32),
                pltpu.VMEM((rows, LANES), bf16),
                pltpu.VMEM((LANES, rows), bf16),
                pltpu.VMEM((LANES, rows), bf16),
            ],
        ),
        out_shape=[
            jax.ShapeDtypeStruct((rows, features), bf16),
            jax.ShapeDtypeStruct((rows, features), f32),
            jax.ShapeDtypeStruct((rows, features), bf16),
            jax.ShapeDtypeStruct((RANK, features), bf16),
            jax.ShapeDtypeStruct((RANK, wide), bf16),
            jax.ShapeDtypeStruct((RANK, wide), bf16),
            jax.ShapeDtypeStruct((RANK, features), bf16),
        ],
        compiler_params=params(("arbitrary",), 58),
        cost_estimate=pl.CostEstimate(
            flops=8 * rows * features * wide,
            bytes_accessed=4 * features * wide + 24 * rows * features,
            transcendentals=2 * rows * wide,
        ),
    )(pick, act, resid, og, w1, b1, w2, b2, down1, up1, down2, up2, mid1, mask, gain)


def unproject_kernel(
    pick_ref, branch_ref, att_ref, weight_ref, down_ref, up_ref, mid_ref, mask_ref, sums_ref,
    grad_ref, inner_ref, gd_ref, gu_ref, turned,
):
    picked = pl.ds(pl.multiple_of(pick_ref[0] * RANK, RANK), RANK)
    branch = branch_ref[...]
    att = att_ref[...]
    middle = (adapter_scale * dot_nn(branch, up_ref[...]) * mask_ref[...]).astype(bf16)
    grad = dot_nt(branch, weight_ref[...]) + dot_nt(middle, down_ref[...])
    grad_ref[...] = grad.astype(bf16)
    product = grad_ref[...].astype(f32) * att.astype(f32)
    high = product.astype(bf16)
    low = (product - high.astype(f32)).astype(bf16)
    inner = dot_nt(sums_ref[...], high) + dot_nt(sums_ref[...], low)
    for head in range(HEADS):
        inner_ref[head] = inner[head : head + 1, :]
    turned[...] = jnp.transpose(middle.astype(f32)).astype(bf16)
    gd_ref[...] = dot_nn(turned[picked, :], att).astype(bf16)
    turned[...] = jnp.transpose(mid_ref[...].astype(f32)).astype(bf16)
    gu_ref[...] = (adapter_scale * dot_nn(turned[picked, :], branch)).astype(bf16)


def unproject_call(pick, branch, att, weight, down, up, mid, mask, sums):
    rows, features = branch.shape
    return pl.pallas_call(
        unproject_kernel,
        name="unproject",
        grid_spec=pltpu.PrefetchScalarGridSpec(
            num_scalar_prefetch=1,
            grid=(1,),
            in_specs=[whole(a.shape) for a in (branch, att, weight, down, up, mid, mask, sums)],
            out_specs=[
                whole((rows, features)),
                whole((HEADS, 1, rows)),
                whole((RANK, features)),
                whole((RANK, features)),
            ],
            scratch_shapes=[pltpu.VMEM((LANES, rows), bf16)],
        ),
        out_shape=[
            jax.ShapeDtypeStruct((rows, features), bf16),
            jax.ShapeDtypeStruct((HEADS, 1, rows), f32),
            jax.ShapeDtypeStruct((RANK, features), bf16),
            jax.ShapeDtypeStruct((RANK, features), bf16),
        ],
        compiler_params=params(("arbitrary",), 50),
        cost_estimate=pl.CostEstimate(
            flops=2 * rows * features * features,
            bytes_accessed=2 * features * features + 8 * rows * features,
            transcendentals=0,
        ),
    )(pick, branch, att, weight, down, up, mid, mask, sums)


def unqkv_kernel(
    pick_ref, dq_ref, dk_ref, dv_ref, weight_ref, down_ref, up_ref, mid_ref, mask_ref, x_ref,
    gain_ref, shift_ref, resid_ref, out_ref, gd_ref, gu_ref, total, gm_sum, mid_t,
):
    step = pl.program_id(0)
    picked = pl.ds(pl.multiple_of(pick_ref[0] * RANK, RANK), RANK)

    @pl.when(step == 0)
    def _():
        total[...] = jnp.zeros_like(total)
        gm_sum[...] = jnp.zeros_like(gm_sum)
        mid_t[...] = jnp.transpose(mid_ref[...].astype(f32)).astype(bf16)

    for index, source in enumerate((dq_ref, dk_ref, dv_ref)):

        @pl.when(step == index)
        def _():
            total[...] += dot_nt(source[...], weight_ref[...])
            gm_sum[...] += dot_nn(source[...], up_ref[...])
            gu_ref[...] = (adapter_scale * dot_nn(mid_t[picked, :], source[...])).astype(bf16)

    @pl.when(step == 2)
    def _():
        middle = (adapter_scale * gm_sum[...] * mask_ref[...]).astype(bf16)
        upstream = total[...] + dot_nt(middle, down_ref[...])
        normed, inverse = normalize(x_ref[...].astype(f32))
        gain = gain_ref[...].astype(f32)
        act = (normed * gain + shift_ref[...].astype(f32)).astype(bf16)
        out_ref[...] = resid_ref[...] + norm_back(upstream * gain, normed, inverse)
        mid_t[...] = jnp.transpose(middle.astype(f32)).astype(bf16)
        gd_ref[...] = dot_nn(mid_t[picked, :], act).astype(bf16)


def unqkv_call(pick, dq, dk, dv, weight, down, up, mid, mask, x, gain, shift, resid):
    rows, features = dq.shape
    return pl.pallas_call(
        unqkv_kernel,
        name="unqkv",
        grid_spec=pltpu.PrefetchScalarGridSpec(
            num_scalar_prefetch=1,
            grid=(3,),
            in_specs=[
                whole((rows, features)),
                whole((rows, features)),
                whole((rows, features)),
                pl.BlockSpec((features, features), lambda j, s: (0, j)),
                whole((features, LANES)),
                pl.BlockSpec((features, LANES), lambda j, s: (j, 0)),
                whole((rows, LANES)),
                whole((1, LANES)),
                whole((rows, features)),
                whole((1, features)),
                whole((1, features)),
                whole((rows, features)),
            ],
            out_specs=[
                whole((rows, features)),
                whole((RANK, features)),
                pl.BlockSpec((RANK, features), lambda j, s: (0, j)),
            ],
            scratch_shapes=[
                pltpu.VMEM((rows, features), f32),
                pltpu.VMEM((rows, LANES), f32),
                pltpu.VMEM((LANES, rows), bf16),
            ],
        ),
        out_shape=[
            jax.ShapeDtypeStruct((rows, features), f32),
            jax.ShapeDtypeStruct((RANK, features), bf16),
            jax.ShapeDtypeStruct((RANK, 3 * features), bf16),
        ],
        compiler_params=params(("arbitrary",), 50),
        cost_estimate=pl.CostEstimate(
            flops=6 * rows * features * features,
            bytes_accessed=6 * features * features + 20 * rows * features,
            transcendentals=0,
        ),
    )(pick, dq, dk, dv, weight, down, up, mid, mask, x, gain, shift, resid)


def position_tables(rel_h, rel_w, length):
    wide = ((0, LANES // 2 - (2 * G - 1)), (0, LANES - HEAD_DIM))
    h = jnp.pad(rel_h, wide)
    w = jnp.pad(rel_w, wide)
    h_back = jnp.pad(rel_h[::-1], wide)
    w_back = jnp.pad(rel_w[::-1], wide)
    forward = jnp.concatenate([h_back, h_back, w_back, w_back], axis=0).T
    backward = jnp.concatenate([h, h, w, w], axis=0)
    spot = jnp.arange(length, dtype=jnp.int32)[:, None]
    lane = jnp.arange(LANES, dtype=jnp.int32)[None, :]
    at = jnp.where((lane // G) % 2 == 0, spot // G, spot % G)
    spots = (lane % G == at).astype(bf16)
    turned = (lane % G == G - 1 - at).astype(bf16)
    return forward, backward, spots, turned


def collect_kernel(lines, chunks, rows_of, count, *refs):
    sources, tokens = refs[:count], refs[count]
    targets, image = refs[count + 1 : 2 * count + 1], refs[2 * count + 1]
    local, sends, arrivals = refs[2 * count + 2 :]
    dp = lax.axis_index("dp")
    seq = lax.axis_index("seq")
    line, column, core = dp // 4, (dp // 2) % 2, dp % 2

    def device(z, x, c, y):
        return (z * 4 + x * 2 + c, y)

    def back(k):
        return lax.rem(line + lines - k, lines)

    ahead = [device(lax.rem(line + k, lines), column, core, seq) for k in range(1, lines)]
    across = device(line, 1 - column, core, seq)
    partner = device(line, column, core, 1 - seq)
    sibling = device(line, column, 1 - core, seq)
    peers = ahead + [across, partner, sibling]

    barrier = pltpu.get_barrier_semaphore()
    for peer in peers:
        pl.semaphore_signal(
            barrier, inc=1, device_id=peer, device_id_type=pl.DeviceIdType.MESH
        )
    pl.semaphore_wait(barrier, len(peers))

    outgoing = []
    used = [0]

    def block(chunk, owner, half):
        array, row, height, col, width = chunk
        by_columns = width >= 2 * LANES
        start = (owner[0] * 2 + owner[1]) * rows_of[array] + row
        if half is not None:
            if by_columns:
                cut = (width // 2 + LANES - 1) // LANES * LANES
                col, width = (col, cut) if half == 0 else (col + cut, width - cut)
            else:
                cut = (height // 2 + 7) // 8 * 8
                start, height = (start, cut) if half == 0 else (start + cut, height - cut)
        if height == 0 or width == 0:
            return None
        return targets[array].at[pl.ds(pl.multiple_of(start, 8), height), pl.ds(col, width)]

    def send(source, target, peer, slot):
        copy = pltpu.make_async_remote_copy(
            src_ref=source,
            dst_ref=target,
            send_sem=sends.at[used[0]],
            recv_sem=arrivals.at[slot],
            device_id=peer,
            device_id_type=pl.DeviceIdType.MESH,
        )
        used[0] += 1
        copy.start()
        outgoing.append(copy)

    def arrive(place, slot):
        pltpu.make_async_copy(place, place, arrivals.at[slot]).wait()

    here = (dp, seq)
    Z, X, Y, S, XD, YD, SX, SY, SD = range(9)
    per = 9 * lines

    def slot(number, kind, k):
        return number * per + kind * lines + k

    keep = []
    part_len = tokens.shape[0]
    mine = image.at[pl.ds(pl.multiple_of(seq * part_len, 8), part_len), :]
    theirs = image.at[pl.ds(pl.multiple_of((1 - seq) * part_len, 8), part_len), :]
    token_slot = len(chunks) * per
    for number, chunk in enumerate(chunks):
        array, row, height, col, width = chunk
        own = sources[array].at[pl.ds(row, height), pl.ds(col, width)]
        place = block(chunk, here, None)
        for k in range(1, lines):
            send(own, place, ahead[k - 1], slot(number, Z, k))
        send(own, place, across, slot(number, X, 0))
        send(own, place, partner, slot(number, Y, 0))
        send(own, place, sibling, slot(number, S, 0))
        copy = pltpu.make_async_copy(own, place, local.at[number])
        copy.start()
        keep.append(copy)
        if number == 0:
            send(tokens, mine, partner, token_slot)
            copy = pltpu.make_async_copy(tokens, mine, local.at[len(chunks)])
            copy.start()
            keep.append(copy)

    def stage_one(number):
        chunk = chunks[number]
        for k in range(1, lines):
            place = block(chunk, device(back(k), column, core, seq), None)
            arrive(place, slot(number, Z, k))
            send(place, place, across, slot(number, X, k))
            send(place, place, partner, slot(number, Y, k))
            send(place, place, sibling, slot(number, S, k))

    def stage_two(number):
        chunk = chunks[number]
        for k in range(lines):
            owner = device(back(k), 1 - column, core, seq)
            place = block(chunk, owner, None)
            arrive(place, slot(number, X, k))
            half = block(chunk, owner, 0)
            send(half, half, partner, slot(number, YD, k))
            send(place, place, sibling, slot(number, SX, k))
            owner = device(back(k), column, core, 1 - seq)
            place = block(chunk, owner, None)
            arrive(place, slot(number, Y, k))
            half = block(chunk, owner, 1)
            if half is not None:
                send(half, half, across, slot(number, XD, k))
            send(place, place, sibling, slot(number, SY, k))

    def stage_three(number):
        chunk = chunks[number]
        for k in range(lines):
            owner = device(back(k), 1 - column, core, 1 - seq)
            place = block(chunk, owner, None)
            arrive(block(chunk, owner, 0), slot(number, YD, k))
            half = block(chunk, owner, 1)
            if half is not None:
                arrive(half, slot(number, XD, k))
            send(place, place, sibling, slot(number, SD, k))

    def stage_four(number):
        chunk = chunks[number]
        for k in range(lines):
            for kind, x, y in (
                (S, column, seq),
                (SX, 1 - column, seq),
                (SY, column, 1 - seq),
                (SD, 1 - column, 1 - seq),
            ):
                place = block(chunk, device(back(k), x, 1 - core, y), None)
                arrive(place, slot(number, kind, k))

    stages = (stage_one, stage_two, stage_three, stage_four)
    for tick in range(len(chunks) + len(stages) - 1):
        for lag, stage in enumerate(stages):
            if 0 <= tick - lag < len(chunks):
                stage(tick - lag)
    arrive(theirs, token_slot)
    for copy in keep:
        copy.wait()
    for copy in outgoing:
        copy.wait_send()


def collect_chunks(arrays):
    chunks = []
    for index, array in enumerate(arrays):
        height, width = array.shape
        wide = width
        while height * wide * 2 > 120_000 and wide % (4 * LANES) == 0 and wide > 1280:
            wide = next(w for w in range(wide - LANES, 0, -LANES) if width % w == 0)
        tall = height
        while tall * wide * 2 > 120_000 and tall % 16 == 0:
            tall //= 2
        for row in range(0, height, tall):
            for col in range(0, width, wide):
                chunks.append((index, row, tall, col, wide))
    return chunks


def collect(mesh_shape, arrays, tokens):
    axes = ("dp", "seq")
    lines = mesh_shape["dp"] // 4
    usable = mesh_shape["seq"] == 2 and mesh_shape["dp"] == 4 * lines and 2 <= lines <= 4
    if not usable or any(a.shape[0] % 8 for a in arrays):
        gathered = [lax.all_gather(a, axes, axis=0, tiled=True) for a in arrays]
        return gathered, lax.all_gather(tokens, "seq", axis=0, tiled=True)
    devices = mesh_shape["dp"] * 2
    chunks = collect_chunks(arrays)
    anywhere = pl.BlockSpec(memory_space=pl.ANY)
    count = len(arrays)
    slots = len(chunks) * 9 * lines + 1
    out = pl.pallas_call(
        functools.partial(
            collect_kernel, lines, chunks, [a.shape[0] for a in arrays], count
        ),
        name="collect",
        in_specs=[anywhere] * (count + 1),
        out_specs=[anywhere] * (count + 1),
        out_shape=[
            jax.ShapeDtypeStruct((devices * a.shape[0], a.shape[1]), a.dtype) for a in arrays
        ]
        + [jax.ShapeDtypeStruct((2 * tokens.shape[0], tokens.shape[1]), tokens.dtype)],
        scratch_shapes=[
            pltpu.SemaphoreType.DMA((len(chunks) + 1,)),
            pltpu.SemaphoreType.DMA((slots,)),
            pltpu.SemaphoreType.DMA((slots,)),
        ],
        compiler_params=pltpu.CompilerParams(collective_id=1, has_side_effects=True),
    )(*arrays, tokens)
    return list(out[:count]), out[count]


def gather_rows(arrays, axes):
    return [lax.all_gather(a, axes, axis=0, tiled=True) for a in arrays]


def per_device(
    mesh_shape,
    tokens,
    adapter_index,
    norm1_gain,
    norm1_bias,
    qkv_weight,
    qkv_bias,
    proj_weight,
    proj_bias,
    norm2_gain,
    norm2_bias,
    fc1_weight,
    fc1_bias,
    fc2_weight,
    fc2_bias,
    rel_pos_h,
    rel_pos_w,
    qkv_down,
    qkv_up,
    proj_down,
    proj_up,
    fc1_down,
    fc1_up,
    fc2_down,
    fc2_up,
    out_grad,
):
    axes = ("dp", "seq")
    part_count = mesh_shape["seq"]
    devices = mesh_shape["dp"] * part_count
    images, part_len, features = tokens.shape
    length = part_len * part_count
    own_tokens = tokens[0]
    og = out_grad[0]
    place = lax.axis_index("seq").astype(jnp.int32).reshape(1)
    pick = adapter_index

    small = [
        norm1_gain, norm1_bias, qkv_bias, proj_bias, norm2_gain, norm2_bias, fc1_bias, fc2_bias,
        adapter_index.astype(bf16),
    ]
    small_sizes = [a.shape[0] for a in small]
    pack_small = jnp.concatenate(small)
    pack_small = jnp.pad(pack_small, (0, 8 * LANES - pack_small.shape[0])).reshape(8, LANES)
    adapters = [qkv_down, proj_down, fc1_down, fc2_down, qkv_up.T, proj_up.T, fc1_up.T, fc2_up.T]
    widths = [a.shape[0] for a in adapters]
    pack_adapters = jnp.concatenate(adapters, axis=0)

    w_fc1, w_fc2 = gather_rows([fc1_weight, fc2_weight], axes)
    (w_qkv, w_proj, all_adapters, all_small), image_tokens = collect(
        mesh_shape, [qkv_weight, proj_weight, pack_adapters, pack_small], own_tokens
    )

    all_small = all_small.reshape(devices, 8 * LANES)
    vectors, at = [], 0
    for size in small_sizes:
        vectors.append(all_small[:, at : at + size].reshape(1, devices * size))
        at += size
    g1, s1, b_qkv, b_proj, g2, s2, b_fc1, b_fc2, picks = vectors
    all_adapters = all_adapters.reshape(devices, sum(widths), LANES)
    maps, at = [], 0
    for size in widths:
        maps.append(all_adapters[:, at : at + size].reshape(devices * size, LANES))
        at += size
    d_qkv, d_proj, d_fc1, d_fc2, u_qkv, u_proj, u_fc1, u_fc2 = maps

    columns = jnp.arange(LANES, dtype=jnp.int32) // RANK
    mask = (columns[None, :] == adapter_index[:, None]).astype(f32)
    forward_table, back_table, spots, turned_spots = position_tables(rel_pos_h, rel_pos_w, length)
    head_of = jnp.arange(features, dtype=jnp.int32)[None, :] // HEAD_DIM
    head_sums = (head_of == jnp.arange(HEADS, dtype=jnp.int32)[:, None]).astype(bf16)

    heads, mid_qkv = qkv_call(image_tokens, g1, s1, w_qkv, b_qkv, d_qkv, u_qkv, mask)
    att, lse, aux = forward_call(place, heads, forward_table, spots, part_len)
    resid, act_two, mid_proj, mid_fc1 = project_call(
        att, own_tokens, w_proj, b_proj, d_proj, u_proj, mask, g2, s2, d_fc1
    )
    block_out, grad_resid, grad_branch, gd_fc1, gu_fc1, gd_fc2, gu_fc2 = feed_call(
        pick, act_two, resid, og, w_fc1, b_fc1, w_fc2, b_fc2, d_fc1, u_fc1, d_fc2, u_fc2,
        mid_fc1, mask, g2,
    )
    grad_att, inner, gd_proj, gu_proj = unproject_call(
        pick, grad_branch, att, w_proj, d_proj, u_proj, mid_proj, mask, head_sums
    )
    if part_count == 2:
        swap = [(0, 1), (1, 0)]
        their_grad, their_lse, their_inner = (
            lax.ppermute(a, "seq", swap)[None] for a in (grad_att, lse, inner)
        )
    else:
        their_grad, their_lse, their_inner = (
            lax.all_gather(a, "seq", axis=0) for a in (grad_att, lse, inner)
        )
    dq, dk_own, dv_own = own_call(
        place, heads, aux, spots, turned_spots, back_table, grad_att, lse, inner
    )
    dk, dv = other_call(
        place, heads, aux, spots, their_grad, their_lse, their_inner, dk_own, dv_own
    )
    mid_own = lax.dynamic_slice_in_dim(mid_qkv, place[0] * part_len, part_len, 0)
    input_grad, gd_qkv, gu_qkv = unqkv_call(
        pick, dq, dk, dv, w_qkv, d_qkv, u_qkv, mid_own, mask, own_tokens, g1, s1, grad_resid
    )

    terms = [gd_qkv, gd_proj, gd_fc1, gd_fc2, gu_qkv, gu_proj, gu_fc1, gu_fc2]
    sent = jnp.concatenate([t.reshape(RANK, devices, -1) for t in terms], axis=2)
    sent = jnp.transpose(sent, (1, 0, 2))
    received = lax.all_to_all(sent, axes, 0, 0, tiled=True)
    source = picks.reshape(mesh_shape["dp"], part_count)[:, :1]
    source = jnp.broadcast_to(source, (mesh_shape["dp"], part_count)).reshape(1, devices)
    chosen = (jnp.arange(ADAPTERS, dtype=jnp.int32)[:, None] == source.astype(jnp.int32)).astype(
        bf16
    )
    summed = jnp.einsum("ad,drc->arc", chosen, received, preferred_element_type=f32)
    summed = summed.reshape(ADAPTERS * RANK, -1)
    pieces, at = [], 0
    for size in widths:
        pieces.append(summed[:, at : at + size])
        at += size
    return (
        block_out[None],
        input_grad[None],
        pieces[0].T,
        pieces[4],
        pieces[1].T,
        pieces[5],
        pieces[2].T,
        pieces[6],
        pieces[3].T,
        pieces[7],
    )


def solution(mesh):
    both = ("dp", "seq")
    return jax.shard_map(
        functools.partial(per_device, dict(mesh.shape)),
        mesh=mesh,
        in_specs=(
            P("dp", "seq", None),
            P("dp"),
            P(both),
            P(both),
            P(both, None),
            P(both),
            P(both, None),
            P(both),
            P(both),
            P(both),
            P(both, None),
            P(both),
            P(both, None),
            P(both),
            P(),
            P(),
            P(both, None),
            P(None, both),
            P(both, None),
            P(None, both),
            P(both, None),
            P(None, both),
            P(both, None),
            P(None, both),
            P("dp", "seq", None),
        ),
        out_specs=(
            P("dp", "seq", None),
            P("dp", "seq", None),
            P(both, None),
            P(None, both),
            P(both, None),
            P(None, both),
            P(both, None),
            P(None, both),
            P(both, None),
            P(None, both),
        ),
        check_vma=False,
    )
```

time: 2200 us -> 460 us (0.21)
  waiting for transfers between devices: 911 us -> 26 us
  blocking collectives: 441 us -> 0 us
  local copies, waits for them, and re-layouts: 424 us -> 67.3 us
  Pallas kernels: 0 us -> 333 us
  matrix products: 285 us -> 0.21 us
  other arithmetic: 102 us -> 2.74 us
    unnamed x22 -> x2, waiting for transfers between devices: 635 us -> 1.38 us
    all_gather x6 -> x0, blocking collectives: 400 us -> none  [the longest x1 74.3 us: per_device(): lax.all_gather(proj_down, ('dp', 'seq'), axis=0, tiled=True)]
    pallas_call x0 -> x9, Pallas kernels: none -> 333 us  [the longest x1 141 us: collect(): pl.pallas_call(functools.partial(collect_kernel, lines, chunks, [a.shape[...]
    add x5 -> x0, local copies, waits for them, and re-layouts: 294 us -> none  [the longest x4 289 us: score_block(): scores.reshape(HEADS, grid_rows, G, key_grid, G) + along_h[..., None]]
    dot_general x43 -> x1, matrix products: 283 us -> 0.21 us  [per_device(): jnp.einsum('ad,drc->arc', chosen, received, preferred_element_type=f32)]
    reduce_scatter x3 -> x0, waiting for transfers between devices: 276 us -> none  [the longest x1 138 us: per_device(): lax.psum_scatter(upper_fc1, ('dp', 'seq'), scatter_dimension=1, tiled=True)]
    convert_element_type x2 -> x1, local copies, waits for them, and re-layouts: 81.5 us -> 0.1 us  [per_device(): source.astype(jnp.int32)]
    reduce_sum x5 -> x0, other arithmetic: 63.8 us -> none  [the longest x1 45.5 us: query_part(): sum_rows = jnp.sum(grid_scores, axis=4, dtype=jnp.float32)]
  transfers between devices with their start and end apart: 16 -> 6, of which waited for: 7 -> 2; matrix products, arithmetic and copies ran while one was open for 31% -> 10% of each run, Pallas kernels for 0% -> 66%
where the time goes in v1:
time: 460 us; the launch traced here: 451 us
  Pallas kernels  333 us (72%)
  local copies, waits for them, and re-layouts  67.3 us (15%)
  waiting for transfers between devices  26 us (6%)
  between operations  15.4 us (3%)
  starting transfers between devices  7.17 us (2%)
    pallas_call x1, Pallas kernels, collect(): pl.pallas_call(functools.partial(collect_kernel, lines, chunks, [a.shape[...  141 us
    pallas_call x1, Pallas kernels, feed_call(): pl.pallas_call(feed_kernel, name='feed', grid_spec=pltpu.PrefetchScalarGr...  48.3 us
    pallas_call x1, Pallas kernels, own_call(): pl.pallas_call(own_kernel, name='back_own', grid_spec=pltpu.PrefetchScala...  37.8 us
    pallas_call x1, Pallas kernels, forward_call(): pl.pallas_call(forward_kernel, name='attend', grid_spec=pltpu.PrefetchSca...  33.5 us
    unnamed x88, local copies, waits for them, and re-layouts  30.5 us
    pallas_call x1, Pallas kernels, qkv_call(): pl.pallas_call(qkv_kernel, name='qkv', grid=(3,), in_specs=[whole((length...  21 us
    pallas_call x1, Pallas kernels, other_call(): pl.pallas_call(other_kernel, name='back_other', grid_spec=pltpu.PrefetchS...  20.9 us
    all_to_all x1, waiting for transfers between devices, per_device(): received = lax.all_to_all(sent, axes, 0, 0, tiled=True)  14.6 us
  transfers between devices with their start and end apart: 6, of which 2 were waited for; matrix products, arithmetic and copies ran while one was open for 10% of the time, Pallas kernels for 66%

profile of v1, /device:TPU:15, one launch (start us, length us, event | category | flops | bytes accessed | tf_op | source)
XLA Modules:
  0.0 451.5 jit_solution(17293179055230295354)
XLA Ops:
  11.2 5.4 %concatenate.16 = bf16[521]{0:T(1024)(128)(2,1)S(1)} concatenate(bf16[40]{0:T(256)(128)(2,1)} %param.27, bf16[40]{0:T(256)(128)(2,1)} %param.28, bf16[120]{0:T(256)(128)(2,1)} %param.30, bf16[40]{0:T(256)(128)(2,1)} %param.32, bf16[40]{0:T(256)(128)(2,1)} %param.33, bf16[40]{0:T(256)(128)(2,1)} %param.34, bf16[160]{0:T(256)(128)(2,1)} %param.36, bf16[40]{0:T(256)(128)(2,1)} %param.38, ...), dimensions={0} | concatenate | bytes 2084 | tf_op jit(solution)/shard_map/concatenate | solution.py:964
  23.7 141.4 %collect.1 = (bf16[1280,3840]{1,0:T(8,128)(2,1)}, bf16[1280,1280]{1,0:T(8,128)(2,1)}, bf16[20480,128]{1,0:T(8,128)(2,1)}, bf16[256,128]{1,0:T(8,128)(2,1)}, bf16[1024,1280]{1,0:T(8,128)(2,1)}) custom-call(bf16[40,3840]{1,0:T(8,128)(2,1)} %refs_0_.1, bf16[40,1280]{1,0:T(8,128)(2,1)} %refs_1_.1, bf16[640,128]{1,0:T(8,128)(2,1)} %copy-done.29, ...), custom_call_target="tpu_custom_call" | custom-call | tf_op jit(solution)/shard_map/collect/pallas_call | solution.py:896
  167.2 1.3 slice.108
  169.7 2.4 fusion.21
  172.0 21.0 %qkv.1 = (bf16[3,16,1024,128]{3,2,1,0:T(8,128)(2,1)}, bf16[1024,128]{1,0:T(8,128)(2,1)S(1)}) custom-call(bf16[1024,1280]{1,0:T(8,128)(2,1)} %get-tuple-element.43.x_ref, bf16[1,1280]{1,0:T(2,128)(2,1)S(1)} %reshape.310.gain_ref, bf16[1,1280]{1,0:T(2,128)(2,1)S(1)} %reshape.311.shift_ref, bf16[1280,3840]{1,0:T(8,128)(2,1)} %get-tuple-element.45.weight_ref, ...), custom_call_target="tpu_custom_call" | custom-call | flops 10066329600 | bytes 20316160 | tf_op jit(solution)/shard_map/qkv/pallas_call | solution.py:95
  193.1 33.5 %attend.1 = (bf16[512,1280]{1,0:T(8,128)(2,1)S(1)}, f32[16,1,512]{2,1,0:T(1,128)}, bf16[16,1024,128]{2,1,0:T(8,128)(2,1)S(1)}) custom-call(s32[1]{0:T(128)} %bitcast.place_ref, bf16[3,16,1024,128]{3,2,1,0:T(8,128)(2,1)} %get-tuple-element.47.q_ref.k_ref.v_ref, bf16[3,16,1024,128]{3,2,1,0:T(8,128)(2,1)} %get-tuple-element.47.q_ref.k_ref.v_ref, ...), custom_call_target="tpu_custom_call" | custom-call | flops 8589934592 | bytes 16777216 | tf_op jit(solution)/shard_map/attend/pallas_call | solution.py:168
  226.7 2.0 copy-done.1
  230.4 1.4 slice.115
  231.8 1.4 reshape.323.b2_ref
  233.2 1.4 reshape.322.b1_ref
  234.6 1.4 reshape.319.gain_ref
  236.0 1.4 reshape.320.shift_ref
  237.4 1.4 reshape.316.bias_ref
  238.8 1.4 pad_maximum_fusion.table_ref
  240.2 1.6 constant_dynamic-slice_fusion.mid_ref
  244.5 6.8 %project.1 = (f32[512,1280]{1,0:T(8,128)}, bf16[512,1280]{1,0:T(8,128)(2,1)S(1)}, bf16[512,128]{1,0:T(8,128)(2,1)S(1)}, bf16[512,128]{1,0:T(8,128)(2,1)S(1)}) custom-call(bf16[512,1280]{1,0:T(8,128)(2,1)S(1)} %get-tuple-element.48.att_ref, bf16[512,1280]{1,0:T(8,128)(2,1)} %bitcast.56, bf16[1280,1280]{1,0:T(8,128)(2,1)} %get-tuple-element.49.weight_ref, ...), custom_call_target="tpu_custom_call" | custom-call | flops 1677721600 | bytes 11141120 | tf_op jit(solution)/shard_map/project/pallas_call | solution.py:414
  251.3 4.0 fusion.22
  255.3 10.0 %all-gather.5.cloned.1.call-done.w2_ref = bf16[5120,1280]{1,0:T(8,128)(2,1)} async-done(((bf16[160,1280]{1,0:T(8,128)(2,1)}), bf16[5120,1280]{1,0:T(8,128)(2,1)}) %all-gather.5.cloned.1.call-update) | async-done | bytes 13107216 | tf_op jit(solution)/shard_map/all_gather | solution.py:918
  265.4 48.3 %feed.1 = (bf16[512,1280]{1,0:T(8,128)(2,1)}, f32[512,1280]{1,0:T(8,128)}, bf16[512,1280]{1,0:T(8,128)(2,1)}, bf16[16,1280]{1,0:T(8,128)(2,1)}, bf16[16,5120]{1,...) custom-call(s32[1]{0:T(128)} %copy.82.pick_ref, bf16[512,1280]{1,0:T(8,128)(2,1)} %copy-done.24, ...), custom_call_target="tpu_custom_call" | custom-call | flops 26843545600 | bytes 41943040 | tf_op jit(solution)/shard_map/feed/pallas_call | solution.py:507
  313.7 1.3 copy-done.9
  315.0 8.3 %unproject.1 = (bf16[512,1280]{1,0:T(8,128)(2,1)}, f32[16,1,512]{2,1,0:T(1,128)S(1)}, bf16[16,1280]{1,0:T(8,128)(2,1)S(1)}, bf16[16,1280]{1,0:T(8,128)(2,1)S(1)}) custom-call(s32[1]{0:T(128)} %copy.82.pick_ref, bf16[512,1280]{1,0:T(8,128)(2,1)S(1)} %copy-done.9, bf16[512,1280]{1,0:T(8,128)(2,1)} %copy-done, bf16[1280,1280]{1,0:T(8,128)(2,1)} %get-tuple-element.49.weight_ref, ...), custom_call_target="tpu_custom_call" | custom-call | flops 1677721600 | bytes 8519680 | tf_op jit(solution)/shard_map/unproject/pallas_call | solution.py:590
  324.8 37.8 %back_own.1 = (bf16[512,1280]{1,0:T(8,128)(2,1)S(1)}, f32[16,512,128]{2,1,0:T(8,128)S(1)}, f32[16,512,128]{2,1,0:T(8,128)S(1)}) custom-call(s32[1]{0:T(128)} %bitcast.place_ref, bf16[3,16,1024,128]{3,2,1,0:T(8,128)(2,1)} %get-tuple-element.47.q_ref.k_ref.v_ref, bf16[16,1024,128]{2,1,0:T(8,128)(2,1)} %copy-done.1, ...), custom_call_target="tpu_custom_call" | custom-call | flops 17179869184 | bytes 25165824 | tf_op jit(solution)/shard_map/back_own/pallas_call | solution.py:263
  362.6 2.0 copy-done.3
  364.6 1.9 copy-done.5
  369.6 1.2 reshape.330
  372.2 2.2 copy-done.2
  374.4 2.2 copy-done.4
  376.6 20.9 %back_other.1 = (bf16[512,1280]{1,0:T(8,128)(2,1)S(1)}, bf16[512,1280]{1,0:T(8,128)(2,1)S(1)}) custom-call(s32[1]{0:T(128)} %bitcast.place_ref, bf16[3,16,1024,128]{3,2,1,0:T(8,128)(2,1)} %get-tuple-element.47.q_ref.k_ref.v_ref, bf16[16,1024,128]{2,1,0:T(8,128)(2,1)S(1)} %copy-done.2, bf16[3,16,1024,128]{3,2,1,0:T(8,128)(2,1)} %get-tuple-element.47.q_ref.k_ref.v_ref, ...), custom_call_target="tpu_custom_call" | custom-call | flops 4294967296 | bytes 25165824 | tf_op jit(solution)/shard_map/back_other/pallas_call | solution.py:357
  399.7 14.6 %unqkv.1 = (f32[512,1280]{1,0:T(8,128)}, bf16[16,1280]{1,0:T(8,128)(2,1)S(1)}, bf16[16,3840]{1,0:T(8,128)(2,1)S(1)}) custom-call(s32[1]{0:T(128)} %copy.82.pick_ref, bf16[512,1280]{1,0:T(8,128)(2,1)S(1)} %get-tuple-element.60.dq_ref, bf16[512,1280]{1,0:T(8,128)(2,1)} %copy-done.6, bf16[512,1280]{1,0:T(8,128)(2,1)} %copy-done.7, ...), custom_call_target="tpu_custom_call" | custom-call | flops 5033164800 | bytes 22937600 | tf_op jit(solution)/shard_map/unqkv/pallas_call | solution.py:655
  414.9 2.2 concatenate.19
  417.1 5.1 %all-to-all-start = ((bf16[32,16,640]{2,1,0:T(8,128)(2,1)}), bf16[32,16,640]{2,1,0:T(8,128)(2,1)S(1)}, u32[]{:S(2)}, u32[]{:S(2)}) async-start(bf16[32,16,640]{2,1,0:T(8,128)(2,1)} %bitcast.25), calls=%async_computation | async-start | bytes 1310720 | tf_op jit(solution)/shard_map/all_to_all | solution.py:1029
  423.5 14.6 %all-to-all-done = bf16[32,16,640]{2,1,0:T(8,128)(2,1)S(1)} async-done(((bf16[32,16,640]{2,1,0:T(8,128)(2,1)}), bf16[32,16,640]{2,1,0:T(8,128)(2,1)S(1)}, u32[]{:S(2)}, u32[]{:S(2)}) %all-to-all-start) | async-done | bytes 655392 | tf_op jit(solution)/shard_map/all_to_all | solution.py:1029
  (139 shorter events, 34.3 us)
Async XLA Ops:
  7.2 248.2 %all-gather.3.cloned.1.call-start = ((), (), s32[]{:S(2)}) async-start(), calls=%async_computation.1 | async-start | bytes 13516800 | tf_op jit(solution)/shard_map/all_gather | solution.py:918
  7.9 257.5 %all-gather.5.cloned.1.call-start = ((), (), s32[]{:S(2)}) async-start(), calls=%async_computation.2 | async-start | bytes 13516800 | tf_op jit(solution)/shard_map/all_gather | solution.py:918
  168.5 24.6 %copy-start.21 = (f32[1,128]{1,0:T(1,128)}, f32[1,128]{1,0:T(1,128)S(1)}, u32[]{:S(2)}) copy-start(f32[1,128]{1,0:T(1,128)S(1)} %compare_convert_fusion.mask_ref) | copy-start | bytes 1540
  172.0 21.0 %copy-start.10 = (bf16[32,40,128]{2,1,0:T(8,128)(2,1)}, bf16[32,40,128]{2,1,0:T(8,128)(2,1)S(1)}, u32[]{:S(2)}) copy-start(bf16[32,40,128]{2,1,0:T(8,128)(2,1)S(1)} %get-tuple-element.100) | copy-start | bytes 983044
  172.0 69.7 %copy-start.8 = (bf16[32,40,128]{2,1,0:T(8,128)(2,1)}, bf16[32,40,128]{2,1,0:T(8,128)(2,1)S(1)}, u32[]{:S(2)}) copy-start(bf16[32,40,128]{2,1,0:T(8,128)(2,1)S(1)} %get-tuple-element.97) | copy-start | bytes 983044
  193.1 33.6 %copy-start.17 = (bf16[1024,128]{1,0:T(8,128)(2,1)}, bf16[1024,128]{1,0:T(8,128)(2,1)S(1)}, u32[]{:S(2)}) copy-start(bf16[1024,128]{1,0:T(8,128)(2,1)S(1)} %get-tuple-element.65) | copy-start | bytes 786436
  193.1 36.0 %copy-start.31 = (bf16[63,80]{1,0:T(8,128)(2,1)S(1)}, bf16[63,80]{1,0:T(8,128)(2,1)}, u32[]{:S(2)}) copy-start(bf16[63,80]{1,0:T(8,128)(2,1)} %param.39) | copy-start | bytes 30244
  193.1 36.7 %copy-start.32 = (bf16[63,80]{1,0:T(8,128)(2,1)S(1)}, bf16[63,80]{1,0:T(8,128)(2,1)}, u32[]{:S(2)}) copy-start(bf16[63,80]{1,0:T(8,128)(2,1)} %param.40) | copy-start | bytes 30244
  226.7 2.0 copy-start.1
  228.6 22.6 %copy-start = (bf16[512,1280]{1,0:T(8,128)(2,1)}, bf16[512,1280]{1,0:T(8,128)(2,1)S(1)}, u32[]{:S(2)}) copy-start(bf16[512,1280]{1,0:T(8,128)(2,1)S(1)} %get-tuple-element.48.att_ref) | copy-start | bytes 3932164
  228.6 143.5 %collective-permute-start.1 = (f32[16,1,512]{2,1,0:T(1,128)}, f32[16,1,512]{2,1,0:T(1,128)}, u32[]{:S(2)}, u32[]{:S(2)}) collective-permute-start(f32[16,1,512]{2,1,0:T(1,128)} %get-tuple-element.58.lse_ref), channel_id=1, source_target_pairs={{0,1},{1,0},{2,3},{3,2},{4,5},{5,4},{6,7},{7,6},{8,9},{9,8},{10,11... | collective-permute-start | bytes 98312 | tf_op jit(solution)/shard_map/ppermute | solution.py:1009
  251.3 4.0 copy-start.14
  251.3 4.0 copy-start.24
  251.3 4.0 copy-start.25
  265.4 48.3 %copy-start.15 = (bf16[512,128]{1,0:T(8,128)(2,1)S(1)}, bf16[512,128]{1,0:T(8,128)(2,1)}, u32[]{:S(2)}) copy-start(bf16[512,128]{1,0:T(8,128)(2,1)} %copy-done.14) | copy-start | bytes 393220
  265.4 48.3 %copy-start.23 = (f32[1,128]{1,0:T(1,128)S(1)}, f32[1,128]{1,0:T(1,128)}, u32[]{:S(2)}) copy-start(f32[1,128]{1,0:T(1,128)} %copy-done.21) | copy-start | bytes 1540
  315.0 9.8 %copy-start.13 = (bf16[1024,128]{1,0:T(8,128)(2,1)S(1)}, bf16[1024,128]{1,0:T(8,128)(2,1)}, u32[]{:S(2)}) copy-start(bf16[1024,128]{1,0:T(8,128)(2,1)} %get-tuple-element.116.turned_spots_ref) | copy-start | bytes 786436
  315.0 9.8 %copy-start.16 = (bf16[256,128]{1,0:T(8,128)(2,1)S(1)}, bf16[256,128]{1,0:T(8,128)(2,1)}, u32[]{:S(2)}) copy-start(bf16[256,128]{1,0:T(8,128)(2,1)} %pad_maximum_fusion.table_ref) | copy-start | bytes 196612
  323.3 48.9 %collective-permute-start.2 = (f32[16,1,512]{2,1,0:T(1,128)S(1)}, f32[16,1,512]{2,1,0:T(1,128)S(1)}, u32[]{:S(2)}, u32[]{:S(2)}) collective-permute-start(f32[16,1,512]{2,1,0:T(1,128)S(1)} %get-tuple-element.59.inner_ref), channel_id=1, source_target_pairs={{0,1},{1,0},{2,3},{3,2},{4,5},{5,4},{6,7},{7,6},{8,9},{9,8},{10,11... | collective-permute-start | bytes 98312 | tf_op jit(solution)/shard_map/ppermute | solution.py:1009
  324.5 47.7 %collective-permute-start = (bf16[512,1280]{1,0:T(8,128)(2,1)}, bf16[512,1280]{1,0:T(8,128)(2,1)}, u32[]{:S(2)}, u32[]{:S(2)}) collective-permute-start(bf16[512,1280]{1,0:T(8,128)(2,1)} %get-tuple-element.57.grad_ref), channel_id=1, source_target_pairs={{0,1},{1,0},{2,3},{3,2},{4,5},{5,4},{6,7},{7,6},{8,9},{9,8},{10,11... | collective-permute-start | bytes 3932168 | tf_op jit(solution)/shard_map/ppermute | solution.py:1009
  324.8 42.9 %copy-start.34 = (bf16[16,1280]{1,0:T(8,128)(2,1)S(1)}, bf16[16,1280]{1,0:T(8,128)(2,1)}, u32[]{:S(2)}) copy-start(bf16[16,1280]{1,0:T(8,128)(2,1)} %get-tuple-element.70) | copy-start | bytes 122884
  324.8 43.9 %copy-start.33 = (bf16[16,1280]{1,0:T(8,128)(2,1)S(1)}, bf16[16,1280]{1,0:T(8,128)(2,1)}, u32[]{:S(2)}) copy-start(bf16[16,1280]{1,0:T(8,128)(2,1)} %get-tuple-element.75) | copy-start | bytes 122884
  362.6 2.0 copy-start.3
  364.6 1.9 copy-start.5
  366.5 4.5 copy-start.30
  372.2 2.2 copy-start.2
  374.4 2.2 copy-start.4
  376.6 23.1 %copy-start.11 = (bf16[32,40,128]{2,1,0:T(8,128)(2,1)S(1)}, bf16[32,40,128]{2,1,0:T(8,128)(2,1)}, u32[]{:S(2)}) copy-start(bf16[32,40,128]{2,1,0:T(8,128)(2,1)} %copy-done.10) | copy-start | bytes 983044
  376.6 23.1 %copy-start.12 = (bf16[512,128]{1,0:T(8,128)(2,1)S(1)}, bf16[512,128]{1,0:T(8,128)(2,1)}, u32[]{:S(2)}) copy-start(bf16[512,128]{1,0:T(8,128)(2,1)} %constant_dynamic-slice_fusion.mid_ref) | copy-start | bytes 393220
  399.6 15.2 %copy-start.26 = (bf16[16,32,160]{2,0,1:T(8,128)(2,1)S(1)}, bf16[16,32,160]{2,0,1:T(8,128)(2,1)}, u32[]{:S(2)}) copy-start(bf16[16,32,160]{2,0,1:T(8,128)(2,1)} %copy.59) | copy-start | bytes 491524
  399.6 15.3 %copy-start.27 = (bf16[16,32,40]{2,0,1:T(8,128)(2,1)S(1)}, bf16[16,32,40]{2,0,1:T(8,128)(2,1)}, u32[]{:S(2)}) copy-start(bf16[16,32,40]{2,0,1:T(8,128)(2,1)} %copy.58) | copy-start | bytes 122884
  417.1 21.0 %all-to-all-start = ((bf16[32,16,640]{2,1,0:T(8,128)(2,1)}), bf16[32,16,640]{2,1,0:T(8,128)(2,1)S(1)}, u32[]{:S(2)}, u32[]{:S(2)}) async-start(bf16[32,16,640]{2,1,0:T(8,128)(2,1)} %bitcast.25), calls=%async_computation | async-start | bytes 1310720 | tf_op jit(solution)/shard_map/all_to_all | solution.py:1029
  (9 other events, 7.8 us)
Sparse Core Ops, SparseCore 0:
  10.9 153.9 all-gather.2
  167.7 97.6 all-gather.4

commit v2 on v1

v2 whole, which is shorter than its diff:
```python
import functools

import jax
import jax.numpy as jnp
import numpy as np
from jax import lax
from jax.experimental import pallas as pl
from jax.experimental.pallas import tpu as pltpu
from jax.sharding import PartitionSpec as P

HEADS = 16
HEAD_DIM = 80
ADAPTERS = 8
RANK = 16
G = 32
LANES = 128
VECTORS = 8
HALF = HEADS // 2

epsilon = 1e-06
adapter_scale = 0.5
log2e = 1.4426950408889634
score_scale = HEAD_DIM ** (-0.5)
exponent_scale = score_scale * log2e
f32 = jnp.float32
bf16 = jnp.bfloat16


def dot_nn(left, right):
    return lax.dot_general(left, right, (((1,), (0,)), ((), ())), preferred_element_type=f32)


def dot_nt(left, right):
    return lax.dot_general(left, right, (((1,), (1,)), ((), ())), preferred_element_type=f32)


def dot_tn(left, right):
    return lax.dot_general(left, right, (((0,), (0,)), ((), ())), preferred_element_type=f32)


def normalize(values):
    average = jnp.mean(values, axis=-1, keepdims=True)
    centered = values - average
    variance = jnp.mean(centered * centered, axis=-1, keepdims=True)
    inverse = lax.rsqrt(variance + epsilon)
    return centered * inverse, inverse


def norm_back(scaled, normed, inverse):
    return inverse * (
        scaled
        - jnp.mean(scaled, axis=-1, keepdims=True)
        - normed * jnp.mean(scaled * normed, axis=-1, keepdims=True)
    )


def chosen_rows(mask, middle):
    rank = lax.broadcasted_iota(jnp.int32, (RANK, LANES), 0)
    column = lax.broadcasted_iota(jnp.int32, (RANK, LANES), 1)
    pick = jnp.where(column % RANK == rank, jnp.broadcast_to(mask, (RANK, LANES)), 0.0)
    return dot_nt(pick.astype(bf16), middle).astype(bf16)


def params(semantics, megabytes):
    return pltpu.CompilerParams(
        dimension_semantics=semantics, vmem_limit_bytes=megabytes * 1024 * 1024
    )


def whole(shape):
    zeros = (0,) * len(shape)
    return pl.BlockSpec(shape, lambda *_: zeros)


Z, X, Y, S, XD, YD, SX, SY, SD = range(9)


class Courier:
    def __init__(self, lines, chunks, rows_of, sources, targets, local, sends, arrivals):
        self.lines = lines
        self.chunks = chunks
        self.rows_of = rows_of
        self.sources, self.targets = sources, targets
        self.local, self.sends, self.arrivals = local, sends, arrivals
        dp = lax.axis_index("dp")
        self.seq = lax.axis_index("seq")
        self.dp = dp
        self.line, self.column, self.core = dp // 4, (dp // 2) % 2, dp % 2
        line, column, core, seq = self.line, self.column, self.core, self.seq
        self.ahead = [
            self.device(lax.rem(line + k, lines), column, core, seq) for k in range(1, lines)
        ]
        self.across = self.device(line, 1 - column, core, seq)
        self.partner = self.device(line, column, core, 1 - seq)
        self.sibling = self.device(line, column, 1 - core, seq)

    @staticmethod
    def device(z, x, c, y):
        return (z * 4 + x * 2 + c, y)

    def owner(self, k, x, c, y):
        return self.device(lax.rem(self.line + self.lines - k, self.lines), x, c, y)

    def greet(self):
        peers = self.ahead + [self.across, self.partner, self.sibling]
        barrier = pltpu.get_barrier_semaphore()
        for peer in peers:
            pl.semaphore_signal(
                barrier, inc=1, device_id=peer, device_id_type=pl.DeviceIdType.MESH
            )
        pl.semaphore_wait(barrier, len(peers))

    def slot(self, number, kind, k):
        return (number * 9 + kind) * self.lines + k

    def part(self, number, half):
        _, row, height, col, width, share = self.chunks[number]
        if half is None:
            return row, height, col, width
        if width >= 2 * LANES:
            cut = width // LANES * share // 4 * LANES
            return (row, height, col, cut) if half == 0 else (row, height, col + cut, width - cut)
        cut = height // 8 * share // 4 * 8
        return (row, cut, col, width) if half == 0 else (row + cut, height - cut, col, width)

    def place(self, number, owner, half=None):
        array = self.chunks[number][0]
        row, height, col, width = self.part(number, half)
        if height == 0 or width == 0:
            return None
        start = (owner[0] * 2 + owner[1]) * self.rows_of[array] + row
        return self.targets[array].at[pl.ds(pl.multiple_of(start, 8), height), pl.ds(col, width)]

    def like(self, number, half=None):
        array = self.chunks[number][0]
        row, height, col, width = self.part(number, half)
        if height == 0 or width == 0:
            return None
        return self.targets[array].at[pl.ds(row, height), pl.ds(col, width)]

    def send(self, source, target, peer, number, kind, k):
        at = self.slot(number, kind, k)
        pltpu.make_async_remote_copy(
            src_ref=source,
            dst_ref=target,
            send_sem=self.sends.at[at],
            recv_sem=self.arrivals.at[at],
            device_id=peer,
            device_id_type=pl.DeviceIdType.MESH,
        ).start()

    def arrive(self, place, number, kind, k):
        pltpu.make_async_copy(place, place, self.arrivals.at[self.slot(number, kind, k)]).wait()

    def start(self, number):
        array, row, height, col, width, _ = self.chunks[number]
        own = self.sources[array].at[pl.ds(row, height), pl.ds(col, width)]
        place = self.place(number, (self.dp, self.seq))
        for k in range(1, self.lines):
            self.send(own, place, self.ahead[k - 1], number, Z, k)
        self.send(own, place, self.across, number, X, 0)
        self.send(own, place, self.partner, number, Y, 0)
        self.send(own, place, self.sibling, number, S, 0)
        pltpu.make_async_copy(own, place, self.local.at[number]).start()

    def stage_one(self, number, k):
        place = self.place(number, self.owner(k, self.column, self.core, self.seq))
        self.arrive(place, number, Z, k)
        self.send(place, place, self.across, number, X, k)
        self.send(place, place, self.partner, number, Y, k)
        self.send(place, place, self.sibling, number, S, k)

    def stage_two(self, number, k):
        owner = self.owner(k, 1 - self.column, self.core, self.seq)
        place = self.place(number, owner)
        self.arrive(place, number, X, k)
        half = self.place(number, owner, 0)
        if half is not None:
            self.send(half, half, self.partner, number, YD, k)
        self.send(place, place, self.sibling, number, SX, k)
        owner = self.owner(k, self.column, self.core, 1 - self.seq)
        place = self.place(number, owner)
        self.arrive(place, number, Y, k)
        half = self.place(number, owner, 1)
        if half is not None:
            self.send(half, half, self.across, number, XD, k)
        self.send(place, place, self.sibling, number, SY, k)

    def stage_three(self, number, k):
        owner = self.owner(k, 1 - self.column, self.core, 1 - self.seq)
        for half, kind in ((0, YD), (1, XD)):
            piece = self.place(number, owner, half)
            if piece is not None:
                self.arrive(piece, number, kind, k)
        place = self.place(number, owner)
        self.send(place, place, self.sibling, number, SD, k)

    def stage_four(self, number, k):
        for kind, x, y in (
            (S, self.column, self.seq),
            (SX, 1 - self.column, self.seq),
            (SY, self.column, 1 - self.seq),
            (SD, 1 - self.column, 1 - self.seq),
        ):
            place = self.place(number, self.owner(k, x, 1 - self.core, y))
            self.arrive(place, number, kind, k)

    def steps(self):
        stages = (self.stage_one, self.stage_two, self.stage_three, self.stage_four)
        order = []
        for tick in range(len(self.chunks) + 3):
            for lag, stage in enumerate(stages):
                if 0 <= tick - lag < len(self.chunks):
                    for k in range(1 if lag == 0 else 0, self.lines):
                        order.append(functools.partial(stage, tick - lag, k))
        return order

    def finish(self):
        for number in range(len(self.chunks)):
            like = self.like(number)
            pltpu.make_async_copy(like, like, self.local.at[number]).wait()
            for kind in range(9):
                half = {YD: 0, XD: 1}.get(kind)
                like = self.like(number, half)
                for k in range(self.lines):
                    if like is not None and not (kind == Z and k == 0):
                        sem = self.sends.at[self.slot(number, kind, k)]
                        pltpu.make_async_copy(like, like, sem).wait()


def cut_chunks(arrays, share=2):
    chunks = []
    for index, array in enumerate(arrays):
        height, width = array.shape
        wide, tall = width, height
        if height * wide * 2 > 120_000 and wide > 1280:
            wide = next(w for w in range(1280, 0, -LANES) if width % w == 0)
        while tall * wide * 2 > 120_000 and tall % 16 == 0:
            tall //= 2
        for row in range(0, height, tall):
            for col in range(0, width, wide):
                chunks.append((index, row, tall, col, wide, share))
    return chunks


def courier_lines(mesh_shape, arrays):
    lines = mesh_shape["dp"] // 4
    fits = mesh_shape["seq"] == 2 and mesh_shape["dp"] == 4 * lines and 2 <= lines <= 4
    return lines if fits and not any(a.shape[0] % 8 for a in arrays) else None


def courier_scratch(lines, chunks):
    slots = len(chunks) * 9 * lines
    return [
        pltpu.SemaphoreType.DMA((len(chunks),)),
        pltpu.SemaphoreType.DMA((slots,)),
        pltpu.SemaphoreType.DMA((slots,)),
    ]


def gathered_shapes(devices, arrays):
    return [jax.ShapeDtypeStruct((devices * a.shape[0], a.shape[1]), a.dtype) for a in arrays]


def collect_kernel(lines, chunks, rows_of, count, *refs):
    sources, tokens = refs[:count], refs[count]
    targets, other = refs[count + 1 : 2 * count + 1], refs[2 * count + 1]
    local, sends, arrivals, token_sem = refs[2 * count + 2 :]
    courier = Courier(lines, chunks, rows_of, sources, targets, local, sends, arrivals)
    courier.greet()
    passed = pltpu.make_async_remote_copy(
        src_ref=tokens,
        dst_ref=other,
        send_sem=token_sem.at[0],
        recv_sem=token_sem.at[1],
        device_id=courier.partner,
        device_id_type=pl.DeviceIdType.MESH,
    )
    for number in range(len(chunks)):
        courier.start(number)
    passed.start()
    for step in courier.steps():
        step()
    passed.wait()
    courier.finish()


def collect(mesh_shape, arrays, tokens):
    axes = ("dp", "seq")
    lines = courier_lines(mesh_shape, arrays)
    if lines is None:
        gathered = [lax.all_gather(a, axes, axis=0, tiled=True) for a in arrays]
        return gathered, [lax.all_gather(tokens, "seq", axis=0, tiled=True)]
    chunks = cut_chunks(arrays, 1)
    anywhere = pl.BlockSpec(memory_space=pl.ANY)
    count = len(arrays)
    out = pl.pallas_call(
        functools.partial(collect_kernel, lines, chunks, [a.shape[0] for a in arrays], count),
        name="collect",
        in_specs=[anywhere] * (count + 1),
        out_specs=[anywhere] * (count + 1),
        out_shape=gathered_shapes(mesh_shape["dp"] * 2, arrays)
        + [jax.ShapeDtypeStruct(tokens.shape, tokens.dtype)],
        scratch_shapes=courier_scratch(lines, chunks) + [pltpu.SemaphoreType.DMA((2,))],
        compiler_params=pltpu.CompilerParams(collective_id=1, has_side_effects=True),
    )(*arrays, tokens)
    return list(out[:count]), [tokens, out[count]]


def qkv_part(part, blocks, gain_ref, shift_ref, weight_ref, bias_ref, down_ref, up_ref, mask_ref,
             heads, mid_ref, act_ref, pause):
    length = act_ref.shape[0]

    @pl.when(part == 0)
    def _():
        part_len = length // len(blocks)
        for index, block in enumerate(blocks):
            place = 0
            if len(blocks) == 2:
                seq = lax.axis_index("seq")
                place = pl.multiple_of((seq if index == 0 else 1 - seq) * part_len, G)
            normed, _ = normalize(block[...].astype(f32))
            act = normed * gain_ref[...].astype(f32) + shift_ref[...].astype(f32)
            act_ref[pl.ds(place, part_len), :] = act.astype(bf16)
        mid_ref[...] = (dot_nn(act_ref[...], down_ref[...]) * mask_ref[...]).astype(bf16)

    rows = min(256, length)
    lane = lax.broadcasted_iota(jnp.int32, (rows, LANES - HEAD_DIM), 1)
    pad = jnp.where((lane == 0) & (part == 2), 1.0, 0.0).astype(bf16)
    for start in range(0, length, rows):
        here = pl.ds(start, rows)
        block = dot_nn(act_ref[here, :], weight_ref[...])
        block = block + bias_ref[...].astype(f32)
        block = block + adapter_scale * dot_nt(mid_ref[here, :], up_ref[...])
        block = block.astype(bf16)
        for head in range(HEADS):
            heads[part, head, here, 0:HEAD_DIM] = block[:, head * HEAD_DIM : (head + 1) * HEAD_DIM]
            heads[part, head, here, HEAD_DIM:LANES] = pad
        pause(start // rows)


def attend_head(head, own, heads, table_ref, spots_ref, att_ref, lse_ref, aux_ref, pause):
    pause(0)
    length = heads.shape[2]
    part_len = att_ref.shape[0]
    lane = lax.broadcasted_iota(jnp.int32, (G, LANES), 1)
    first = lane < LANES // 2
    even = (lane // G) % 2 == 0
    raw = dot_nn(heads[0, head], table_ref[...]) * (HEAD_DIM**0.5)
    for row in range(length // G):
        block = raw[row * G : (row + 1) * G, :]
        high = block.astype(bf16).astype(f32)
        mixed_h = jnp.where(first, high[:, :LANES], block[:, :LANES] - high[:, :LANES])
        mixed_w = jnp.where(first, high[:, LANES:], block[:, LANES:] - high[:, LANES:])
        along_h = pltpu.roll(mixed_h, LANES - G + 1 + row, 1)
        along_w = pltpu.roll(mixed_w, 1, 1, stride=1, stride_axis=0)
        aux_ref[0, pl.ds(row * G, G), :] = jnp.where(even, along_h, along_w).astype(bf16)
    pause(1)
    left = jnp.concatenate([heads[0, head, own, :], aux_ref[0, own, :]], axis=1)
    right = jnp.concatenate([heads[1, head], spots_ref[...]], axis=1)
    scores = dot_nt(left, right)
    top = jnp.max(scores, axis=1, keepdims=True)
    shares = jnp.exp2((scores - top) * exponent_scale).astype(bf16)
    mixed = dot_nn(shares, heads[2, head])
    total = mixed[:, HEAD_DIM : HEAD_DIM + 1]
    att = (mixed[:, :HEAD_DIM] / total).astype(bf16)
    logs = top * exponent_scale + jnp.log2(total)
    lse_ref[0] = jnp.transpose(jnp.broadcast_to(logs, (part_len, LANES)))[0:1, :]
    for slot in range(HALF):

        @pl.when(head % HALF == slot)
        def _():
            att_ref[:, slot * HEAD_DIM : (slot + 1) * HEAD_DIM] = att


def front_kernel(
    lines, chunks, rows_of, count, pair,
    gain_ref, shift_ref, weight_ref, bias_ref, down_ref, up_ref, mask_ref, table_ref,
    spots_ref, *refs,
):
    blocks, refs = refs[:pair], refs[pair:]
    sources = refs[:count]
    heads_out, mid_ref, att_ref, lse_ref, aux_ref = refs[count : count + 5]
    targets = refs[count + 5 : 2 * count + 5]
    heads, act_ref, out_sem = refs[2 * count + 5 : 2 * count + 8]
    step = pl.program_id(0)
    last = pl.num_programs(0) - 1
    courier = None
    plan = {}
    if count:
        courier = Courier(lines, chunks, rows_of, sources, targets, *refs[2 * count + 8 :])

        @pl.when(step == 0)
        def _():
            courier.greet()
            for number in range(len(chunks)):
                courier.start(number)

        pieces = act_ref.shape[0] // min(256, act_ref.shape[0])
        places = [(part, piece, 7.0 / pieces) for part in range(3) for piece in range(pieces)]
        places += [(3 + head, piece, 1.0) for head in range(HEADS) for piece in range(2)]
        work = courier.steps()
        whole_time = sum(p[2] for p in places)
        done, spent = 0, 0.0
        for at, piece, time in places:
            spent += time
            upto = min(len(work), int(len(work) * spent / whole_time + 1e-6))
            plan[at, piece] = work[done:upto]
            done = upto

    def pause(first, count_of):
        def run(piece):
            for at in range(first, first + count_of):
                items = plan.get((at, piece))
                if items:

                    @pl.when(step == at)
                    def _():
                        for item in items:
                            item()

        return run

    @pl.when(step < 3)
    def _():
        qkv_part(
            step, blocks, gain_ref, shift_ref, weight_ref, bias_ref, down_ref, up_ref, mask_ref,
            heads, mid_ref, act_ref, pause(0, 3),
        )
        pltpu.make_async_copy(heads.at[step], heads_out.at[step], out_sem.at[step]).start()

    part_len = att_ref.shape[0]
    own = pl.ds(pl.multiple_of(lax.axis_index("seq") * part_len, G), part_len)

    @pl.when(step >= 3)
    def _():
        attend_head(
            step - 3, own, heads, table_ref, spots_ref, att_ref, lse_ref, aux_ref, pause(3, HEADS)
        )

    @pl.when(step == last)
    def _():
        for part in range(3):
            pltpu.make_async_copy(heads.at[part], heads_out.at[part], out_sem.at[part]).wait()
        if courier is not None:
            courier.finish()


def front_call(
    mesh_shape, part_len, tokens, gain, shift, weight, bias, down, up, mask, table, spots, arrays
):
    length = sum(t.shape[0] for t in tokens)
    features = weight.shape[0]
    lines = courier_lines(mesh_shape, arrays)
    later = []
    if lines is None:
        axes = ("dp", "seq")
        later = [lax.all_gather(a, axes, axis=0, tiled=True) for a in arrays]
        arrays = []
    chunks = cut_chunks(arrays)
    count = len(arrays)
    anywhere = pl.BlockSpec(memory_space=pl.ANY)

    def head(i):
        return jnp.maximum(i - 3, 0)

    def part(i):
        return jnp.minimum(i, 2)

    def fixed(shape):
        zeros = (0,) * len(shape)
        return pl.BlockSpec(shape, lambda i: zeros, pipeline_mode=pl.Buffered(1))

    options = dict(collective_id=2, has_side_effects=True) if count else {}
    out = pl.pallas_call(
        functools.partial(
            front_kernel, lines, chunks, [a.shape[0] for a in arrays], count, len(tokens)
        ),
        name="front",
        grid=(3 + HEADS,),
        in_specs=[
            fixed((1, features)),
            fixed((1, features)),
            pl.BlockSpec((features, features), lambda i: (0, part(i))),
            pl.BlockSpec((1, features), lambda i: (0, part(i))),
            fixed((features, LANES)),
            pl.BlockSpec((features, LANES), lambda i: (part(i), 0)),
            fixed((1, LANES)),
            fixed((LANES, 2 * LANES)),
            fixed((length, LANES)),
        ]
        + [fixed(t.shape) for t in tokens]
        + [anywhere] * count,
        out_specs=[
            anywhere,
            whole((length, LANES)),
            pl.BlockSpec((part_len, features // 2), lambda i: (0, head(i) // HALF)),
            pl.BlockSpec((1, 1, part_len), lambda i: (head(i), 0, 0)),
            pl.BlockSpec((1, length, LANES), lambda i: (head(i), 0, 0)),
        ]
        + [anywhere] * count,
        out_shape=[
            jax.ShapeDtypeStruct((3, HEADS, length, LANES), bf16),
            jax.ShapeDtypeStruct((length, LANES), bf16),
            jax.ShapeDtypeStruct((part_len, features), bf16),
            jax.ShapeDtypeStruct((HEADS, 1, part_len), f32),
            jax.ShapeDtypeStruct((HEADS, length, LANES), bf16),
        ]
        + gathered_shapes(mesh_shape["dp"] * mesh_shape["seq"], arrays),
        scratch_shapes=[
            pltpu.VMEM((3, HEADS, length, LANES), bf16),
            pltpu.VMEM((length, features), bf16),
            pltpu.SemaphoreType.DMA((3,)),
        ]
        + (courier_scratch(lines, chunks) if count else []),
        compiler_params=pltpu.CompilerParams(
            dimension_semantics=("arbitrary",), vmem_limit_bytes=58 * 1024 * 1024, **options
        ),
        cost_estimate=pl.CostEstimate(
            flops=6 * length * features * features
            + 8 * HEADS * part_len * length * LANES,
            bytes_accessed=2 * (3 * features * features + 8 * length * features),
            transcendentals=HEADS * part_len * length,
        ),
    )(gain, shift, weight, bias, down, up, mask, table, spots, *tokens, *arrays)
    return out[:5], list(out[5:]) + later


def head_lanes(source, head, padded):
    padded[:, HEAD_DIM:LANES] = jnp.zeros((padded.shape[0], LANES - HEAD_DIM), bf16)
    for slot in range(HALF):

        @pl.when(head % HALF == slot)
        def _():
            padded[:, 0:HEAD_DIM] = source[:, slot * HEAD_DIM : (slot + 1) * HEAD_DIM]


def own_kernel(
    place_ref, q_ref, aux_ref, k_ref, v_ref, spots_ref, turned_spots_ref, table_ref, grad_ref,
    lse_ref, inner_ref, dq_ref, dk_ref, dv_ref, shares_ref, dscores_ref, padded,
):
    head = pl.program_id(0)
    part_len = q_ref.shape[2]
    head_lanes(grad_ref, head, padded)
    queries = q_ref[0, 0]
    keys = k_ref[0, 0]
    left = jnp.concatenate([keys, spots_ref[...]], axis=1)
    right = jnp.concatenate([queries, aux_ref[0]], axis=1)
    shares = jnp.exp2(dot_nt(left, right) * exponent_scale - lse_ref[0])
    grad_shares = dot_nt(v_ref[0, 0], padded[...])
    shares_ref[...] = shares.astype(bf16)
    dscores_ref[...] = (shares * (grad_shares - inner_ref[0])).astype(bf16)
    flat = dot_tn(jnp.concatenate([keys, turned_spots_ref[...]], axis=1), dscores_ref[...])
    turned = jnp.transpose(flat)
    lane = lax.broadcasted_iota(jnp.int32, (G, LANES), 1)
    first = lane < LANES // 2
    even = (lane // G) % 2 == 0
    start = place_ref[0] * (part_len // G)
    pieces_h, pieces_w = [], []
    for row in range(part_len // G):
        sums = turned[row * G : (row + 1) * G, LANES:]
        high = sums.astype(bf16).astype(f32)
        mixed = jnp.where(first, high, sums - high)
        pieces_h.append(pltpu.roll(jnp.where(even, mixed, 0.0), start + row, 1))
        pieces_w.append(
            pltpu.roll(jnp.where(even, 0.0, mixed), LANES - G, 1, stride=1, stride_axis=0)
        )
    spread = jnp.concatenate(
        [jnp.concatenate(pieces_h, axis=0), jnp.concatenate(pieces_w, axis=0)], axis=1
    ).astype(bf16)
    grad_query = turned[:, :LANES] * score_scale + dot_nn(spread, table_ref[...])
    grad_query = grad_query[:, :HEAD_DIM].astype(bf16)
    for slot in range(HALF):

        @pl.when(head % HALF == slot)
        def _():
            dq_ref[:, slot * HEAD_DIM : (slot + 1) * HEAD_DIM] = grad_query

    here = pl.ds(pl.multiple_of(place_ref[0] * part_len, G), part_len)
    dk_ref[0] = dot_nn(dscores_ref[here, :], queries)
    dv_ref[0] = dot_nn(shares_ref[here, :], padded[...])


def own_call(place, heads, aux, spots, turned_spots, table, grad, lse, inner):
    length = heads.shape[2]
    part_len, features = grad.shape

    def part(index):
        return pl.BlockSpec((1, 1, length, LANES), lambda n, s: (index, n, 0, 0))

    return pl.pallas_call(
        own_kernel,
        name="back_own",
        grid_spec=pltpu.PrefetchScalarGridSpec(
            num_scalar_prefetch=1,
            grid=(HEADS,),
            in_specs=[
                pl.BlockSpec((1, 1, part_len, LANES), lambda n, s: (0, n, s[0], 0)),
                pl.BlockSpec((1, part_len, LANES), lambda n, s: (n, s[0], 0)),
                part(1),
                part(2),
                whole((length, LANES)),
                whole((length, LANES)),
                whole((2 * LANES, LANES)),
                pl.BlockSpec((part_len, features // 2), lambda n, s: (0, n // HALF)),
                pl.BlockSpec((1, 1, part_len), lambda n, s: (n, 0, 0)),
                pl.BlockSpec((1, 1, part_len), lambda n, s: (n, 0, 0)),
            ],
            out_specs=[
                pl.BlockSpec((part_len, features // 2), lambda n, s: (0, n // HALF)),
                pl.BlockSpec((1, part_len, LANES), lambda n, s: (n, 0, 0)),
                pl.BlockSpec((1, part_len, LANES), lambda n, s: (n, 0, 0)),
            ],
            scratch_shapes=[
                pltpu.VMEM((length, part_len), bf16),
                pltpu.VMEM((length, part_len), bf16),
                pltpu.VMEM((part_len, LANES), bf16),
            ],
        ),
        out_shape=[
            jax.ShapeDtypeStruct((part_len, features), bf16),
            jax.ShapeDtypeStruct((HEADS, part_len, LANES), f32),
            jax.ShapeDtypeStruct((HEADS, part_len, LANES), f32),
        ],
        compiler_params=params(("arbitrary",), 40),
        cost_estimate=pl.CostEstimate(
            flops=8 * HEADS * part_len * length * LANES * 2,
            bytes_accessed=12 * HEADS * length * LANES,
            transcendentals=HEADS * part_len * length,
        ),
    )(place, heads, aux, heads, heads, spots, turned_spots, table, grad, lse, inner)


def other_kernel(
    place_ref, q_ref, aux_ref, k_ref, v_ref, spots_ref, grad_ref, lse_ref, inner_ref, dk_in, dv_in,
    dk_ref, dv_ref, dk_sum, dv_sum, padded,
):
    head = pl.program_id(0)
    step = pl.program_id(1)
    head_lanes(grad_ref.at[0], head, padded)
    queries = q_ref[0, 0]
    left = jnp.concatenate([k_ref[0, 0], spots_ref[...]], axis=1)
    right = jnp.concatenate([queries, aux_ref[0]], axis=1)
    shares = jnp.exp2(dot_nt(left, right) * exponent_scale - lse_ref[0, 0])
    grad_shares = dot_nt(v_ref[0, 0], padded[...])
    dscores = (shares * (grad_shares - inner_ref[0, 0])).astype(bf16)

    @pl.when(step == 0)
    def _():
        dk_sum[...] = dk_in[0]
        dv_sum[...] = dv_in[0]

    dk_sum[...] += dot_nn(dscores, queries)
    dv_sum[...] += dot_nn(shares.astype(bf16), padded[...])

    @pl.when(step == pl.num_programs(1) - 1)
    def _():
        grad_key = (dk_sum[:, :HEAD_DIM] * score_scale).astype(bf16)
        grad_value = dv_sum[:, :HEAD_DIM].astype(bf16)
        for slot in range(HALF):

            @pl.when(head % HALF == slot)
            def _():
                dk_ref[:, slot * HEAD_DIM : (slot + 1) * HEAD_DIM] = grad_key
                dv_ref[:, slot * HEAD_DIM : (slot + 1) * HEAD_DIM] = grad_value


def other_call(place, heads, aux, spots, grads, lses, inners, dk, dv):
    length = heads.shape[2]
    blocks, part_len, features = grads.shape
    count = length // part_len

    def theirs(i, s):
        return lax.rem(s[0] + 1 + i, count)

    def given(i, s):
        return theirs(i, s) if blocks > 1 else 0

    def own(index):
        return pl.BlockSpec((1, 1, part_len, LANES), lambda n, i, s: (index, n, s[0], 0))

    stats = pl.BlockSpec((1, 1, 1, part_len), lambda n, i, s: (given(i, s), n, 0, 0))
    sums = pl.BlockSpec((1, part_len, LANES), lambda n, i, s: (n, 0, 0))
    dense = pl.BlockSpec((part_len, features // 2), lambda n, i, s: (0, n // HALF))
    return pl.pallas_call(
        other_kernel,
        name="back_other",
        grid_spec=pltpu.PrefetchScalarGridSpec(
            num_scalar_prefetch=1,
            grid=(HEADS, count - 1),
            in_specs=[
                pl.BlockSpec((1, 1, part_len, LANES), lambda n, i, s: (0, n, theirs(i, s), 0)),
                pl.BlockSpec((1, part_len, LANES), lambda n, i, s: (n, theirs(i, s), 0)),
                own(1),
                own(2),
                pl.BlockSpec((part_len, LANES), lambda n, i, s: (s[0], 0)),
                pl.BlockSpec(
                    (1, part_len, features // 2), lambda n, i, s: (given(i, s), 0, n // HALF)
                ),
                stats,
                stats,
                sums,
                sums,
            ],
            out_specs=[dense, dense],
            scratch_shapes=[
                pltpu.VMEM((part_len, LANES), f32),
                pltpu.VMEM((part_len, LANES), f32),
                pltpu.VMEM((part_len, LANES), bf16),
            ],
        ),
        out_shape=[
            jax.ShapeDtypeStruct((part_len, features), bf16),
            jax.ShapeDtypeStruct((part_len, features), bf16),
        ],
        compiler_params=params(("arbitrary", "arbitrary"), 40),
        cost_estimate=pl.CostEstimate(
            flops=4 * HEADS * part_len * (length - part_len) * LANES * 2,
            bytes_accessed=12 * HEADS * length * LANES,
            transcendentals=HEADS * part_len * (length - part_len),
        ),
    )(place, heads, aux, heads, heads, spots, grads, lses, inners, dk, dv)


def gelu_parts(hidden):
    size = jnp.abs(hidden) * (0.5**0.5)
    bell = jnp.exp2(hidden * hidden * (-0.5 * log2e))
    t = 1.0 / (1.0 + 0.3275911 * size)
    poly = t * (
        0.254829592
        + t * (-0.284496736 + t * (1.421413741 + t * (-1.453152027 + t * 1.061405429)))
    )
    tail = 0.5 * poly * bell
    cumulative = jnp.where(hidden < 0.0, tail, 1.0 - tail)
    return hidden * cumulative, cumulative + hidden * bell * 0.3989422804014327


def before_kernel(
    att_ref, x_ref, og_ref, wp_ref, bp_ref, dp_ref, up_ref, mask_ref, gain_ref, shift_ref,
    w2_ref, down1_ref, down2_ref, up2_ref,
    resid_ref, act_ref, midp_ref, mid1_ref, gm2_ref, grad_act_ref,
):
    mask = mask_ref[...]

    @pl.when(pl.program_id(0) == 0)
    def _():
        att = att_ref[...]
        midp_ref[...] = (dot_nn(att, dp_ref[...]) * mask).astype(bf16)
        branch = dot_nn(att, wp_ref[...]) + bp_ref[...]
        branch = branch + adapter_scale * dot_nt(midp_ref[...], up_ref[...])
        resid = x_ref[...].astype(f32) + branch
        resid_ref[...] = resid
        normed, _ = normalize(resid)
        act_ref[...] = (normed * gain_ref[...] + shift_ref[...]).astype(bf16)
        mid1_ref[...] = (dot_nn(act_ref[...], down1_ref[...]) * mask).astype(bf16)
        middle = adapter_scale * dot_nn(og_ref[...], up2_ref[...]) * mask
        gm2_ref[...] = middle.astype(bf16)

    grad_act_ref[...] = dot_nt(og_ref[...], w2_ref[...]) + dot_nt(gm2_ref[...], down2_ref[...])


def before_call(att, x, og, wp, bp, dp, up, mask, gain, shift, w2, down1, down2, up2):
    rows, features = att.shape
    wide = w2.shape[0]
    block = 1024

    def fixed(shape):
        zeros = (0,) * len(shape)
        return pl.BlockSpec(shape, lambda j: zeros, pipeline_mode=pl.Buffered(1))

    ins = [att, x, og, wp, bp, dp, up, mask, gain, shift, w2, down1, down2, up2]
    specs = [fixed(a.shape) for a in ins]
    specs[10] = pl.BlockSpec((block, features), lambda j: (j, 0))
    specs[12] = pl.BlockSpec((block, LANES), lambda j: (j, 0))
    shapes = [
        jax.ShapeDtypeStruct((rows, features), f32),
        jax.ShapeDtypeStruct((rows, features), bf16),
        jax.ShapeDtypeStruct((rows, LANES), bf16),
        jax.ShapeDtypeStruct((rows, LANES), bf16),
        jax.ShapeDtypeStruct((rows, LANES), bf16),
        jax.ShapeDtypeStruct((rows, wide), f32),
    ]
    return pl.pallas_call(
        before_kernel,
        name="before",
        grid=(wide // block,),
        in_specs=specs,
        out_specs=[fixed(a.shape) for a in shapes[:5]]
        + [pl.BlockSpec((rows, block), lambda j: (0, j))],
        out_shape=shapes,
        compiler_params=params(("arbitrary",), 56),
        cost_estimate=pl.CostEstimate(
            flops=2 * rows * features * (wide + features),
            bytes_accessed=2 * features * wide + 4 * rows * wide + 16 * rows * features,
            transcendentals=0,
        ),
    )(*ins)


def feed_kernel(
    resid_ref, act_ref, mid1_ref, gm2_ref, grad_act_ref, og_ref, mask_ref, gain_ref,
    w1_ref, b1_ref, w2_ref, b2_ref, down1_ref, up1_ref, down2_ref, up2_ref,
    out_ref, grad_ref, branch_ref, gd1_ref, gu1_ref, gd2_ref, gu2_ref,
    total, back, mid2_sum, gm1_sum, gm2_t, mid1_t,
):
    step = pl.program_id(0)
    steps = pl.num_programs(0)
    mask = mask_ref[...]

    @pl.when(step == 0)
    def _():
        total[...] = jnp.zeros_like(total)
        back[...] = jnp.zeros_like(back)
        mid2_sum[...] = jnp.zeros_like(mid2_sum)
        gm1_sum[...] = jnp.zeros_like(gm1_sum)
        gm2_t[...] = chosen_rows(mask, gm2_ref[...])
        mid1_t[...] = chosen_rows(mask, mid1_ref[...])

    weight = w1_ref[...]
    hidden = dot_nn(act_ref[...], weight) + b1_ref[...]
    hidden = hidden + adapter_scale * dot_nt(mid1_ref[...], up1_ref[...])
    value, slope = gelu_parts(hidden)
    activated = value.astype(bf16)
    grad_hidden = (grad_act_ref[...] * slope).astype(bf16)
    total[...] += dot_nn(activated, w2_ref[...])
    mid2_sum[...] += dot_nn(activated, down2_ref[...])
    back[...] += dot_nt(grad_hidden, weight)
    gm1_sum[...] += dot_nn(grad_hidden, up1_ref[...])
    gd2_ref[...] = dot_nn(gm2_t[...], activated).astype(bf16)
    gu1_ref[...] = (adapter_scale * dot_nn(mid1_t[...], grad_hidden)).astype(bf16)

    @pl.when(step == steps - 1)
    def _():
        mid2 = mid2_sum[...] * mask
        mid2_low = mid2.astype(bf16)
        resid = resid_ref[...]
        final = resid + total[...] + b2_ref[...]
        final = final + adapter_scale * dot_nt(mid2_low, up2_ref[...])
        out_ref[...] = final.astype(bf16)
        gm1 = adapter_scale * gm1_sum[...] * mask
        gm1_low = gm1.astype(bf16)
        upstream = back[...] + dot_nt(gm1_low, down1_ref[...])
        normed, inverse = normalize(resid)
        grad = og_ref[...].astype(f32) + norm_back(upstream * gain_ref[...], normed, inverse)
        grad_ref[...] = grad
        branch_ref[...] = grad.astype(bf16)
        gd1_ref[...] = dot_nn(chosen_rows(mask, gm1_low), act_ref[...]).astype(bf16)
        gu2_ref[...] = (adapter_scale * dot_nn(chosen_rows(mask, mid2_low), og_ref[...])).astype(bf16)


def feed_call(
    resid, act, mid1, gm2, grad_act, og, mask, gain, w1, b1, w2, b2, down1, up1, down2, up2
):
    rows, features = act.shape
    wide = b1.shape[1]
    block = 512

    def fixed(shape):
        zeros = (0,) * len(shape)
        return pl.BlockSpec(shape, lambda j: zeros, pipeline_mode=pl.Buffered(1))

    def by_columns(height):
        return pl.BlockSpec((height, block), lambda j: (0, j))

    def by_rows(width):
        return pl.BlockSpec((block, width), lambda j: (j, 0))

    ins = [
        resid, act, mid1, gm2, grad_act, og, mask, gain, w1, b1, w2, b2, down1, up1, down2, up2
    ]
    specs = [fixed(a.shape) for a in ins]
    specs[4] = by_columns(rows)
    specs[8] = by_columns(features)
    specs[9] = by_columns(1)
    specs[10] = by_rows(features)
    specs[13] = by_rows(LANES)
    specs[14] = by_rows(LANES)
    return pl.pallas_call(
        feed_kernel,
        name="feed",
        grid=(wide // block,),
        in_specs=specs,
        out_specs=[
            fixed((rows, features)),
            fixed((rows, features)),
            fixed((rows, features)),
            fixed((RANK, features)),
            by_columns(RANK),
            by_columns(RANK),
            fixed((RANK, features)),
        ],
        scratch_shapes=[
            pltpu.VMEM((rows, features), f32),
            pltpu.VMEM((rows, features), f32),
            pltpu.VMEM((rows, LANES), f32),
            pltpu.VMEM((rows, LANES), f32),
            pltpu.VMEM((RANK, rows), bf16),
            pltpu.VMEM((RANK, rows), bf16),
        ],
        out_shape=[
            jax.ShapeDtypeStruct((rows, features), bf16),
            jax.ShapeDtypeStruct((rows, features), f32),
            jax.ShapeDtypeStruct((rows, features), bf16),
            jax.ShapeDtypeStruct((RANK, features), bf16),
            jax.ShapeDtypeStruct((RANK, wide), bf16),
            jax.ShapeDtypeStruct((RANK, wide), bf16),
            jax.ShapeDtypeStruct((RANK, features), bf16),
        ],
        compiler_params=params(("arbitrary",), 58),
        cost_estimate=pl.CostEstimate(
            flops=6 * rows * features * wide,
            bytes_accessed=4 * features * wide + 4 * rows * wide + 24 * rows * features,
            transcendentals=2 * rows * wide,
        ),
    )(*ins)


def unproject_kernel(
    branch_ref, att_ref, weight_ref, down_ref, up_ref, mid_ref, mask_ref, sums_ref,
    grad_ref, inner_ref, gd_ref, gu_ref,
):
    branch = branch_ref[...]
    att = att_ref[...]
    middle = (adapter_scale * dot_nn(branch, up_ref[...]) * mask_ref[...]).astype(bf16)
    grad = dot_nt(branch, weight_ref[...]) + dot_nt(middle, down_ref[...])
    grad_ref[...] = grad.astype(bf16)
    product = grad_ref[...].astype(f32) * att.astype(f32)
    high = product.astype(bf16)
    low = (product - high.astype(f32)).astype(bf16)
    inner = dot_nt(sums_ref[...], high) + dot_nt(sums_ref[...], low)
    for head in range(HEADS):
        inner_ref[head] = inner[head : head + 1, :]
    gd_ref[...] = dot_nn(chosen_rows(mask_ref[...], middle), att).astype(bf16)
    own_t = chosen_rows(mask_ref[...], mid_ref[...])
    gu_ref[...] = (adapter_scale * dot_nn(own_t, branch)).astype(bf16)


def unproject_call(branch, att, weight, down, up, mid, mask, sums):
    rows, features = branch.shape
    return pl.pallas_call(
        unproject_kernel,
        name="unproject",
        out_shape=[
            jax.ShapeDtypeStruct((rows, features), bf16),
            jax.ShapeDtypeStruct((HEADS, 1, rows), f32),
            jax.ShapeDtypeStruct((RANK, features), bf16),
            jax.ShapeDtypeStruct((RANK, features), bf16),
        ],
        compiler_params=params(None, 50),
        cost_estimate=pl.CostEstimate(
            flops=2 * rows * features * features,
            bytes_accessed=2 * features * features + 8 * rows * features,
            transcendentals=0,
        ),
    )(branch, att, weight, down, up, mid, mask, sums)


def close_kernel(
    shape, widths, dq_ref, dk_ref, dv_ref, weight_ref, down_ref, up_ref, mid_ref,
    mask_ref, x_ref, gain_ref, shift_ref, *refs,
):
    count, parts = shape
    devices = count * parts
    remote = courier_lines(dict(dp=count, seq=parts), []) is not None
    terms, refs = refs[:6], refs[6:]
    if remote:
        packs_ref, part_ref = refs[:2]
        grads, refs = refs[2:10], refs[10:]
    else:
        part_ref, out_ref = refs[:2]
        refs = refs[2:]
    total, normed_ref, grad_up, grad_down, stage = refs[:5]
    step = pl.program_id(0)
    features = x_ref.shape[1]
    if remote:
        landed, sends, arrivals = refs[5:]
        me = lax.axis_index("dp") * parts + lax.axis_index("seq")
        barrier = pltpu.get_barrier_semaphore()

        def peer(k):
            at = lax.rem(me + k, devices)
            return (at // parts, at % parts)

        def rows(at):
            return pl.ds(pl.multiple_of(at * RANK, RANK), RANK)

        def copy_to(k):
            at = lax.rem(me + k, devices)
            return pltpu.make_async_remote_copy(
                src_ref=stage.at[rows(at), :],
                dst_ref=landed.at[rows(me), :],
                send_sem=sends.at[k],
                recv_sem=arrivals.at[k],
                device_id=peer(k),
                device_id_type=pl.DeviceIdType.MESH,
            )

    @pl.when(step == 0)
    def _():
        if remote:

            def greet(k, carry):
                pl.semaphore_signal(
                    barrier, inc=1, device_id=peer(k), device_id_type=pl.DeviceIdType.MESH
                )
                return carry

            lax.fori_loop(1, devices, greet, 0)
        total[...] = jnp.zeros_like(total)
        own_t = chosen_rows(mask_ref[...], mid_ref[...])
        middle = jnp.zeros((x_ref.shape[0], LANES), f32)
        for index, source in enumerate((dq_ref, dk_ref, dv_ref)):
            at = pl.ds(index * features, features)
            middle += dot_nn(source[...], up_ref[at, :])
            grad_up[:, at] = (adapter_scale * dot_nn(own_t, source[...])).astype(bf16)
        middle = (adapter_scale * middle * mask_ref[...]).astype(bf16)
        normed, _ = normalize(x_ref[...].astype(f32))
        normed_ref[...] = normed
        act = (normed * gain_ref[...].astype(f32) + shift_ref[...].astype(f32)).astype(bf16)
        total[...] = dot_nt(middle, down_ref[...])
        grad_down[...] = dot_nn(chosen_rows(mask_ref[...], middle), act).astype(bf16)
        at = 0
        for source, width in zip((grad_down, *terms[:3], grad_up, *terms[3:]), widths):
            for device in range(devices):
                stage[device * RANK : (device + 1) * RANK, at : at + width] = source[
                    :, device * width : (device + 1) * width
                ]
            at += width
        if remote:
            pl.semaphore_wait(barrier, devices - 1)

            def send(k, carry):
                copy_to(k).start()
                return carry

            lax.fori_loop(1, devices, send, 0)
            landed[rows(me), :] = stage[rows(me), :]
        else:
            out_ref[...] = stage[...]

    for index, source in enumerate((dq_ref, dk_ref, dv_ref)):

        @pl.when(step == index)
        def _():
            total[...] += dot_nt(source[...], weight_ref[...])

    @pl.when(step == 2)
    def _():
        _, inverse = normalize(x_ref[...].astype(f32))
        scaled = total[...] * gain_ref[...].astype(f32)
        part_ref[...] = norm_back(scaled, normed_ref[...], inverse)
        if remote:
            row = lax.broadcasted_iota(jnp.int32, (devices * RANK, packs_ref.shape[0]), 0)
            column = lax.broadcasted_iota(jnp.int32, (devices * RANK, packs_ref.shape[0]), 1)
            chosen = (column == row // RANK * (packs_ref.shape[0] // devices) + VECTORS).astype(bf16)
            adapter = dot_nn(chosen, packs_ref[:, :LANES])[:, 0:1]
            row = lax.broadcasted_iota(jnp.int32, (devices * RANK, LANES), 0)
            column = lax.broadcasted_iota(jnp.int32, (devices * RANK, LANES), 1)
            same = (column // RANK).astype(f32) == adapter
            spread = jnp.where(same & (row % RANK == column % RANK), 1.0, 0.0).astype(bf16)

            def wait(k, carry):
                copy_to(k).wait()
                return carry

            lax.fori_loop(1, devices, wait, 0)
            sums = dot_tn(landed[...], spread)
            at = 0
            for target, width in zip(grads, widths):
                target[...] = sums[at : at + width, :]
                at += width


def close_call(
    mesh_shape, widths, dq, dk, dv, weight, down, up, mid, mask, x, gain, shift, terms,
    packs,
):
    rows, features = dq.shape
    devices = mesh_shape["dp"] * mesh_shape["seq"]
    remote = courier_lines(mesh_shape, []) is not None
    span = sum(widths)

    def fixed(shape):
        zeros = (0,) * len(shape)
        return pl.BlockSpec(shape, lambda j: zeros, pipeline_mode=pl.Buffered(1))

    ins = [dq, dk, dv, weight, down, up, mid, mask, x, gain, shift, *terms]
    specs = [fixed(a.shape) for a in ins]
    specs[3] = pl.BlockSpec((features, features), lambda j: (0, j))
    shapes = [jax.ShapeDtypeStruct((rows, features), f32)]
    scratch = [
        pltpu.VMEM((rows, features), f32),
        pltpu.VMEM((rows, features), f32),
        pltpu.VMEM((RANK, 3 * features), bf16),
        pltpu.VMEM((RANK, features), bf16),
        pltpu.VMEM((devices * RANK, span), bf16),
    ]
    options = {}
    if remote:
        ins.append(packs)
        specs.append(fixed(packs.shape))
        shapes += [jax.ShapeDtypeStruct((width, LANES), f32) for width in widths]
        scratch += [
            pltpu.VMEM((devices * RANK, span), bf16),
            pltpu.SemaphoreType.DMA((devices,)),
            pltpu.SemaphoreType.DMA((devices,)),
        ]
        options = dict(collective_id=4, has_side_effects=True)
    else:
        shapes.append(jax.ShapeDtypeStruct((devices * RANK, span), bf16))
    out = pl.pallas_call(
        functools.partial(close_kernel, (mesh_shape["dp"], mesh_shape["seq"]), widths),
        name="close",
        grid=(3,),
        in_specs=specs,
        out_specs=[fixed(a.shape) for a in shapes],
        scratch_shapes=scratch,
        out_shape=shapes,
        compiler_params=pltpu.CompilerParams(
            dimension_semantics=("arbitrary",), vmem_limit_bytes=56 * 1024 * 1024, **options
        ),
        cost_estimate=pl.CostEstimate(
            flops=6 * rows * features * features,
            bytes_accessed=6 * features * features + 20 * rows * features,
            transcendentals=0,
        ),
    )(*ins)
    if remote:
        return out[0], out[1:]
    received = lax.all_to_all(
        out[1].reshape(devices, RANK, span), ("dp", "seq"), 0, 0, tiled=True
    ).reshape(devices * RANK, span)
    rank = np.arange(devices * RANK)[:, None] % RANK
    column = np.arange(LANES)[None, :]
    source = packs.reshape(devices, -1, packs.shape[1])[:, VECTORS, 0].astype(jnp.int32)
    images = jnp.broadcast_to(source[:, None], (devices, RANK)).reshape(devices * RANK, 1)
    spread = ((images == column // RANK) & (rank == column % RANK)).astype(bf16)
    sums = dot_tn(received, spread)
    grads, at = [], 0
    for width in widths:
        grads.append(sums[at : at + width])
        at += width
    return out[0], grads


def position_tables(rel_h, rel_w, length):
    wide = ((0, LANES // 2 - (2 * G - 1)), (0, LANES - HEAD_DIM))
    h = jnp.pad(rel_h, wide)
    w = jnp.pad(rel_w, wide)
    h_back = jnp.pad(rel_h[::-1], wide)
    w_back = jnp.pad(rel_w[::-1], wide)
    forward = jnp.concatenate([h_back, h_back, w_back, w_back], axis=0).T
    backward = jnp.concatenate([h, h, w, w], axis=0)
    spot = np.arange(length)[:, None]
    lane = np.arange(LANES)[None, :]
    at = np.where((lane // G) % 2 == 0, spot // G, spot % G)
    spots = jnp.asarray(lane % G == at, bf16)
    turned = jnp.asarray(lane % G == G - 1 - at, bf16)
    return forward, backward, spots, turned


def vectors_kernel(devices, sizes, source, target):
    rows = source.shape[0] // devices
    target[...] = jnp.zeros_like(target)
    packs = source[...].astype(f32)
    for line, size in enumerate(sizes):
        for device in range(devices):
            at = device * rows + line
            target[line : line + 1, device * size : (device + 1) * size] = packs[
                at : at + 1, 0:size
            ]


def vectors_call(gathered, devices, sizes):
    return pl.pallas_call(
        functools.partial(vectors_kernel, devices, sizes),
        name="vectors",
        out_shape=jax.ShapeDtypeStruct((VECTORS, devices * max(sizes)), f32),
        compiler_params=params(None, 16),
    )(gathered)


def per_device(
    mesh_shape,
    tokens,
    adapter_index,
    norm1_gain,
    norm1_bias,
    qkv_weight,
    qkv_bias,
    proj_weight,
    proj_bias,
    norm2_gain,
    norm2_bias,
    fc1_weight,
    fc1_bias,
    fc2_weight,
    fc2_bias,
    rel_pos_h,
    rel_pos_w,
    qkv_down,
    qkv_up,
    proj_down,
    proj_up,
    fc1_down,
    fc1_up,
    fc2_down,
    fc2_up,
    out_grad,
):
    axes = ("dp", "seq")
    part_count = mesh_shape["seq"]
    devices = mesh_shape["dp"] * part_count
    images, part_len, features = tokens.shape
    length = part_len * part_count
    own_tokens = tokens[0]
    og = out_grad[0]
    place = lax.axis_index("seq").astype(jnp.int32).reshape(1)

    small = [
        norm1_gain, norm1_bias, qkv_bias, proj_bias, norm2_gain, norm2_bias, fc1_bias, fc2_bias,
        adapter_index.astype(bf16),
    ]
    sizes = [a.shape[0] for a in small]
    pack = jnp.concatenate([jnp.pad(a, (0, 2 * LANES - a.shape[0])) for a in small])
    pack = jnp.pad(pack.reshape(len(small), 2 * LANES), ((0, 16 - len(small)), (0, 0)))

    columns = jnp.arange(LANES, dtype=jnp.int32) // RANK
    mask = (columns[None, :] == adapter_index[:, None]).astype(f32)
    forward_table, back_table, spots, turned_spots = position_tables(rel_pos_h, rel_pos_w, length)
    head_of = np.arange(features)[None, :] // HEAD_DIM
    head_sums = jnp.asarray(head_of == np.arange(HEADS)[:, None], bf16)

    w_fc2 = lax.all_gather(fc2_weight, axes, axis=0, tiled=True)
    w_fc1 = lax.all_gather(fc1_weight, axes, axis=0, tiled=True)
    (w_qkv, d_qkv, u_qkv, all_small), image_tokens = collect(
        mesh_shape, [qkv_weight, qkv_down, qkv_up.T, pack], own_tokens
    )
    vectors = vectors_call(all_small, devices, sizes[:VECTORS])
    g1, s1, b_qkv, b_proj, g2, s2, b_fc1, b_fc2 = (
        vectors[i : i + 1, : devices * sizes[i]] for i in range(VECTORS)
    )
    (heads, mid_qkv, att, lse, aux), rest = front_call(
        mesh_shape, part_len, image_tokens, g1, s1, w_qkv, b_qkv, d_qkv, u_qkv, mask,
        forward_table, spots,
        [proj_weight, proj_down, fc1_down, fc2_down, proj_up.T, fc1_up.T, fc2_up.T],
    )
    w_proj, d_proj, d_fc1, d_fc2, u_proj, u_fc1, u_fc2 = rest
    resid, act_two, mid_proj, mid_fc1, gm_fc2, grad_act = before_call(
        att, own_tokens, og, w_proj, b_proj, d_proj, u_proj, mask, g2, s2, w_fc2, d_fc1, d_fc2,
        u_fc2,
    )
    block_out, grad_resid, grad_branch, gd_fc1, gu_fc1, gd_fc2, gu_fc2 = feed_call(
        resid, act_two, mid_fc1, gm_fc2, grad_act, og, mask, g2, w_fc1, b_fc1, w_fc2, b_fc2,
        d_fc1, u_fc1, d_fc2, u_fc2,
    )
    grad_att, inner, gd_proj, gu_proj = unproject_call(
        grad_branch, att, w_proj, d_proj, u_proj, mid_proj, mask, head_sums
    )
    if part_count == 2:
        swap = [(0, 1), (1, 0)]
        their_grad, their_lse, their_inner = (
            lax.ppermute(a, "seq", swap)[None] for a in (grad_att, lse, inner)
        )
    else:
        their_grad, their_lse, their_inner = (
            lax.all_gather(a, "seq", axis=0) for a in (grad_att, lse, inner)
        )
    dq, dk_own, dv_own = own_call(
        place, heads, aux, spots, turned_spots, back_table, grad_att, lse, inner
    )
    dk, dv = other_call(
        place, heads, aux, spots, their_grad, their_lse, their_inner, dk_own, dv_own
    )
    mid_own = lax.dynamic_slice_in_dim(mid_qkv, place[0] * part_len, part_len, 0)
    widths = [a.shape[0] for a in (qkv_down, proj_down, fc1_down, fc2_down)]
    widths += [a.shape[1] for a in (qkv_up, proj_up, fc1_up, fc2_up)]
    last_part, grads = close_call(
        mesh_shape, widths, dq, dk, dv, w_qkv, d_qkv, u_qkv, mid_own, mask, own_tokens, g1,
        s1, [gd_proj, gd_fc1, gd_fc2, gu_proj, gu_fc1, gu_fc2], all_small,
    )
    return (
        block_out[None],
        (grad_resid + last_part)[None],
        grads[0],
        grads[4].T,
        grads[1],
        grads[5].T,
        grads[2],
        grads[6].T,
        grads[3],
        grads[7].T,
    )


def solution(mesh):
    both = ("dp", "seq")
    return jax.shard_map(
        functools.partial(per_device, dict(mesh.shape)),
        mesh=mesh,
        in_specs=(
            P("dp", "seq", None),
            P("dp"),
            P(both),
            P(both),
            P(both, None),
            P(both),
            P(both, None),
            P(both),
            P(both),
            P(both),
            P(both, None),
            P(both),
            P(both, None),
            P(both),
            P(),
            P(),
            P(both, None),
            P(None, both),
            P(both, None),
            P(None, both),
            P(both, None),
            P(None, both),
            P(both, None),
            P(None, both),
            P("dp", "seq", None),
        ),
        out_specs=(
            P("dp", "seq", None),
            P("dp", "seq", None),
            P(both, None),
            P(None, both),
            P(both, None),
            P(None, both),
            P(both, None),
            P(None, both),
            P(both, None),
            P(None, both),
        ),
        check_vma=False,
    )
```

time: 460 us -> 431 us (0.937)
  local copies, waits for them, and re-layouts: 67.3 us -> 25.9 us
  Pallas kernels: 333 us -> 364 us
  waiting for transfers between devices: 26 us -> 11 us
    pallas_call x6, Pallas kernels: 133 us -> 196 us  [the longest x1 90.3 us: front_call(): pl.pallas_call(functools.partial(front_kernel, lines, chunks, [a.shape[0]...]
    pallas_call x1, Pallas kernels: 141 us -> 109 us  [collect(): pl.pallas_call(functools.partial(collect_kernel, lines, chunks, [a.shape[...]
    reshape x26 -> x1, local copies, waits for them, and re-layouts: 15 us -> 0.01 us  [per_device(): pack.reshape(len(small), 2 * LANES)]
    all_to_all x1 -> x0, waiting for transfers between devices: 14.6 us -> none  [per_device(): received = lax.all_to_all(sent, axes, 0, 0, tiled=True)]
    unnamed x88 -> x74, local copies, waits for them, and re-layouts: 30.5 us -> 16.3 us
    concatenate x3 -> x1, local copies, waits for them, and re-layouts: 8.35 us -> 0.01 us  [per_device(): jnp.concatenate([jnp.pad(a, (0, 2 * LANES - a.shape[0])) for a in small])]
    slice x8 -> x3, local copies, waits for them, and re-layouts: 10 us -> 1.86 us  [per_device(): vectors[i:i + 1, :devices * sizes[i]]]
    pad x0 -> x9, local copies, waits for them, and re-layouts: none -> 5.89 us  [the longest x8 5.28 us: per_device(): jnp.pad(a, (0, 2 * LANES - a.shape[0]))]
  transfers between devices with their start and end apart: 6 -> 5, of which waited for: 2 -> 1; matrix products, arithmetic and copies ran while one was open for 10% -> 3% of each run, Pallas kernels for 66% -> 74%
where the time goes in v2:
time: 431 us; the launch traced here: 425 us
  Pallas kernels  364 us (84%)
  local copies, waits for them, and re-layouts  25.9 us (6%)
  between operations  15.3 us (4%)
  waiting for transfers between devices  11 us (3%)
  other arithmetic  4.96 us (1%)
    pallas_call x1, Pallas kernels, collect(): pl.pallas_call(functools.partial(collect_kernel, lines, chunks, [a.shape[...  109 us
    pallas_call x1, Pallas kernels, front_call(): pl.pallas_call(functools.partial(front_kernel, lines, chunks, [a.shape[0]...  90.3 us
    pallas_call x1, Pallas kernels, feed_call(): pl.pallas_call(feed_kernel, name='feed', grid=(wide // block,), in_specs=...  47.3 us
    pallas_call x1, Pallas kernels, own_call(): pl.pallas_call(own_kernel, name='back_own', grid_spec=pltpu.PrefetchScala...  37.7 us
    pallas_call x1, Pallas kernels, close_call(): pl.pallas_call(functools.partial(close_kernel, (mesh_shape['dp'], mesh_sh...  29.2 us
    pallas_call x1, Pallas kernels, other_call(): pl.pallas_call(other_kernel, name='back_other', grid_spec=pltpu.PrefetchS...  20.9 us
    pallas_call x1, Pallas kernels, before_call(): pl.pallas_call(before_kernel, name='before', grid=(wide // block,), in_sp...  20.1 us
    unnamed x74, local copies, waits for them, and re-layouts  16.3 us
  transfers between devices with their start and end apart: 5, of which 1 were waited for; matrix products, arithmetic and copies ran while one was open for 3% of the time, Pallas kernels for 74%

profile of v2, /device:TPU:15, one launch (start us, length us, event | category | flops | bytes accessed | tf_op | source)
XLA Modules:
  0.0 425.2 jit_solution(15027828411065334299)
XLA Ops:
  7.2 0.7 all-gather.3.cloned.1.call-update
  8.0 0.7 all-gather.5.cloned.1.call-update
  9.3 0.7 pad.48
  10.0 0.7 pad.49
  10.6 0.7 pad.50
  11.3 0.7 pad.51
  12.0 0.7 pad.52
  12.6 0.7 pad.53
  13.3 0.7 pad.54
  13.9 0.7 pad.55
  16.9 0.8 copy.38
  17.8 0.8 copy.39
  18.7 109.4 %collect.1 = (bf16[1280,3840]{1,0:T(8,128)(2,1)}, bf16[1280,128]{1,0:T(8,128)(2,1)}, bf16[3840,128]{1,0:T(8,128)(2,1)}, bf16[512,256]{1,0:T(8,128)(2,1)}, bf16[512,1280]{1,0:T(8,128)(2,1)}) custom-call(bf16[40,3840]{1,0:T(8,128)(2,1)} %refs_0_.1, bf16[40,128]{1,0:T(8,128)(2,1)} %refs_1_.1, bf16[120,128]{1,0:T(8,128)(2,1)} %bitcast.30, ...), custom_call_target="tpu_custom_call" | custom-call | tf_op jit(solution)/shard_map/collect/pallas_call | solution.py:297
  128.2 0.9 copy-done.6
  130.5 0.7 maximum_bitcast_fusion.table_ref
  131.9 90.3 %front.1 = (bf16[3,16,1024,128]{3,2,1,0:T(8,128)(2,1)}, bf16[1024,128]{1,0:T(8,128)(2,1)}, bf16[512,1280]{1,0:T(8,128)(2,1)}, f32[16,1,512]{2,1,0:T(1,128)}, bf1...) custom-call(f32[1,1280]{1,0:T(1,128)} %get-tuple-element.111.gain_re, ...), custom_call_target="tpu_custom_call" | custom-call | flops 18656264192 | bytes 30801920 | tf_op jit(solution)/shard_map/front/pallas_call | solution.py:475
  222.2 2.8 collective-permute-start.1
  225.6 1.6 constant_dynamic-slice_fusion.mid_ref
  227.2 20.1 %before.1 = (f32[512,1280]{1,0:T(8,128)}, bf16[512,1280]{1,0:T(8,128)(2,1)}, bf16[512,128]{1,0:T(8,128)(2,1)}, bf16[512,128]{1,0:T(8,128)(2,1)}, bf16[512,128]{1,0:T(8,128)(2,1)}, /*index=5*/f32[512,5120]{1,0:T(8,128)}) custom-call(bf16[512,1280]{1,0:T(8,128)(2,1)} %get-tuple-element.63.att_ref, bf16[512,1280]{1,0:T(8,128)(2,1)} %bitcast.26, ...), custom_call_target="tpu_custom_call" | custom-call | flops 8388608000 | bytes 34078720 | tf_op jit(solution)/shard_map/before/pallas_call | solution.py:783
  247.3 9.6 %all-gather.5.cloned.1.call-done.w1_ref = bf16[1280,5120]{1,0:T(8,128)(2,1)} async-done(((bf16[40,5120]{1,0:T(8,128)(2,1)}), bf16[1280,5120]{1,0:T(8,128)(2,1)}) %all-gather.5.cloned.1.call-update) | async-done | bytes 13107216 | tf_op jit(solution)/shard_map/all_gather | solution.py:1235
  256.9 47.3 %feed.1 = (bf16[512,1280]{1,0:T(8,128)(2,1)}, f32[512,1280]{1,0:T(8,128)}, bf16[512,1280]{1,0:T(8,128)(2,1)}, bf16[16,1280]{1,0:T(8,128)(2,1)}, bf16[16,5120]{1,...) custom-call(f32[512,1280]{1,0:T(8,128)} %get-tuple-element.70.resid_ref, ...), custom_call_target="tpu_custom_call" | custom-call | flops 20132659200 | bytes 52428800 | tf_op jit(solution)/shard_map/feed/pallas_call | solution.py:878
  304.3 1.3 copy-done.2
  305.6 8.6 %unproject.1 = (bf16[512,1280]{1,0:T(8,128)(2,1)S(1)}, f32[16,1,512]{2,1,0:T(1,128)S(1)}, bf16[16,1280]{1,0:T(8,128)(2,1)S(1)}, bf16[16,1280]{1,0:T(8,128)(2,1)S(1)}) custom-call(bf16[512,1280]{1,0:T(8,128)(2,1)S(1)} %copy-done.2, bf16[512,1280]{1,0:T(8,128)(2,1)} %get-tuple-element.63.att_ref, bf16[1280,1280]{1,0:T(8,128)(2,1)} %get-tuple-element.64.wp_ref.weight_ref, ...), custom_call_target="tpu_custom_call" | custom-call | flops 1677721600 | bytes 8519680 | tf_op jit(solution)/shard_map/unproject/pallas_call | solution.py:940
  314.8 1.2 collective-permute-start.2
  316.3 37.7 %back_own.1 = (bf16[512,1280]{1,0:T(8,128)(2,1)S(1)}, f32[16,512,128]{2,1,0:T(8,128)S(1)}, f32[16,512,128]{2,1,0:T(8,128)S(1)}) custom-call(s32[1]{0:T(128)} %bitcast.9.place_ref, bf16[3,16,1024,128]{3,2,1,0:T(8,128)(2,1)} %get-tuple-element.78.q_ref.k_ref.v_ref, bf16[16,1024,128]{2,1,0:T(8,128)(2,1)} %get-tuple-element.79.aux_ref, ...), custom_call_target="tpu_custom_call" | custom-call | flops 17179869184 | bytes 25165824 | tf_op jit(solution)/shard_map/back_own/pallas_call | solution.py:591
  354.1 2.0 copy-done.1
  356.0 1.1 copy-done.16
  357.1 20.9 %back_other.1 = (bf16[512,1280]{1,0:T(8,128)(2,1)S(1)}, bf16[512,1280]{1,0:T(8,128)(2,1)S(1)}) custom-call(s32[1]{0:T(128)} %bitcast.9.place_ref, bf16[3,16,1024,128]{3,2,1,0:T(8,128)(2,1)} %get-tuple-element.78.q_ref.k_ref.v_ref, bf16[16,1024,128]{2,1,0:T(8,128)(2,1)S(1)} %copy-done, bf16[3,16,1024,128]{3,2,1,0:T(8,128)(2,1)} %get-tuple-element.78.q_ref.k_ref.v_ref, ...), custom_call_target="tpu_custom_call" | custom-call | flops 4294967296 | bytes 25165824 | tf_op jit(solution)/shard_map/back_other/pallas_call | solution.py:685
  378.0 1.1 copy-done.10
  379.1 1.1 copy-done.11
  380.2 29.2 %close.1 = (f32[512,1280]{1,0:T(8,128)}, f32[40,128]{1,0:T(8,128)}, f32[40,128]{1,0:T(8,128)}, f32[40,128]{1,0:T(8,128)}, f32[160,128]{1,0:T(8,128)}, /*index=5*...) custom-call(bf16[512,1280]{1,0:T(8,128)(2,1)} %copy-done.16, ...), custom_call_target="tpu_custom_call" | custom-call | flops 5033164800 | bytes 22937600 | tf_op jit(solution)/shard_map/close/pallas_call | solution.py:1111
  409.5 3.6 add_bitcast_fusion
  (89 shorter events, 11.2 us)
Async XLA Ops:
  7.2 220.0 %all-gather.3.cloned.1.call-start = ((), (), s32[]{:S(2)}) async-start(), calls=%async_computation | async-start | bytes 13516800 | tf_op jit(solution)/shard_map/all_gather | solution.py:1234
  7.9 249.0 %all-gather.5.cloned.1.call-start = ((), (), s32[]{:S(2)}) async-start(), calls=%async_computation.1 | async-start | bytes 13516800 | tf_op jit(solution)/shard_map/all_gather | solution.py:1235
  128.1 1.0 copy-start.6
  131.9 93.1 %copy-start.20 = (bf16[63,80]{1,0:T(8,128)(2,1)S(1)}, bf16[63,80]{1,0:T(8,128)(2,1)}, u32[]{:S(2)}) copy-start(bf16[63,80]{1,0:T(8,128)(2,1)} %param.42) | copy-start | bytes 30244
  131.9 93.1 %copy-start.21 = (bf16[63,80]{1,0:T(8,128)(2,1)S(1)}, bf16[63,80]{1,0:T(8,128)(2,1)}, u32[]{:S(2)}) copy-start(bf16[63,80]{1,0:T(8,128)(2,1)} %param.43) | copy-start | bytes 30244
  222.2 134.9 %collective-permute-start.1 = (f32[16,1,512]{2,1,0:T(1,128)}, f32[16,1,512]{2,1,0:T(1,128)S(1)}, u32[]{:S(2)}, u32[]{:S(2)}) collective-permute-start(f32[16,1,512]{2,1,0:T(1,128)} %get-tuple-element.83.lse_ref), channel_id=1, source_target_pairs={{0,1},{1,0},{2,3},{3,2},{4,5},{5,4},{6,7},{7,6},{8,9},{9,8},{10,11... | collective-permute-start | bytes 98312 | tf_op jit(solution)/shard_map/ppermute | solution.py:1263
  256.9 47.4 %copy-start.3 = (bf16[1280,128]{1,0:T(8,128)(2,1)S(1)}, bf16[1280,128]{1,0:T(8,128)(2,1)}, u32[]{:S(2)}) copy-start(bf16[1280,128]{1,0:T(8,128)(2,1)} %get-tuple-element.65.dp_ref.down_ref) | copy-start | bytes 983044
  256.9 47.4 %copy-start.4 = (bf16[1280,128]{1,0:T(8,128)(2,1)S(1)}, bf16[1280,128]{1,0:T(8,128)(2,1)}, u32[]{:S(2)}) copy-start(bf16[1280,128]{1,0:T(8,128)(2,1)} %get-tuple-element.66.up_ref) | copy-start | bytes 983044
  256.9 47.4 %copy-start.7 = (bf16[512,128]{1,0:T(8,128)(2,1)S(1)}, bf16[512,128]{1,0:T(8,128)(2,1)}, u32[]{:S(2)}) copy-start(bf16[512,128]{1,0:T(8,128)(2,1)} %get-tuple-element.81.mid_ref) | copy-start | bytes 393220
  256.9 47.4 %copy-start.8 = (bf16[16,1280]{1,0:T(8,128)(2,1)S(1)}, bf16[16,1280]{1,0:T(8,128)(2,1)}, u32[]{:S(2)}) copy-start(bf16[16,1280]{1,0:T(8,128)(2,1)} %constant.37.clone.sums_ref) | copy-start | bytes 122884
  256.9 47.4 %copy-start.9 = (f32[1,128]{1,0:T(1,128)S(1)}, f32[1,128]{1,0:T(1,128)}, u32[]{:S(2)}) copy-start(f32[1,128]{1,0:T(1,128)} %compare_convert_fusion.mask_ref) | copy-start | bytes 1540
  304.3 1.3 copy-start.2
  305.6 10.7 %copy-start.5 = (bf16[1024,128]{1,0:T(8,128)(2,1)S(1)}, bf16[1024,128]{1,0:T(8,128)(2,1)}, u32[]{:S(2)}) copy-start(bf16[1024,128]{1,0:T(8,128)(2,1)} %constant.35.clone.spots_ref) | copy-start | bytes 786436
  305.6 10.7 %copy-start.14 = (f32[16,1,512]{2,1,0:T(1,128)S(1)}, f32[16,1,512]{2,1,0:T(1,128)}, u32[]{:S(2)}) copy-start(f32[16,1,512]{2,1,0:T(1,128)} %get-tuple-element.83.lse_ref) | copy-start | bytes 98308
  305.6 10.7 %copy-start.15 = (bf16[1024,128]{1,0:T(8,128)(2,1)S(1)}, bf16[1024,128]{1,0:T(8,128)(2,1)}, u32[]{:S(2)}) copy-start(bf16[1024,128]{1,0:T(8,128)(2,1)} %constant.36.clone.turned_spots_ref) | copy-start | bytes 786436
  314.8 39.2 %copy-start.13 = (bf16[16,1280]{1,0:T(8,128)(2,1)}, bf16[16,1280]{1,0:T(8,128)(2,1)S(1)}, u32[]{:S(2)}) copy-start(bf16[16,1280]{1,0:T(8,128)(2,1)S(1)} %get-tuple-element.94.refs_3_) | copy-start | bytes 122884
  314.8 42.3 %collective-permute-start.2 = (f32[16,1,512]{2,1,0:T(1,128)S(1)}, f32[16,1,512]{2,1,0:T(1,128)S(1)}, u32[]{:S(2)}, u32[]{:S(2)}) collective-permute-start(f32[16,1,512]{2,1,0:T(1,128)S(1)} %get-tuple-element.84.inner_ref), channel_id=1, source_target_pairs={{0,1},{1,0},{2,3},{3,2},{4,5},{5,4},{6,7},{7,6},{8,9},{9,8},{10,11... | collective-permute-start | bytes 98312 | tf_op jit(solution)/shard_map/ppermute | solution.py:1263
  316.0 41.1 %collective-permute-start = (bf16[512,1280]{1,0:T(8,128)(2,1)S(1)}, bf16[512,1280]{1,0:T(8,128)(2,1)S(1)}, u32[]{:S(2)}, u32[]{:S(2)}) collective-permute-start(bf16[512,1280]{1,0:T(8,128)(2,1)S(1)} %get-tuple-element.82.grad_ref), channel_id=1, source_target_pairs={{0,1},{1,0},{2,3},{3,2},{4,5},{5,4},{6,7},{7,6},{8,9},{9,8},{10,11... | collective-permute-start | bytes 3932168 | tf_op jit(solution)/shard_map/ppermute | solution.py:1263
  316.3 40.8 %copy-start = (bf16[16,1024,128]{2,1,0:T(8,128)(2,1)S(1)}, bf16[16,1024,128]{2,1,0:T(8,128)(2,1)}, u32[]{:S(2)}) copy-start(bf16[16,1024,128]{2,1,0:T(8,128)(2,1)} %get-tuple-element.79.aux_ref) | copy-start | bytes 12582916
  354.1 2.0 copy-start.1
  356.0 1.1 copy-start.16
  378.0 1.1 copy-start.10
  379.1 1.1 copy-start.11
  380.2 29.2 %copy-start.17 = (f32[512,1280]{1,0:T(8,128)S(1)}, f32[512,1280]{1,0:T(8,128)}, u32[]{:S(2)}) copy-start(f32[512,1280]{1,0:T(8,128)} %get-tuple-element.77) | copy-start | bytes 7864324
  409.4 3.7 copy-start.27
  409.4 4.3 %copy-start.22 = (f32[120,128]{1,0:T(8,128)S(1)}, f32[120,128]{1,0:T(8,128)}, u32[]{:S(2)}) copy-start(f32[120,128]{1,0:T(8,128)} %get-tuple-element.99) | copy-start | bytes 184324
  409.4 4.9 %copy-start.26 = (f32[40,128]{1,0:T(8,128)S(1)}, f32[40,128]{1,0:T(8,128)}, u32[]{:S(2)}) copy-start(f32[40,128]{1,0:T(8,128)} %get-tuple-element.126) | copy-start | bytes 61444
  409.4 5.5 %copy-start.25 = (f32[40,128]{1,0:T(8,128)S(1)}, f32[40,128]{1,0:T(8,128)}, u32[]{:S(2)}) copy-start(f32[40,128]{1,0:T(8,128)} %get-tuple-element.101) | copy-start | bytes 61444
  409.4 6.1 %copy-start.24 = (f32[40,128]{1,0:T(8,128)S(1)}, f32[40,128]{1,0:T(8,128)}, u32[]{:S(2)}) copy-start(f32[40,128]{1,0:T(8,128)} %get-tuple-element.128) | copy-start | bytes 61444
  409.4 6.7 %copy-start.19 = (f32[160,128]{1,0:T(8,128)S(1)}, f32[160,128]{1,0:T(8,128)}, u32[]{:S(2)}) copy-start(f32[160,128]{1,0:T(8,128)} %get-tuple-element.103) | copy-start | bytes 245764
  409.5 7.3 %copy-start.18 = (f32[160,128]{1,0:T(8,128)S(1)}, f32[160,128]{1,0:T(8,128)}, u32[]{:S(2)}) copy-start(f32[160,128]{1,0:T(8,128)} %get-tuple-element.130) | copy-start | bytes 245764
  409.5 8.0 %copy-start.23 = (f32[40,128]{1,0:T(8,128)S(1)}, f32[40,128]{1,0:T(8,128)}, u32[]{:S(2)}) copy-start(f32[40,128]{1,0:T(8,128)} %get-tuple-element.105) | copy-start | bytes 61444
  (1 other events, 0.6 us)
Sparse Core Ops, SparseCore 0:
  10.9 136.5 all-gather.2
  150.3 106.5 all-gather.4

commit v3 on v2

--- a/solution.py
+++ b/solution.py
@@ -526,59 +526,44 @@
     return out[:5], list(out[5:]) + later
 
 
-def head_lanes(source, head, padded):
-    padded[:, HEAD_DIM:LANES] = jnp.zeros((padded.shape[0], LANES - HEAD_DIM), bf16)
-    for slot in range(HALF):
-
-        @pl.when(head % HALF == slot)
-        def _():
-            padded[:, 0:HEAD_DIM] = source[:, slot * HEAD_DIM : (slot + 1) * HEAD_DIM]
-
-
 def own_kernel(
     place_ref, q_ref, aux_ref, k_ref, v_ref, spots_ref, turned_spots_ref, table_ref, grad_ref,
     lse_ref, inner_ref, dq_ref, dk_ref, dv_ref, shares_ref, dscores_ref, padded,
 ):
-    head = pl.program_id(0)
     part_len = q_ref.shape[2]
-    head_lanes(grad_ref, head, padded)
-    queries = q_ref[0, 0]
-    keys = k_ref[0, 0]
-    left = jnp.concatenate([keys, spots_ref[...]], axis=1)
-    right = jnp.concatenate([queries, aux_ref[0]], axis=1)
-    shares = jnp.exp2(dot_nt(left, right) * exponent_scale - lse_ref[0])
-    grad_shares = dot_nt(v_ref[0, 0], padded[...])
-    shares_ref[...] = shares.astype(bf16)
-    dscores_ref[...] = (shares * (grad_shares - inner_ref[0])).astype(bf16)
-    flat = dot_tn(jnp.concatenate([keys, turned_spots_ref[...]], axis=1), dscores_ref[...])
-    turned = jnp.transpose(flat)
     lane = lax.broadcasted_iota(jnp.int32, (G, LANES), 1)
-    first = lane < LANES // 2
-    even = (lane // G) % 2 == 0
     start = place_ref[0] * (part_len // G)
-    pieces_h, pieces_w = [], []
-    for row in range(part_len // G):
-        sums = turned[row * G : (row + 1) * G, LANES:]
-        high = sums.astype(bf16).astype(f32)
-        mixed = jnp.where(first, high, sums - high)
-        pieces_h.append(pltpu.roll(jnp.where(even, mixed, 0.0), start + row, 1))
-        pieces_w.append(
-            pltpu.roll(jnp.where(even, 0.0, mixed), LANES - G, 1, stride=1, stride_axis=0)
+    here = pl.ds(pl.multiple_of(place_ref[0] * part_len, G), part_len)
+    for slot in range(HALF):
+        cols = slice(slot * HEAD_DIM, (slot + 1) * HEAD_DIM)
+        spare = slot % 2
+        padded[spare, :, HEAD_DIM:LANES] = jnp.zeros((part_len, LANES - HEAD_DIM), bf16)
+        padded[spare, :, 0:HEAD_DIM] = grad_ref[:, cols]
+        queries = q_ref[0, slot]
+        keys = k_ref[0, slot]
+        left = jnp.concatenate([keys, spots_ref[...]], axis=1)
+        right = jnp.concatenate([queries, aux_ref[slot]], axis=1)
+        shares = jnp.exp2(dot_nt(left, right) * exponent_scale - lse_ref[slot])
+        grad_shares = dot_nt(v_ref[0, slot], padded[spare])
+        shares_ref[spare] = shares.astype(bf16)
+        dscores_ref[spare] = (shares * (grad_shares - inner_ref[slot])).astype(bf16)
+        flat = dot_tn(
+            jnp.concatenate([keys, turned_spots_ref[...]], axis=1), dscores_ref[spare]
         )
-    spread = jnp.concatenate(
-        [jnp.concatenate(pieces_h, axis=0), jnp.concatenate(pieces_w, axis=0)], axis=1
-    ).astype(bf16)
-    grad_query = turned[:, :LANES] * score_scale + dot_nn(spread, table_ref[...])
-    grad_query = grad_query[:, :HEAD_DIM].astype(bf16)
-    for slot in range(HALF):
-
-        @pl.when(head % HALF == slot)
-        def _():
-            dq_ref[:, slot * HEAD_DIM : (slot + 1) * HEAD_DIM] = grad_query
-
-    here = pl.ds(pl.multiple_of(place_ref[0] * part_len, G), part_len)
-    dk_ref[0] = dot_nn(dscores_ref[here, :], queries)
-    dv_ref[0] = dot_nn(shares_ref[here, :], padded[...])
+        turned = jnp.transpose(flat)
+        spread = []
+        for row in range(part_len // G):
+            sums = turned[row * G : (row + 1) * G, LANES:]
+            along_h = pltpu.roll(jnp.where(lane < G, sums, 0.0), start + row, 1)
+            along_w = pltpu.roll(
+                jnp.where((lane >= G) & (lane < 2 * G), sums, 0.0), G, 1, stride=1, stride_axis=0
+            )
+            spread.append((along_h + along_w).astype(bf16))
+        spread = jnp.concatenate(spread, axis=0)
+        grad_query = turned[:, :LANES] * score_scale + dot_nn(spread, table_ref[...])
+        dq_ref[:, cols] = grad_query[:, :HEAD_DIM].astype(bf16)
+        dk_ref[slot] = dot_nn(dscores_ref[spare, here, :], queries)
+        dv_ref[slot] = dot_nn(shares_ref[spare, here, :], padded[spare])
 
 
 def own_call(place, heads, aux, spots, turned_spots, table, grad, lse, inner):
@@ -586,35 +571,35 @@
     part_len, features = grad.shape
 
     def part(index):
-        return pl.BlockSpec((1, 1, length, LANES), lambda n, s: (index, n, 0, 0))
+        return pl.BlockSpec((1, HALF, length, LANES), lambda n, s: (index, n, 0, 0))
 
     return pl.pallas_call(
         own_kernel,
         name="back_own",
         grid_spec=pltpu.PrefetchScalarGridSpec(
             num_scalar_prefetch=1,
-            grid=(HEADS,),
+            grid=(HEADS // HALF,),
             in_specs=[
-                pl.BlockSpec((1, 1, part_len, LANES), lambda n, s: (0, n, s[0], 0)),
-                pl.BlockSpec((1, part_len, LANES), lambda n, s: (n, s[0], 0)),
+                pl.BlockSpec((1, HALF, part_len, LANES), lambda n, s: (0, n, s[0], 0)),
+                pl.BlockSpec((HALF, part_len, LANES), lambda n, s: (n, s[0], 0)),
                 part(1),
                 part(2),
                 whole((length, LANES)),
                 whole((length, LANES)),
-                whole((2 * LANES, LANES)),
-                pl.BlockSpec((part_len, features // 2), lambda n, s: (0, n // HALF)),
-                pl.BlockSpec((1, 1, part_len), lambda n, s: (n, 0, 0)),
-                pl.BlockSpec((1, 1, part_len), lambda n, s: (n, 0, 0)),
+                whole((LANES, LANES)),
+                pl.BlockSpec((part_len, features // 2), lambda n, s: (0, n)),
+                pl.BlockSpec((HALF, 1, part_len), lambda n, s: (n, 0, 0)),
+                pl.BlockSpec((HALF, 1, part_len), lambda n, s: (n, 0, 0)),
             ],
             out_specs=[
-                pl.BlockSpec((part_len, features // 2), lambda n, s: (0, n // HALF)),
-                pl.BlockSpec((1, part_len, LANES), lambda n, s: (n, 0, 0)),
-                pl.BlockSpec((1, part_len, LANES), lambda n, s: (n, 0, 0)),
+                pl.BlockSpec((part_len, features // 2), lambda n, s: (0, n)),
+                pl.BlockSpec((HALF, part_len, LANES), lambda n, s: (n, 0, 0)),
+                pl.BlockSpec((HALF, part_len, LANES), lambda n, s: (n, 0, 0)),
             ],
             scratch_shapes=[
-                pltpu.VMEM((length, part_len), bf16),
-                pltpu.VMEM((length, part_len), bf16),
-                pltpu.VMEM((part_len, LANES), bf16),
+                pltpu.VMEM((2, length, part_len), bf16),
+                pltpu.VMEM((2, length, part_len), bf16),
+                pltpu.VMEM((2, part_len, LANES), bf16),
             ],
         ),
         out_shape=[
@@ -622,7 +607,7 @@
             jax.ShapeDtypeStruct((HEADS, part_len, LANES), f32),
             jax.ShapeDtypeStruct((HEADS, part_len, LANES), f32),
         ],
-        compiler_params=params(("arbitrary",), 40),
+        compiler_params=params(("arbitrary",), 60),
         cost_estimate=pl.CostEstimate(
             flops=8 * HEADS * part_len * length * LANES * 2,
             bytes_accessed=12 * HEADS * length * LANES,
@@ -632,37 +617,49 @@
 
 
 def other_kernel(
-    place_ref, q_ref, aux_ref, k_ref, v_ref, spots_ref, grad_ref, lse_ref, inner_ref, dk_in, dv_in,
-    dk_ref, dv_ref, dk_sum, dv_sum, padded,
+    steps, place_ref, q_ref, aux_ref, k_ref, v_ref, spots_ref, grad_ref, lse_ref, inner_ref,
+    dk_in, dv_in, dk_ref, dv_ref, padded, *sums,
 ):
-    head = pl.program_id(0)
     step = pl.program_id(1)
-    head_lanes(grad_ref.at[0], head, padded)
-    queries = q_ref[0, 0]
-    left = jnp.concatenate([k_ref[0, 0], spots_ref[...]], axis=1)
-    right = jnp.concatenate([queries, aux_ref[0]], axis=1)
-    shares = jnp.exp2(dot_nt(left, right) * exponent_scale - lse_ref[0, 0])
-    grad_shares = dot_nt(v_ref[0, 0], padded[...])
-    dscores = (shares * (grad_shares - inner_ref[0, 0])).astype(bf16)
-
-    @pl.when(step == 0)
-    def _():
-        dk_sum[...] = dk_in[0]
-        dv_sum[...] = dv_in[0]
-
-    dk_sum[...] += dot_nn(dscores, queries)
-    dv_sum[...] += dot_nn(shares.astype(bf16), padded[...])
-
-    @pl.when(step == pl.num_programs(1) - 1)
-    def _():
-        grad_key = (dk_sum[:, :HEAD_DIM] * score_scale).astype(bf16)
-        grad_value = dv_sum[:, :HEAD_DIM].astype(bf16)
-        for slot in range(HALF):
-
-            @pl.when(head % HALF == slot)
-            def _():
-                dk_ref[:, slot * HEAD_DIM : (slot + 1) * HEAD_DIM] = grad_key
-                dv_ref[:, slot * HEAD_DIM : (slot + 1) * HEAD_DIM] = grad_value
+    part_len = q_ref.shape[2]
+    if sums:
+        dk_sum, dv_sum = sums
+
+        @pl.when(step == 0)
+        def _():
+            dk_sum[...] = dk_in[...]
+            dv_sum[...] = dv_in[...]
+
+    for slot in range(HALF):
+        cols = slice(slot * HEAD_DIM, (slot + 1) * HEAD_DIM)
+        spare = slot % 2
+        padded[spare, :, HEAD_DIM:LANES] = jnp.zeros((part_len, LANES - HEAD_DIM), bf16)
+        padded[spare, :, 0:HEAD_DIM] = grad_ref[0, :, cols]
+        queries = q_ref[0, slot]
+        left = jnp.concatenate([k_ref[0, slot], spots_ref[...]], axis=1)
+        right = jnp.concatenate([queries, aux_ref[slot]], axis=1)
+        shares = jnp.exp2(dot_nt(left, right) * exponent_scale - lse_ref[0, slot])
+        grad_shares = dot_nt(v_ref[0, slot], padded[spare])
+        dscores = (shares * (grad_shares - inner_ref[0, slot])).astype(bf16)
+        grad_key = dot_nn(dscores, queries)
+        grad_value = dot_nn(shares.astype(bf16), padded[spare])
+        if sums:
+            dk_sum[slot] += grad_key
+            dv_sum[slot] += grad_value
+        else:
+            grad_key = (grad_key + dk_in[slot])[:, :HEAD_DIM] * score_scale
+            grad_value = (grad_value + dv_in[slot])[:, :HEAD_DIM]
+            dk_ref[:, cols] = grad_key.astype(bf16)
+            dv_ref[:, cols] = grad_value.astype(bf16)
+
+    if sums:
+
+        @pl.when(step == steps - 1)
+        def _():
+            for slot in range(HALF):
+                cols = slice(slot * HEAD_DIM, (slot + 1) * HEAD_DIM)
+                dk_ref[:, cols] = (dk_sum[slot, :, :HEAD_DIM] * score_scale).astype(bf16)
+                dv_ref[:, cols] = dv_sum[slot, :, :HEAD_DIM].astype(bf16)
 
 
 def other_call(place, heads, aux, spots, grads, lses, inners, dk, dv):
@@ -677,25 +674,25 @@
         return theirs(i, s) if blocks > 1 else 0
 
     def own(index):
-        return pl.BlockSpec((1, 1, part_len, LANES), lambda n, i, s: (index, n, s[0], 0))
-
-    stats = pl.BlockSpec((1, 1, 1, part_len), lambda n, i, s: (given(i, s), n, 0, 0))
-    sums = pl.BlockSpec((1, part_len, LANES), lambda n, i, s: (n, 0, 0))
-    dense = pl.BlockSpec((part_len, features // 2), lambda n, i, s: (0, n // HALF))
+        return pl.BlockSpec((1, HALF, part_len, LANES), lambda n, i, s: (index, n, s[0], 0))
+
+    stats = pl.BlockSpec((1, HALF, 1, part_len), lambda n, i, s: (given(i, s), n, 0, 0))
+    sums = pl.BlockSpec((HALF, part_len, LANES), lambda n, i, s: (n, 0, 0))
+    dense = pl.BlockSpec((part_len, features // 2), lambda n, i, s: (0, n))
     return pl.pallas_call(
-        other_kernel,
+        functools.partial(other_kernel, count - 1),
         name="back_other",
         grid_spec=pltpu.PrefetchScalarGridSpec(
             num_scalar_prefetch=1,
-            grid=(HEADS, count - 1),
+            grid=(HEADS // HALF, count - 1),
             in_specs=[
-                pl.BlockSpec((1, 1, part_len, LANES), lambda n, i, s: (0, n, theirs(i, s), 0)),
-                pl.BlockSpec((1, part_len, LANES), lambda n, i, s: (n, theirs(i, s), 0)),
+                pl.BlockSpec((1, HALF, part_len, LANES), lambda n, i, s: (0, n, theirs(i, s), 0)),
+                pl.BlockSpec((HALF, part_len, LANES), lambda n, i, s: (n, theirs(i, s), 0)),
                 own(1),
                 own(2),
                 pl.BlockSpec((part_len, LANES), lambda n, i, s: (s[0], 0)),
                 pl.BlockSpec(
-                    (1, part_len, features // 2), lambda n, i, s: (given(i, s), 0, n // HALF)
+                    (1, part_len, features // 2), lambda n, i, s: (given(i, s), 0, n)
                 ),
                 stats,
                 stats,
@@ -703,17 +700,14 @@
                 sums,
             ],
             out_specs=[dense, dense],
-            scratch_shapes=[
-                pltpu.VMEM((part_len, LANES), f32),
-                pltpu.VMEM((part_len, LANES), f32),
-                pltpu.VMEM((part_len, LANES), bf16),
-            ],
+            scratch_shapes=[pltpu.VMEM((2, part_len, LANES), bf16)]
+            + [pltpu.VMEM((HALF, part_len, LANES), f32)] * (2 if count > 2 else 0),
         ),
         out_shape=[
             jax.ShapeDtypeStruct((part_len, features), bf16),
             jax.ShapeDtypeStruct((part_len, features), bf16),
         ],
-        compiler_params=params(("arbitrary", "arbitrary"), 40),
+        compiler_params=params(("arbitrary", "arbitrary"), 60),
         cost_estimate=pl.CostEstimate(
             flops=4 * HEADS * part_len * (length - part_len) * LANES * 2,
             bytes_accessed=12 * HEADS * length * LANES,
@@ -798,17 +792,31 @@
 
 
 def feed_kernel(
-    resid_ref, act_ref, mid1_ref, gm2_ref, grad_act_ref, og_ref, mask_ref, gain_ref,
+    act_ref, mid1_ref, gm2_ref, grad_act_ref, mask_ref, gain_ref,
     w1_ref, b1_ref, w2_ref, b2_ref, down1_ref, up1_ref, down2_ref, up2_ref,
-    out_ref, grad_ref, branch_ref, gd1_ref, gu1_ref, gd2_ref, gu2_ref,
-    total, back, mid2_sum, gm1_sum, gm2_t, mid1_t,
+    dp_ref, up_ref, midp_ref, sums_ref, *refs,
 ):
+    late = refs[:4]
+    (out_ref, grad_ref, grad_att_ref, inner_ref, gd1_ref, gu1_ref, gd2_ref, gu2_ref, gdp_ref,
+     gup_ref) = refs[4:14]
+    total, back, mid2_sum, gm1_sum, gm2_t, mid1_t, late_sem = refs[14:21]
+    held = refs[21:]
+    resid_ref, og_ref, att_ref, wp_ref = held
+
     step = pl.program_id(0)
     steps = pl.num_programs(0)
     mask = mask_ref[...]
 
+    def copies():
+        return [
+            pltpu.make_async_copy(source, target, late_sem.at[index])
+            for index, (source, target) in enumerate(zip(late, held))
+        ]
+
     @pl.when(step == 0)
     def _():
+        for copy in copies():
+            copy.start()
         total[...] = jnp.zeros_like(total)
         back[...] = jnp.zeros_like(back)
         mid2_sum[...] = jnp.zeros_like(mid2_sum)
@@ -831,6 +839,8 @@
 
     @pl.when(step == steps - 1)
     def _():
+        for copy in copies():
+            copy.wait()
         mid2 = mid2_sum[...] * mask
         mid2_low = mid2.astype(bf16)
         resid = resid_ref[...]
@@ -843,13 +853,26 @@
         normed, inverse = normalize(resid)
         grad = og_ref[...].astype(f32) + norm_back(upstream * gain_ref[...], normed, inverse)
         grad_ref[...] = grad
-        branch_ref[...] = grad.astype(bf16)
+        branch = grad.astype(bf16)
         gd1_ref[...] = dot_nn(chosen_rows(mask, gm1_low), act_ref[...]).astype(bf16)
         gu2_ref[...] = (adapter_scale * dot_nn(chosen_rows(mask, mid2_low), og_ref[...])).astype(bf16)
+        middle = (adapter_scale * dot_nn(branch, up_ref[...]) * mask).astype(bf16)
+        grad_att = dot_nt(branch, wp_ref[...]) + dot_nt(middle, dp_ref[...])
+        grad_att_ref[...] = grad_att.astype(bf16)
+        product = grad_att_ref[...].astype(f32) * att_ref[...].astype(f32)
+        high = product.astype(bf16)
+        low = (product - high.astype(f32)).astype(bf16)
+        inner = dot_nt(sums_ref[...], high) + dot_nt(sums_ref[...], low)
+        for head in range(HEADS):
+            inner_ref[head] = inner[head : head + 1, :]
+        gdp_ref[...] = dot_nn(chosen_rows(mask, middle), att_ref[...]).astype(bf16)
+        own_t = chosen_rows(mask, midp_ref[...])
+        gup_ref[...] = (adapter_scale * dot_nn(own_t, branch)).astype(bf16)
 
 
 def feed_call(
-    resid, act, mid1, gm2, grad_act, og, mask, gain, w1, b1, w2, b2, down1, up1, down2, up2
+    act, mid1, gm2, grad_act, mask, gain, w1, b1, w2, b2, down1, up1, down2, up2, dp, up, midp,
+    sums, late,
 ):
     rows, features = act.shape
     wide = b1.shape[1]
@@ -866,15 +889,17 @@
         return pl.BlockSpec((block, width), lambda j: (j, 0))
 
     ins = [
-        resid, act, mid1, gm2, grad_act, og, mask, gain, w1, b1, w2, b2, down1, up1, down2, up2
+        act, mid1, gm2, grad_act, mask, gain, w1, b1, w2, b2, down1, up1, down2, up2, dp, up,
+        midp, sums,
     ]
     specs = [fixed(a.shape) for a in ins]
-    specs[4] = by_columns(rows)
-    specs[8] = by_columns(features)
-    specs[9] = by_columns(1)
-    specs[10] = by_rows(features)
-    specs[13] = by_rows(LANES)
-    specs[14] = by_rows(LANES)
+    specs[3] = by_columns(rows)
+    specs[6] = by_columns(features)
+    specs[7] = by_columns(1)
+    specs[8] = by_rows(features)
+    specs[11] = by_rows(LANES)
+    specs[12] = by_rows(LANES)
+    specs += [pl.BlockSpec(memory_space=pl.ANY)] * len(late)
     return pl.pallas_call(
         feed_kernel,
         name="feed",
@@ -884,9 +909,12 @@
             fixed((rows, features)),
             fixed((rows, features)),
             fixed((rows, features)),
+            fixed((HEADS, 1, rows)),
             fixed((RANK, features)),
             by_columns(RANK),
             by_columns(RANK),
+            fixed((RANK, features)),
+            fixed((RANK, features)),
             fixed((RANK, features)),
         ],
         scratch_shapes=[
@@ -896,63 +924,28 @@
             pltpu.VMEM((rows, LANES), f32),
             pltpu.VMEM((RANK, rows), bf16),
             pltpu.VMEM((RANK, rows), bf16),
-        ],
+            pltpu.SemaphoreType.DMA((len(late),)),
+        ]
+        + [pltpu.VMEM(a.shape, a.dtype) for a in late],
         out_shape=[
             jax.ShapeDtypeStruct((rows, features), bf16),
             jax.ShapeDtypeStruct((rows, features), f32),
             jax.ShapeDtypeStruct((rows, features), bf16),
+            jax.ShapeDtypeStruct((HEADS, 1, rows), f32),
             jax.ShapeDtypeStruct((RANK, features), bf16),
             jax.ShapeDtypeStruct((RANK, wide), bf16),
             jax.ShapeDtypeStruct((RANK, wide), bf16),
             jax.ShapeDtypeStruct((RANK, features), bf16),
+            jax.ShapeDtypeStruct((RANK, features), bf16),
+            jax.ShapeDtypeStruct((RANK, features), bf16),
         ],
-        compiler_params=params(("arbitrary",), 58),
+        compiler_params=params(("arbitrary",), 60),
         cost_estimate=pl.CostEstimate(
             flops=6 * rows * features * wide,
             bytes_accessed=4 * features * wide + 4 * rows * wide + 24 * rows * features,
             transcendentals=2 * rows * wide,
         ),
-    )(*ins)
-
-
-def unproject_kernel(
-    branch_ref, att_ref, weight_ref, down_ref, up_ref, mid_ref, mask_ref, sums_ref,
-    grad_ref, inner_ref, gd_ref, gu_ref,
-):
-    branch = branch_ref[...]
-    att = att_ref[...]
-    middle = (adapter_scale * dot_nn(branch, up_ref[...]) * mask_ref[...]).astype(bf16)
-    grad = dot_nt(branch, weight_ref[...]) + dot_nt(middle, down_ref[...])
-    grad_ref[...] = grad.astype(bf16)
-    product = grad_ref[...].astype(f32) * att.astype(f32)
-    high = product.astype(bf16)
-    low = (product - high.astype(f32)).astype(bf16)
-    inner = dot_nt(sums_ref[...], high) + dot_nt(sums_ref[...], low)
-    for head in range(HEADS):
-        inner_ref[head] = inner[head : head + 1, :]
-    gd_ref[...] = dot_nn(chosen_rows(mask_ref[...], middle), att).astype(bf16)
-    own_t = chosen_rows(mask_ref[...], mid_ref[...])
-    gu_ref[...] = (adapter_scale * dot_nn(own_t, branch)).astype(bf16)
-
-
-def unproject_call(branch, att, weight, down, up, mid, mask, sums):
-    rows, features = branch.shape
-    return pl.pallas_call(
-        unproject_kernel,
-        name="unproject",
-        out_shape=[
-            jax.ShapeDtypeStruct((rows, features), bf16),
-            jax.ShapeDtypeStruct((HEADS, 1, rows), f32),
-            jax.ShapeDtypeStruct((RANK, features), bf16),
-            jax.ShapeDtypeStruct((RANK, features), bf16),
-        ],
-        compiler_params=params(None, 50),
-        cost_estimate=pl.CostEstimate(
-            flops=2 * rows * features * features,
-            bytes_accessed=2 * features * features + 8 * rows * features,
-            transcendentals=0,
-        ),
-    )(branch, att, weight, down, up, mid, mask, sums)
+    )(*ins, *late)
 
 
 def close_kernel(
@@ -963,17 +956,13 @@
     devices = count * parts
     remote = courier_lines(dict(dp=count, seq=parts), []) is not None
     terms, refs = refs[:6], refs[6:]
-    if remote:
-        packs_ref, part_ref = refs[:2]
-        grads, refs = refs[2:10], refs[10:]
-    else:
-        part_ref, out_ref = refs[:2]
-        refs = refs[2:]
-    total, normed_ref, grad_up, grad_down, stage = refs[:5]
+    part_ref, out_ref = refs[:2]
+    refs = refs[2:]
+    total, grad_up, grad_down, stage = refs[:4]
     step = pl.program_id(0)
     features = x_ref.shape[1]
     if remote:
-        landed, sends, arrivals = refs[5:]
+        landed, sends, arrivals = refs[4:]
         me = lax.axis_index("dp") * parts + lax.axis_index("seq")
         barrier = pltpu.get_barrier_semaphore()
 
@@ -1015,7 +1004,6 @@
             grad_up[:, at] = (adapter_scale * dot_nn(own_t, source[...])).astype(bf16)
         middle = (adapter_scale * middle * mask_ref[...]).astype(bf16)
         normed, _ = normalize(x_ref[...].astype(f32))
-        normed_ref[...] = normed
         act = (normed * gain_ref[...].astype(f32) + shift_ref[...].astype(f32)).astype(bf16)
         total[...] = dot_nt(middle, down_ref[...])
         grad_down[...] = dot_nn(chosen_rows(mask_ref[...], middle), act).astype(bf16)
@@ -1046,34 +1034,19 @@
 
     @pl.when(step == 2)
     def _():
-        _, inverse = normalize(x_ref[...].astype(f32))
-        scaled = total[...] * gain_ref[...].astype(f32)
-        part_ref[...] = norm_back(scaled, normed_ref[...], inverse)
+        part_ref[...] = total[...]
         if remote:
-            row = lax.broadcasted_iota(jnp.int32, (devices * RANK, packs_ref.shape[0]), 0)
-            column = lax.broadcasted_iota(jnp.int32, (devices * RANK, packs_ref.shape[0]), 1)
-            chosen = (column == row // RANK * (packs_ref.shape[0] // devices) + VECTORS).astype(bf16)
-            adapter = dot_nn(chosen, packs_ref[:, :LANES])[:, 0:1]
-            row = lax.broadcasted_iota(jnp.int32, (devices * RANK, LANES), 0)
-            column = lax.broadcasted_iota(jnp.int32, (devices * RANK, LANES), 1)
-            same = (column // RANK).astype(f32) == adapter
-            spread = jnp.where(same & (row % RANK == column % RANK), 1.0, 0.0).astype(bf16)
 
             def wait(k, carry):
                 copy_to(k).wait()
                 return carry
 
             lax.fori_loop(1, devices, wait, 0)
-            sums = dot_tn(landed[...], spread)
-            at = 0
-            for target, width in zip(grads, widths):
-                target[...] = sums[at : at + width, :]
-                at += width
+            out_ref[...] = landed[...]
 
 
 def close_call(
     mesh_shape, widths, dq, dk, dv, weight, down, up, mid, mask, x, gain, shift, terms,
-    packs,
 ):
     rows, features = dq.shape
     devices = mesh_shape["dp"] * mesh_shape["seq"]
@@ -1087,9 +1060,11 @@
     ins = [dq, dk, dv, weight, down, up, mid, mask, x, gain, shift, *terms]
     specs = [fixed(a.shape) for a in ins]
     specs[3] = pl.BlockSpec((features, features), lambda j: (0, j))
-    shapes = [jax.ShapeDtypeStruct((rows, features), f32)]
+    shapes = [
+        jax.ShapeDtypeStruct((rows, features), f32),
+        jax.ShapeDtypeStruct((devices * RANK, span), bf16),
+    ]
     scratch = [
-        pltpu.VMEM((rows, features), f32),
         pltpu.VMEM((rows, features), f32),
         pltpu.VMEM((RANK, 3 * features), bf16),
         pltpu.VMEM((RANK, features), bf16),
@@ -1097,17 +1072,12 @@
     ]
     options = {}
     if remote:
-        ins.append(packs)
-        specs.append(fixed(packs.shape))
-        shapes += [jax.ShapeDtypeStruct((width, LANES), f32) for width in widths]
         scratch += [
             pltpu.VMEM((devices * RANK, span), bf16),
             pltpu.SemaphoreType.DMA((devices,)),
             pltpu.SemaphoreType.DMA((devices,)),
         ]
         options = dict(collective_id=4, has_side_effects=True)
-    else:
-        shapes.append(jax.ShapeDtypeStruct((devices * RANK, span), bf16))
     out = pl.pallas_call(
         functools.partial(close_kernel, (mesh_shape["dp"], mesh_shape["seq"]), widths),
         name="close",
@@ -1126,21 +1096,61 @@
         ),
     )(*ins)
     if remote:
-        return out[0], out[1:]
-    received = lax.all_to_all(
+        return out
+    landed = lax.all_to_all(
         out[1].reshape(devices, RANK, span), ("dp", "seq"), 0, 0, tiled=True
     ).reshape(devices * RANK, span)
-    rank = np.arange(devices * RANK)[:, None] % RANK
-    column = np.arange(LANES)[None, :]
-    source = packs.reshape(devices, -1, packs.shape[1])[:, VECTORS, 0].astype(jnp.int32)
-    images = jnp.broadcast_to(source[:, None], (devices, RANK)).reshape(devices * RANK, 1)
-    spread = ((images == column // RANK) & (rank == column % RANK)).astype(bf16)
-    sums = dot_tn(received, spread)
-    grads, at = [], 0
-    for width in widths:
-        grads.append(sums[at : at + width])
-        at += width
-    return out[0], grads
+    return out[0], landed
+
+
+def last_kernel(
+    devices, widths, upstream_ref, x_ref, gain_ref, resid_ref, landed_ref, packs_ref, out_ref,
+    *grads,
+):
+    normed, inverse = normalize(x_ref[...].astype(f32))
+    out_ref[...] = resid_ref[...] + norm_back(
+        upstream_ref[...] * gain_ref[...].astype(f32), normed, inverse
+    )
+
+    @pl.when(pl.program_id(0) == 0)
+    def _():
+        every = packs_ref.shape[0]
+        row = lax.broadcasted_iota(jnp.int32, (devices * RANK, every), 0)
+        column = lax.broadcasted_iota(jnp.int32, (devices * RANK, every), 1)
+        chosen = (column == row // RANK * (every // devices) + VECTORS).astype(bf16)
+        adapter = dot_nn(chosen, packs_ref[:, :LANES])[:, 0:1]
+        row = lax.broadcasted_iota(jnp.int32, (devices * RANK, LANES), 0)
+        column = lax.broadcasted_iota(jnp.int32, (devices * RANK, LANES), 1)
+        same = (column // RANK).astype(f32) == adapter
+        spread = jnp.where(same & (row % RANK == column % RANK), 1.0, 0.0).astype(bf16)
+        sums = dot_tn(landed_ref[...], spread)
+        at = 0
+        for target, width in zip(grads, widths):
+            target[...] = sums[at : at + width, :]
+            at += width
+
+
+def last_call(devices, widths, upstream, x, gain, resid, landed, packs):
+    rows, features = x.shape
+    tall = rows // 4 if rows % 64 == 0 else rows
+    by_rows = pl.BlockSpec((tall, features), lambda i: (i, 0))
+    return pl.pallas_call(
+        functools.partial(last_kernel, devices, widths),
+        name="last",
+        grid=(rows // tall,),
+        in_specs=[
+            by_rows,
+            by_rows,
+            whole((1, features)),
+            by_rows,
+            whole(landed.shape),
+            whole(packs.shape),
+        ],
+        out_specs=[by_rows] + [whole((width, LANES)) for width in widths],
+        out_shape=[jax.ShapeDtypeStruct((rows, features), f32)]
+        + [jax.ShapeDtypeStruct((width, LANES), f32) for width in widths],
+        compiler_params=params(("arbitrary",), 50),
+    )(upstream, x, gain, resid, landed, packs)
 
 
 def position_tables(rel_h, rel_w, length):
@@ -1150,7 +1160,7 @@
     h_back = jnp.pad(rel_h[::-1], wide)
     w_back = jnp.pad(rel_w[::-1], wide)
     forward = jnp.concatenate([h_back, h_back, w_back, w_back], axis=0).T
-    backward = jnp.concatenate([h, h, w, w], axis=0)
+    backward = jnp.concatenate([h, w], axis=0)
     spot = np.arange(length)[:, None]
     lane = np.arange(LANES)[None, :]
     at = np.where((lane // G) % 2 == 0, spot // G, spot % G)
@@ -1250,12 +1260,10 @@
         att, own_tokens, og, w_proj, b_proj, d_proj, u_proj, mask, g2, s2, w_fc2, d_fc1, d_fc2,
         u_fc2,
     )
-    block_out, grad_resid, grad_branch, gd_fc1, gu_fc1, gd_fc2, gu_fc2 = feed_call(
-        resid, act_two, mid_fc1, gm_fc2, grad_act, og, mask, g2, w_fc1, b_fc1, w_fc2, b_fc2,
-        d_fc1, u_fc1, d_fc2, u_fc2,
-    )
-    grad_att, inner, gd_proj, gu_proj = unproject_call(
-        grad_branch, att, w_proj, d_proj, u_proj, mid_proj, mask, head_sums
+    (block_out, grad_resid, grad_att, inner, gd_fc1, gu_fc1, gd_fc2, gu_fc2, gd_proj,
+     gu_proj) = feed_call(
+        act_two, mid_fc1, gm_fc2, grad_act, mask, g2, w_fc1, b_fc1, w_fc2, b_fc2, d_fc1, u_fc1,
+        d_fc2, u_fc2, d_proj, u_proj, mid_proj, head_sums, [resid, og, att, w_proj],
     )
     if part_count == 2:
         swap = [(0, 1), (1, 0)]
@@ -1275,13 +1283,16 @@
     mid_own = lax.dynamic_slice_in_dim(mid_qkv, place[0] * part_len, part_len, 0)
     widths = [a.shape[0] for a in (qkv_down, proj_down, fc1_down, fc2_down)]
     widths += [a.shape[1] for a in (qkv_up, proj_up, fc1_up, fc2_up)]
-    last_part, grads = close_call(
-        mesh_shape, widths, dq, dk, dv, w_qkv, d_qkv, u_qkv, mid_own, mask, own_tokens, g1,
-        s1, [gd_proj, gd_fc1, gd_fc2, gu_proj, gu_fc1, gu_fc2], all_small,
+    upstream, landed = close_call(
+        mesh_shape, widths, dq, dk, dv, w_qkv, d_qkv, u_qkv, mid_own, mask, own_tokens, g1, s1,
+        [gd_proj, gd_fc1, gd_fc2, gu_proj, gu_fc1, gu_fc2],
+    )
+    input_grad, *grads = last_call(
+        devices, widths, upstream, own_tokens, g1, grad_resid, landed, all_small
     )
     return (
         block_out[None],
-        (grad_resid + last_part)[None],
+        input_grad[None],
         grads[0],
         grads[4].T,
         grads[1],

time: 431 us -> 406 us (0.942)
  Pallas kernels: 364 us -> 351 us
  local copies, waits for them, and re-layouts: 25.9 us -> 15.9 us
    unnamed x74 -> x30, local copies, waits for them, and re-layouts: 16.3 us -> 6.36 us
    pallas_call x1, Pallas kernels: 37.7 us -> 28.9 us  [own_call(): pl.pallas_call(own_kernel, name='back_own', grid_spec=pltpu.PrefetchScala...]
    pallas_call x2, Pallas kernels: 29.5 us -> 21 us  [the longest x1 14.7 us: other_call(): pl.pallas_call(functools.partial(other_kernel, count - 1), name='back_oth...]
    pallas_call x1, Pallas kernels: 47.3 us -> 52.8 us  [feed_call(): pl.pallas_call(feed_kernel, name='feed', grid=(wide // block,), in_specs=...]
  transfers between devices with their start and end apart: 5 -> 5, of which waited for: 1 -> 2; matrix products, arithmetic and copies ran while one was open for 3% -> 4% of each run, Pallas kernels for 74% -> 75%
where the time goes in v3:
time: 406 us; the launch traced here: 401 us
  Pallas kernels  351 us (86%)
  local copies, waits for them, and re-layouts  15.9 us (4%)
  between operations  15.1 us (4%)
  waiting for transfers between devices  12.9 us (3%)
    pallas_call x1, Pallas kernels, collect(): pl.pallas_call(functools.partial(collect_kernel, lines, chunks, [a.shape[...  109 us
    pallas_call x1, Pallas kernels, front_call(): pl.pallas_call(functools.partial(front_kernel, lines, chunks, [a.shape[0]...  90.3 us
    pallas_call x1, Pallas kernels, feed_call(): pl.pallas_call(feed_kernel, name='feed', grid=(wide // block,), in_specs=...  52.8 us
    pallas_call x1, Pallas kernels, own_call(): pl.pallas_call(own_kernel, name='back_own', grid_spec=pltpu.PrefetchScala...  28.9 us
    pallas_call x1, Pallas kernels, close_call(): pl.pallas_call(functools.partial(close_kernel, (mesh_shape['dp'], mesh_sh...  28.6 us
    pallas_call x1, Pallas kernels, before_call(): pl.pallas_call(before_kernel, name='before', grid=(wide // block,), in_sp...  20.1 us
    pallas_call x1, Pallas kernels, other_call(): pl.pallas_call(functools.partial(other_kernel, count - 1), name='back_oth...  14.7 us
    all_gather x1, waiting for transfers between devices, per_device(): w_fc1 = lax.all_gather(fc1_weight, axes, axis=0, tiled=True)  10.6 us
  transfers between devices with their start and end apart: 5, of which 2 were waited for; matrix products, arithmetic and copies ran while one was open for 4% of the time, Pallas kernels for 75%

profile of v3, /device:TPU:15, one launch (start us, length us, event | category | flops | bytes accessed | tf_op | source)
XLA Modules:
  0.0 401.0 jit_solution(11142622621675988983)
XLA Ops:
  7.2 0.7 all-gather.3.cloned.1.call-update
  8.0 0.7 all-gather.5.cloned.1.call-update
  9.3 0.7 pad.48
  10.0 0.7 pad.49
  10.6 0.7 pad.50
  11.3 0.7 pad.51
  12.0 0.7 pad.52
  12.6 0.7 pad.53
  13.3 0.7 pad.54
  13.9 0.7 pad.55
  16.9 0.8 copy.38
  17.8 0.8 copy.39
  18.7 109.4 %collect.1 = (bf16[1280,3840]{1,0:T(8,128)(2,1)}, bf16[1280,128]{1,0:T(8,128)(2,1)}, bf16[3840,128]{1,0:T(8,128)(2,1)}, bf16[512,256]{1,0:T(8,128)(2,1)}, bf16[512,1280]{1,0:T(8,128)(2,1)}) custom-call(bf16[40,3840]{1,0:T(8,128)(2,1)} %refs_0_.1, bf16[40,128]{1,0:T(8,128)(2,1)} %refs_1_.1, bf16[120,128]{1,0:T(8,128)(2,1)} %bitcast.28, ...), custom_call_target="tpu_custom_call" | custom-call | tf_op jit(solution)/shard_map/collect/pallas_call | solution.py:297
  128.2 0.9 copy-done.1
  130.5 0.7 maximum_bitcast_fusion.table_ref
  131.2 0.6 fusion.3
  131.9 90.3 %front.1 = (bf16[3,16,1024,128]{3,2,1,0:T(8,128)(2,1)}, bf16[1024,128]{1,0:T(8,128)(2,1)}, bf16[512,1280]{1,0:T(8,128)(2,1)}, f32[16,1,512]{2,1,0:T(1,128)}, bf1...) custom-call(f32[1,1280]{1,0:T(1,128)} %get-tuple-element.113.gain_re, ...), custom_call_target="tpu_custom_call" | custom-call | flops 18656264192 | bytes 30801920 | tf_op jit(solution)/shard_map/front/pallas_call | solution.py:475
  222.2 2.2 collective-permute-start.1
  224.5 0.6 slice.38.b1_ref
  225.1 0.6 fusion.2.table_ref
  225.7 1.5 constant_dynamic-slice_fusion.mid_ref
  227.3 20.1 %before.1 = (f32[512,1280]{1,0:T(8,128)}, bf16[512,1280]{1,0:T(8,128)(2,1)}, bf16[512,128]{1,0:T(8,128)(2,1)}, bf16[512,128]{1,0:T(8,128)(2,1)}, bf16[512,128]{1,0:T(8,128)(2,1)}, /*index=5*/f32[512,5120]{1,0:T(8,128)}) custom-call(bf16[512,1280]{1,0:T(8,128)(2,1)} %get-tuple-element.64.att_ref.refs_2_, bf16[512,1280]{1,0:T(8,128)(2,1)} %bitcast.22, ...), custom_call_target="tpu_custom_call" | custom-call | flops 8388608000 | bytes 34078720 | tf_op jit(solution)/shard_map/before/pallas_call | solution.py:777
  247.3 10.6 %all-gather.5.cloned.1.call-done.w1_ref = bf16[1280,5120]{1,0:T(8,128)(2,1)} async-done(((bf16[40,5120]{1,0:T(8,128)(2,1)}), bf16[1280,5120]{1,0:T(8,128)(2,1)}) %all-gather.5.cloned.1.call-update) | async-done | bytes 13107216 | tf_op jit(solution)/shard_map/all_gather | solution.py:1245
  258.0 52.8 %feed.1 = (bf16[512,1280]{1,0:T(8,128)(2,1)}, f32[512,1280]{1,0:T(8,128)}, bf16[512,1280]{1,0:T(8,128)(2,1)}, f32[16,1,512]{2,1,0:T(1,128)}, bf16[16,1280]{1,0:T...) custom-call(bf16[512,1280]{1,0:T(8,128)(2,1)} %get-tuple-element.71., ...), custom_call_target="tpu_custom_call" | custom-call | flops 20132659200 | bytes 52428800 | tf_op jit(solution)/shard_map/feed/pallas_call | solution.py:903
  310.8 1.3 collective-permute-start.2
  312.4 28.9 %back_own.1 = (bf16[512,1280]{1,0:T(8,128)(2,1)}, f32[16,512,128]{2,1,0:T(8,128)}, f32[16,512,128]{2,1,0:T(8,128)}) custom-call(s32[1]{0:T(128)} %bitcast.9.place_ref, bf16[3,16,1024,128]{3,2,1,0:T(8,128)(2,1)} %get-tuple-element.79.q_ref.k_ref.v_ref, bf16[16,1024,128]{2,1,0:T(8,128)(2,1)} %get-tuple-element.80.aux_ref, ...), custom_call_target="tpu_custom_call" | custom-call | flops 17179869184 | bytes 25165824 | tf_op jit(solution)/shard_map/back_own/pallas_call | solution.py:576
  341.3 0.9 collective-permute-done
  342.1 1.1 copy-done.5
  343.2 14.7 %back_other.1 = (bf16[512,1280]{1,0:T(8,128)(2,1)}, bf16[512,1280]{1,0:T(8,128)(2,1)}) custom-call(s32[1]{0:T(128)} %bitcast.9.place_ref, bf16[3,16,1024,128]{3,2,1,0:T(8,128)(2,1)} %get-tuple-element.79.q_ref.k_ref.v_ref, bf16[16,1024,128]{2,1,0:T(8,128)(2,1)} %get-tuple-element.80.aux_ref, bf16[3,16,1024,128]{3,2,1,0:T(8,128)(2,1)} %get-tuple-element.79.q_ref.k_ref.v_ref, ...), custom_call_target="tpu_custom_call" | custom-call | flops 4294967296 | bytes 25165824 | tf_op jit(solution)/shard_map/back_other/pallas_call | solution.py:682
  358.0 28.6 %close.1 = (f32[512,1280]{1,0:T(8,128)}, bf16[512,640]{1,0:T(8,128)(2,1)}) custom-call(bf16[512,1280]{1,0:T(8,128)(2,1)} %get-tuple-element.84.dq_ref, bf16[512,1280]{1,0:T(8,128)(2,1)} %get-tuple-element.87.dk_ref, bf16[512,1280]{1,0:T(8,128)(2,1)} %get-tuple-element.88.dv_ref, bf16[1280,3840]{1,0:T(8,128)(2,1)} %get-tuple-element.60.weight_ref, ...), custom_call_target="tpu_custom_call" | custom-call | flops 5033164800 | bytes 22937600 | tf_op jit(solution)/shard_map/close/pallas_call | solution.py:1081
  386.7 1.1 copy-done.3
  387.8 6.2 %last.1 = (f32[512,1280]{1,0:T(8,128)}, f32[40,128]{1,0:T(8,128)}, f32[40,128]{1,0:T(8,128)}, f32[40,128]{1,0:T(8,128)}, f32[160,128]{1,0:T(8,128)}, /*index=5*/...) custom-call(f32[512,1280]{1,0:T(8,128)} %get-tuple-element.96.upstream_ref, ...), custom_call_target="tpu_custom_call" | custom-call | tf_op jit(solution)/shard_map/last/pallas_call | solution.py:1137
  (42 shorter events, 4.2 us)
Async XLA Ops:
  7.2 220.1 %all-gather.3.cloned.1.call-start = ((), (), s32[]{:S(2)}) async-start(), calls=%async_computation | async-start | bytes 13516800 | tf_op jit(solution)/shard_map/all_gather | solution.py:1244
  7.9 250.1 %all-gather.5.cloned.1.call-start = ((), (), s32[]{:S(2)}) async-start(), calls=%async_computation.1 | async-start | bytes 13516800 | tf_op jit(solution)/shard_map/all_gather | solution.py:1245
  128.1 1.0 copy-start.1
  131.9 93.2 %copy-start.6 = (bf16[63,80]{1,0:T(8,128)(2,1)S(1)}, bf16[63,80]{1,0:T(8,128)(2,1)}, u32[]{:S(2)}) copy-start(bf16[63,80]{1,0:T(8,128)(2,1)} %param.43) | copy-start | bytes 30244
  131.9 93.2 %copy-start.7 = (bf16[63,80]{1,0:T(8,128)(2,1)S(1)}, bf16[63,80]{1,0:T(8,128)(2,1)}, u32[]{:S(2)}) copy-start(bf16[63,80]{1,0:T(8,128)(2,1)} %param.42) | copy-start | bytes 30244
  222.2 119.0 %collective-permute-start.1 = (f32[16,1,512]{2,1,0:T(1,128)}, f32[16,1,512]{2,1,0:T(1,128)S(1)}, u32[]{:S(2)}, u32[]{:S(2)}) collective-permute-start(f32[16,1,512]{2,1,0:T(1,128)} %get-tuple-element.82.lse_ref), channel_id=1, source_target_pairs={{0,1},{1,0},{2,3},{3,2},{4,5},{5,4},{6,7},{7,6},{8,9},{9,8},{10,11... | collective-permute-start | bytes 98312 | tf_op jit(solution)/shard_map/ppermute | solution.py:1271
  310.8 30.4 %collective-permute-start.2 = (f32[16,1,512]{2,1,0:T(1,128)}, f32[16,1,512]{2,1,0:T(1,128)S(1)}, u32[]{:S(2)}, u32[]{:S(2)}) collective-permute-start(f32[16,1,512]{2,1,0:T(1,128)} %get-tuple-element.83.inner_ref), channel_id=1, source_target_pairs={{0,1},{1,0},{2,3},{3,2},{4,5},{5,4},{6,7},{7,6},{8,9},{9,8},{10,11... | collective-permute-start | bytes 98312 | tf_op jit(solution)/shard_map/ppermute | solution.py:1271
  312.1 30.0 %collective-permute-start = (bf16[512,1280]{1,0:T(8,128)(2,1)}, bf16[512,1280]{1,0:T(8,128)(2,1)S(1)}, u32[]{:S(2)}, u32[]{:S(2)}) collective-permute-start(bf16[512,1280]{1,0:T(8,128)(2,1)} %get-tuple-element.81.grad_ref), channel_id=1, source_target_pairs={{0,1},{1,0},{2,3},{3,2},{4,5},{5,4},{6,7},{7,6},{8,9},{9,8},{10,11... | collective-permute-start | bytes 3932168 | tf_op jit(solution)/shard_map/ppermute | solution.py:1271
  341.2 0.9 copy-start.8
  341.3 0.9 copy-start.9
  342.1 1.1 copy-start.5
  358.0 28.7 %copy-start = (bf16[1,512,1280]{2,1,0:T(8,128)(2,1)S(1)}, bf16[1,512,1280]{2,1,0:T(8,128)(2,1)}, u32[]{:S(2)}) copy-start(bf16[1,512,1280]{2,1,0:T(8,128)(2,1)} %param.28) | copy-start | bytes 3932164
  358.0 28.7 %copy-start.2 = (bf16[512,256]{1,0:T(8,128)(2,1)S(1)}, bf16[512,256]{1,0:T(8,128)(2,1)}, u32[]{:S(2)}) copy-start(bf16[512,256]{1,0:T(8,128)(2,1)} %get-tuple-element.59.source.packs_ref) | copy-start | bytes 786436
  358.0 28.7 %copy-start.4 = (f32[1,1280]{1,0:T(1,128)S(1)}, f32[1,1280]{1,0:T(1,128)}, u32[]{:S(2)}) copy-start(f32[1,1280]{1,0:T(1,128)} %get-tuple-element.113.gain_ref) | copy-start | bytes 15364
  386.7 1.1 copy-start.3
Sparse Core Ops, SparseCore 0:
  10.9 136.8 all-gather.2
  150.6 107.3 all-gather.4

commit v4 on v3

--- a/solution.py
+++ b/solution.py
@@ -263,48 +263,35 @@
 
 
 def collect_kernel(lines, chunks, rows_of, count, *refs):
-    sources, tokens = refs[:count], refs[count]
-    targets, other = refs[count + 1 : 2 * count + 1], refs[2 * count + 1]
-    local, sends, arrivals, token_sem = refs[2 * count + 2 :]
-    courier = Courier(lines, chunks, rows_of, sources, targets, local, sends, arrivals)
+    courier = Courier(lines, chunks, rows_of, refs[:count], refs[count : 2 * count], *refs[2 * count :])
     courier.greet()
-    passed = pltpu.make_async_remote_copy(
-        src_ref=tokens,
-        dst_ref=other,
-        send_sem=token_sem.at[0],
-        recv_sem=token_sem.at[1],
-        device_id=courier.partner,
-        device_id_type=pl.DeviceIdType.MESH,
-    )
     for number in range(len(chunks)):
         courier.start(number)
-    passed.start()
     for step in courier.steps():
         step()
-    passed.wait()
     courier.finish()
 
 
-def collect(mesh_shape, arrays, tokens):
-    axes = ("dp", "seq")
+def collect(mesh_shape, arrays):
     lines = courier_lines(mesh_shape, arrays)
     if lines is None:
-        gathered = [lax.all_gather(a, axes, axis=0, tiled=True) for a in arrays]
-        return gathered, [lax.all_gather(tokens, "seq", axis=0, tiled=True)]
-    chunks = cut_chunks(arrays, 1)
+        return [lax.all_gather(a, ("dp", "seq"), axis=0, tiled=True) for a in arrays]
+    chunks = cut_chunks(arrays, 2)
     anywhere = pl.BlockSpec(memory_space=pl.ANY)
     count = len(arrays)
-    out = pl.pallas_call(
+    size = sum(a.size for a in arrays)
+    return pl.pallas_call(
         functools.partial(collect_kernel, lines, chunks, [a.shape[0] for a in arrays], count),
         name="collect",
-        in_specs=[anywhere] * (count + 1),
-        out_specs=[anywhere] * (count + 1),
-        out_shape=gathered_shapes(mesh_shape["dp"] * 2, arrays)
-        + [jax.ShapeDtypeStruct(tokens.shape, tokens.dtype)],
-        scratch_shapes=courier_scratch(lines, chunks) + [pltpu.SemaphoreType.DMA((2,))],
+        in_specs=[anywhere] * count,
+        out_specs=[anywhere] * count,
+        out_shape=gathered_shapes(mesh_shape["dp"] * 2, arrays),
+        scratch_shapes=courier_scratch(lines, chunks),
         compiler_params=pltpu.CompilerParams(collective_id=1, has_side_effects=True),
-    )(*arrays, tokens)
-    return list(out[:count]), [tokens, out[count]]
+        cost_estimate=pl.CostEstimate(
+            flops=0, bytes_accessed=64 * mesh_shape["dp"] * size, transcendentals=0
+        ),
+    )(*arrays)
 
 
 def qkv_part(part, blocks, gain_ref, shift_ref, weight_ref, bias_ref, down_ref, up_ref, mask_ref,
@@ -799,8 +786,8 @@
     late = refs[:4]
     (out_ref, grad_ref, grad_att_ref, inner_ref, gd1_ref, gu1_ref, gd2_ref, gu2_ref, gdp_ref,
      gup_ref) = refs[4:14]
-    total, back, mid2_sum, gm1_sum, gm2_t, mid1_t, late_sem = refs[14:21]
-    held = refs[21:]
+    total, back, mid2_sum, gm1_sum, gm2_t, mid1_t, late_sem, acts, grads = refs[14:23]
+    held = refs[23:]
     resid_ref, og_ref, att_ref, wp_ref = held
 
     step = pl.program_id(0)
@@ -824,15 +811,29 @@
         gm2_t[...] = chosen_rows(mask, gm2_ref[...])
         mid1_t[...] = chosen_rows(mask, mid1_ref[...])
 
-    weight = w1_ref[...]
-    hidden = dot_nn(act_ref[...], weight) + b1_ref[...]
-    hidden = hidden + adapter_scale * dot_nt(mid1_ref[...], up1_ref[...])
-    value, slope = gelu_parts(hidden)
-    activated = value.astype(bf16)
-    grad_hidden = (grad_act_ref[...] * slope).astype(bf16)
+    wide = w2_ref.shape[0] // 4
+
+    def first(at):
+        cols = pl.ds(at, wide)
+        hidden = dot_nn(act_ref[...], w1_ref[:, cols]) + b1_ref[:, cols]
+        return hidden + adapter_scale * dot_nt(mid1_ref[...], up1_ref[cols, :])
+
+    sums = []
+    coming = first(0)
+    for at in range(0, w2_ref.shape[0], wide):
+        cols = pl.ds(at, wide)
+        hidden = coming
+        if at + wide < w2_ref.shape[0]:
+            coming = first(at + wide)
+        value, slope = gelu_parts(hidden)
+        activated = value.astype(bf16)
+        grad_hidden = (grad_act_ref[:, cols] * slope).astype(bf16)
+        acts[:, cols] = activated
+        grads[:, cols] = grad_hidden
+    activated, grad_hidden = acts[...], grads[...]
     total[...] += dot_nn(activated, w2_ref[...])
     mid2_sum[...] += dot_nn(activated, down2_ref[...])
-    back[...] += dot_nt(grad_hidden, weight)
+    back[...] += dot_nt(grad_hidden, w1_ref[...])
     gm1_sum[...] += dot_nn(grad_hidden, up1_ref[...])
     gd2_ref[...] = dot_nn(gm2_t[...], activated).astype(bf16)
     gu1_ref[...] = (adapter_scale * dot_nn(mid1_t[...], grad_hidden)).astype(bf16)
@@ -876,7 +877,7 @@
 ):
     rows, features = act.shape
     wide = b1.shape[1]
-    block = 512
+    block = 1024
 
     def fixed(shape):
         zeros = (0,) * len(shape)
@@ -925,6 +926,8 @@
             pltpu.VMEM((RANK, rows), bf16),
             pltpu.VMEM((RANK, rows), bf16),
             pltpu.SemaphoreType.DMA((len(late),)),
+            pltpu.VMEM((rows, block), bf16),
+            pltpu.VMEM((rows, block), bf16),
         ]
         + [pltpu.VMEM(a.shape, a.dtype) for a in late],
         out_shape=[
@@ -1243,9 +1246,11 @@
 
     w_fc2 = lax.all_gather(fc2_weight, axes, axis=0, tiled=True)
     w_fc1 = lax.all_gather(fc1_weight, axes, axis=0, tiled=True)
-    (w_qkv, d_qkv, u_qkv, all_small), image_tokens = collect(
-        mesh_shape, [qkv_weight, qkv_down, qkv_up.T, pack], own_tokens
-    )
+    if part_count == 2:
+        image_tokens = [own_tokens, lax.ppermute(own_tokens, "seq", [(0, 1), (1, 0)])]
+    else:
+        image_tokens = [lax.all_gather(own_tokens, "seq", axis=0, tiled=True)]
+    w_qkv, d_qkv, u_qkv, all_small = collect(mesh_shape, [qkv_weight, qkv_down, qkv_up.T, pack])
     vectors = vectors_call(all_small, devices, sizes[:VECTORS])
     g1, s1, b_qkv, b_proj, g2, s2, b_fc1, b_fc2 = (
         vectors[i : i + 1, : devices * sizes[i]] for i in range(VECTORS)

time: 406 us -> 399 us (0.983)
  Pallas kernels: 351 us -> 334 us
  waiting for transfers between devices: 12.9 us -> 22.9 us
    pallas_call x1, Pallas kernels: 109 us -> 86.7 us  [collect(): pl.pallas_call(functools.partial(collect_kernel, lines, chunks, [a.shape[...]
    all_gather x1, waiting for transfers between devices: 10.6 us -> 21 us  [per_device(): w_fc1 = lax.all_gather(fc1_weight, axes, axis=0, tiled=True)]
    pallas_call x1, Pallas kernels: 90.3 us -> 97.8 us  [front_call(): pl.pallas_call(functools.partial(front_kernel, lines, chunks, [a.shape[0]...]
  transfers between devices with their start and end apart: 5 -> 6, of which waited for: 2 -> 2; matrix products, arithmetic and copies ran while one was open for 4% -> 4% of each run, Pallas kernels for 75% -> 72%
where the time goes in v4:
time: 399 us; the launch traced here: 394 us
  Pallas kernels  334 us (84%)
  waiting for transfers between devices  22.9 us (6%)
  local copies, waits for them, and re-layouts  16.9 us (4%)
  between operations  15.1 us (4%)
    pallas_call x1, Pallas kernels, front_call(): pl.pallas_call(functools.partial(front_kernel, lines, chunks, [a.shape[0]...  97.8 us
    pallas_call x1, Pallas kernels, collect(): pl.pallas_call(functools.partial(collect_kernel, lines, chunks, [a.shape[...  86.7 us
    pallas_call x1, Pallas kernels, feed_call(): pl.pallas_call(feed_kernel, name='feed', grid=(wide // block,), in_specs=...  49.3 us
    pallas_call x1, Pallas kernels, own_call(): pl.pallas_call(own_kernel, name='back_own', grid_spec=pltpu.PrefetchScala...  29.1 us
    pallas_call x1, Pallas kernels, close_call(): pl.pallas_call(functools.partial(close_kernel, (mesh_shape['dp'], mesh_sh...  28.4 us
    pallas_call x1, Pallas kernels, before_call(): pl.pallas_call(before_kernel, name='before', grid=(wide // block,), in_sp...  21.6 us
    all_gather x1, waiting for transfers between devices, per_device(): w_fc1 = lax.all_gather(fc1_weight, axes, axis=0, tiled=True)  21 us
    pallas_call x1, Pallas kernels, other_call(): pl.pallas_call(functools.partial(other_kernel, count - 1), name='back_oth...  14.7 us
  transfers between devices with their start and end apart: 6, of which 2 were waited for; matrix products, arithmetic and copies ran while one was open for 4% of the time, Pallas kernels for 72%

profile of v4, /device:TPU:15, one launch (start us, length us, event | category | flops | bytes accessed | tf_op | source)
XLA Modules:
  0.0 393.6 jit_solution(14581382503226788968)
XLA Ops:
  7.2 0.7 all-gather.3.cloned.1.call-update
  8.0 0.7 all-gather.5.cloned.1.call-update
  9.6 0.7 pad.48
  10.3 0.7 pad.49
  10.9 0.7 pad.50
  11.6 0.7 pad.51
  12.3 0.7 pad.52
  12.9 0.7 pad.53
  13.6 0.7 pad.54
  14.2 0.7 pad.55
  17.1 86.7 %collect.1 = (bf16[1280,3840]{1,0:T(8,128)(2,1)}, bf16[1280,128]{1,0:T(8,128)(2,1)}, bf16[3840,128]{1,0:T(8,128)(2,1)}, bf16[512,256]{1,0:T(8,128)(2,1)}) custom-call(bf16[40,3840]{1,0:T(8,128)(2,1)} %refs_0_.1, bf16[40,128]{1,0:T(8,128)(2,1)} %refs_1_.1, bf16[120,128]{1,0:T(8,128)(2,1)} %bitcast.28, bf16[16,256]{1,0:T(8,128)(2,1)} %pad.57.refs_3_), custom_call_target="tpu_custom_call" | custom-call | bytes 182452224 | tf_op jit(solution)/shard_map/collect/pallas_call | solution.py:283
  103.9 0.9 copy-done.1
  105.0 0.6 slice.34.bias_ref
  105.7 0.6 slice.38.b1_ref
  106.3 0.8 copy.38
  107.2 0.8 copy.39
  108.7 1.4 fusion.2.table_ref
  110.1 0.7 maximum_bitcast_fusion.table_ref
  110.8 0.6 fusion.3
  111.5 1.1 copy-done.8
  112.5 97.8 %front.1 = (bf16[3,16,1024,128]{3,2,1,0:T(8,128)(2,1)}, bf16[1024,128]{1,0:T(8,128)(2,1)}, bf16[512,1280]{1,0:T(8,128)(2,1)}, f32[16,1,512]{2,1,0:T(1,128)}, bf1...) custom-call(f32[1,1280]{1,0:T(1,128)} %get-tuple-element.111.gain_re, ...), custom_call_target="tpu_custom_call" | custom-call | flops 18656264192 | bytes 30801920 | tf_op jit(solution)/shard_map/front/pallas_call | solution.py:462
  210.4 1.6 constant_dynamic-slice_fusion.mid_ref
  211.9 21.6 %before.1 = (f32[512,1280]{1,0:T(8,128)}, bf16[512,1280]{1,0:T(8,128)(2,1)}, bf16[512,128]{1,0:T(8,128)(2,1)}, bf16[512,128]{1,0:T(8,128)(2,1)}, bf16[512,128]{1,0:T(8,128)(2,1)}, /*index=5*/f32[512,5120]{1,0:T(8,128)}) custom-call(bf16[512,1280]{1,0:T(8,128)(2,1)} %get-tuple-element.62.att_ref.refs_2_, bf16[512,1280]{1,0:T(8,128)(2,1)} %bitcast.22, ...), custom_call_target="tpu_custom_call" | custom-call | flops 8388608000 | bytes 34078720 | tf_op jit(solution)/shard_map/before/pallas_call | solution.py:764
  233.5 21.0 %all-gather.5.cloned.1.call-done.w1_ref = bf16[1280,5120]{1,0:T(8,128)(2,1)} async-done(((bf16[40,5120]{1,0:T(8,128)(2,1)}), bf16[1280,5120]{1,0:T(8,128)(2,1)}) %all-gather.5.cloned.1.call-update) | async-done | bytes 13107216 | tf_op jit(solution)/shard_map/all_gather | solution.py:1248
  254.5 49.3 %feed.1 = (bf16[512,1280]{1,0:T(8,128)(2,1)}, f32[512,1280]{1,0:T(8,128)}, bf16[512,1280]{1,0:T(8,128)(2,1)}, f32[16,1,512]{2,1,0:T(1,128)}, bf16[16,1280]{1,0:T...) custom-call(bf16[512,1280]{1,0:T(8,128)(2,1)} %get-tuple-element.69., ...), custom_call_target="tpu_custom_call" | custom-call | flops 20132659200 | bytes 52428800 | tf_op jit(solution)/shard_map/feed/pallas_call | solution.py:904
  303.8 1.2 collective-permute-start.3
  305.4 29.1 %back_own.1 = (bf16[512,1280]{1,0:T(8,128)(2,1)}, f32[16,512,128]{2,1,0:T(8,128)}, f32[16,512,128]{2,1,0:T(8,128)}) custom-call(s32[1]{0:T(128)} %bitcast.9.place_ref, bf16[3,16,1024,128]{3,2,1,0:T(8,128)(2,1)} %get-tuple-element.77.q_ref.k_ref.v_ref, bf16[16,1024,128]{2,1,0:T(8,128)(2,1)} %get-tuple-element.78.aux_ref, ...), custom_call_target="tpu_custom_call" | custom-call | flops 17179869184 | bytes 25165824 | tf_op jit(solution)/shard_map/back_own/pallas_call | solution.py:563
  335.1 1.0 copy-done.5
  336.1 14.7 %back_other.1 = (bf16[512,1280]{1,0:T(8,128)(2,1)}, bf16[512,1280]{1,0:T(8,128)(2,1)}) custom-call(s32[1]{0:T(128)} %bitcast.9.place_ref, bf16[3,16,1024,128]{3,2,1,0:T(8,128)(2,1)} %get-tuple-element.77.q_ref.k_ref.v_ref, bf16[16,1024,128]{2,1,0:T(8,128)(2,1)} %get-tuple-element.78.aux_ref, bf16[3,16,1024,128]{3,2,1,0:T(8,128)(2,1)} %get-tuple-element.77.q_ref.k_ref.v_ref, ...), custom_call_target="tpu_custom_call" | custom-call | flops 4294967296 | bytes 25165824 | tf_op jit(solution)/shard_map/back_other/pallas_call | solution.py:669
  350.8 28.4 %close.1 = (f32[512,1280]{1,0:T(8,128)}, bf16[512,640]{1,0:T(8,128)(2,1)}) custom-call(bf16[512,1280]{1,0:T(8,128)(2,1)} %get-tuple-element.82.dq_ref, bf16[512,1280]{1,0:T(8,128)(2,1)} %get-tuple-element.85.dk_ref, bf16[512,1280]{1,0:T(8,128)(2,1)} %get-tuple-element.86.dv_ref, bf16[1280,3840]{1,0:T(8,128)(2,1)} %get-tuple-element.59.weight_ref, ...), custom_call_target="tpu_custom_call" | custom-call | flops 5033164800 | bytes 22937600 | tf_op jit(solution)/shard_map/close/pallas_call | solution.py:1084
  379.2 1.1 copy-done.3
  380.3 6.2 %last.1 = (f32[512,1280]{1,0:T(8,128)}, f32[40,128]{1,0:T(8,128)}, f32[40,128]{1,0:T(8,128)}, f32[40,128]{1,0:T(8,128)}, f32[160,128]{1,0:T(8,128)}, /*index=5*/...) custom-call(f32[512,1280]{1,0:T(8,128)} %get-tuple-element.94.upstream_ref, ...), custom_call_target="tpu_custom_call" | custom-call | tf_op jit(solution)/shard_map/last/pallas_call | solution.py:1140
  (42 shorter events, 4.7 us)
Async XLA Ops:
  7.2 204.8 %all-gather.3.cloned.1.call-start = ((), (), s32[]{:S(2)}) async-start(), calls=%async_computation | async-start | bytes 13516800 | tf_op jit(solution)/shard_map/all_gather | solution.py:1247
  7.9 246.6 %all-gather.5.cloned.1.call-start = ((), (), s32[]{:S(2)}) async-start(), calls=%async_computation.1 | async-start | bytes 13516800 | tf_op jit(solution)/shard_map/all_gather | solution.py:1248
  8.7 102.8 %collective-permute-start = (bf16[512,1280]{1,0:T(8,128)(2,1)}, bf16[512,1280]{1,0:T(8,128)(2,1)S(1)}, u32[]{:S(2)}, u32[]{:S(2)}) collective-permute-start(bf16[512,1280]{1,0:T(8,128)(2,1)} %bitcast.20), channel_id=1, source_target_pairs={{0,1},{1,0},{2,3},{3,2},{4,5},{5,4},{6,7},{7,6},{8,9},{9,8},{10,11... | collective-permute-start | bytes 3932168 | tf_op jit(solution)/shard_map/ppermute | solution.py:1250
  103.9 1.0 copy-start.1
  111.4 1.1 copy-start.8
  210.3 124.2 %collective-permute-start.2 = (f32[16,1,512]{2,1,0:T(1,128)}, f32[16,1,512]{2,1,0:T(1,128)S(1)}, u32[]{:S(2)}, u32[]{:S(2)}) collective-permute-start(f32[16,1,512]{2,1,0:T(1,128)} %get-tuple-element.80.lse_ref), channel_id=1, source_target_pairs={{0,1},{1,0},{2,3},{3,2},{4,5},{5,4},{6,7},{7,6},{8,9},{9,8},{10,11... | collective-permute-start | bytes 98312 | tf_op jit(solution)/shard_map/ppermute | solution.py:1276
  303.8 30.7 %collective-permute-start.3 = (f32[16,1,512]{2,1,0:T(1,128)}, f32[16,1,512]{2,1,0:T(1,128)S(1)}, u32[]{:S(2)}, u32[]{:S(2)}) collective-permute-start(f32[16,1,512]{2,1,0:T(1,128)} %get-tuple-element.81.inner_ref), channel_id=1, source_target_pairs={{0,1},{1,0},{2,3},{3,2},{4,5},{5,4},{6,7},{7,6},{8,9},{9,8},{10,11... | collective-permute-start | bytes 98312 | tf_op jit(solution)/shard_map/ppermute | solution.py:1276
  305.0 30.0 %collective-permute-start.1 = (bf16[512,1280]{1,0:T(8,128)(2,1)}, bf16[512,1280]{1,0:T(8,128)(2,1)S(1)}, u32[]{:S(2)}, u32[]{:S(2)}) collective-permute-start(bf16[512,1280]{1,0:T(8,128)(2,1)} %get-tuple-element.79.grad_ref), channel_id=1, source_target_pairs={{0,1},{1,0},{2,3},{3,2},{4,5},{5,4},{6,7},{7,6},{8,9},{9,8},{10,11... | collective-permute-start | bytes 3932168 | tf_op jit(solution)/shard_map/ppermute | solution.py:1276
  334.5 0.6 copy-start.6
  334.5 0.6 copy-start.7
  335.0 1.1 copy-start.5
  350.8 28.4 %copy-start = (bf16[1,512,1280]{2,1,0:T(8,128)(2,1)S(1)}, bf16[1,512,1280]{2,1,0:T(8,128)(2,1)}, u32[]{:S(2)}) copy-start(bf16[1,512,1280]{2,1,0:T(8,128)(2,1)} %param.28) | copy-start | bytes 3932164
  350.8 28.4 %copy-start.2 = (bf16[512,256]{1,0:T(8,128)(2,1)S(1)}, bf16[512,256]{1,0:T(8,128)(2,1)}, u32[]{:S(2)}) copy-start(bf16[512,256]{1,0:T(8,128)(2,1)} %get-tuple-element.58.source.packs_ref) | copy-start | bytes 786436
  350.8 28.4 %copy-start.4 = (f32[1,1280]{1,0:T(1,128)S(1)}, f32[1,1280]{1,0:T(1,128)}, u32[]{:S(2)}) copy-start(f32[1,1280]{1,0:T(1,128)} %get-tuple-element.111.gain_ref) | copy-start | bytes 15364
  379.2 1.1 copy-start.3
Sparse Core Ops, SparseCore 0:
  10.9 134.3 all-gather.2
  148.1 106.3 all-gather.4

commit v5 on v4

--- a/solution.py
+++ b/solution.py
@@ -377,15 +377,13 @@
     if count:
         courier = Courier(lines, chunks, rows_of, sources, targets, *refs[2 * count + 8 :])
 
-        @pl.when(step == 0)
+        @pl.when(step == 3)
         def _():
             courier.greet()
             for number in range(len(chunks)):
                 courier.start(number)
 
-        pieces = act_ref.shape[0] // min(256, act_ref.shape[0])
-        places = [(part, piece, 7.0 / pieces) for part in range(3) for piece in range(pieces)]
-        places += [(3 + head, piece, 1.0) for head in range(HEADS) for piece in range(2)]
+        places = [(3 + head, piece, 1.0) for head in range(HEADS) for piece in range(2)]
         work = courier.steps()
         whole_time = sum(p[2] for p in places)
         done, spent = 0, 0.0

time: 399 us -> 394 us (0.987)
  no operation moved by 1% of the time
where the time goes in v5:
time: 394 us; the launch traced here: 389 us
  Pallas kernels  331 us (84%)
  waiting for transfers between devices  21.2 us (5%)
  local copies, waits for them, and re-layouts  16.9 us (4%)
  between operations  15.1 us (4%)
    pallas_call x1, Pallas kernels, front_call(): pl.pallas_call(functools.partial(front_kernel, lines, chunks, [a.shape[0]...  95.9 us
    pallas_call x1, Pallas kernels, collect(): pl.pallas_call(functools.partial(collect_kernel, lines, chunks, [a.shape[...  86.7 us
    pallas_call x1, Pallas kernels, feed_call(): pl.pallas_call(feed_kernel, name='feed', grid=(wide // block,), in_specs=...  49.3 us
    pallas_call x1, Pallas kernels, own_call(): pl.pallas_call(own_kernel, name='back_own', grid_spec=pltpu.PrefetchScala...  28.9 us
    pallas_call x1, Pallas kernels, close_call(): pl.pallas_call(functools.partial(close_kernel, (mesh_shape['dp'], mesh_sh...  28.6 us
    pallas_call x1, Pallas kernels, before_call(): pl.pallas_call(before_kernel, name='before', grid=(wide // block,), in_sp...  20.1 us
    all_gather x1, waiting for transfers between devices, per_device(): w_fc1 = lax.all_gather(fc1_weight, axes, axis=0, tiled=True)  19 us
    pallas_call x1, Pallas kernels, other_call(): pl.pallas_call(functools.partial(other_kernel, count - 1), name='back_oth...  14.8 us
  transfers between devices with their start and end apart: 6, of which 2 were waited for; matrix products, arithmetic and copies ran while one was open for 4% of the time, Pallas kernels for 72%

profile of v5, /device:TPU:15, one launch (start us, length us, event | category | flops | bytes accessed | tf_op | source)
XLA Modules:
  0.0 388.7 jit_solution(3838221053491566044)
XLA Ops:
  7.2 0.7 all-gather.3.cloned.1.call-update
  8.0 0.7 all-gather.5.cloned.1.call-update
  9.6 0.7 pad.48
  10.3 0.7 pad.49
  10.9 0.7 pad.50
  11.6 0.7 pad.51
  12.3 0.7 pad.52
  12.9 0.7 pad.53
  13.6 0.7 pad.54
  14.2 0.7 pad.55
  17.1 86.7 %collect.1 = (bf16[1280,3840]{1,0:T(8,128)(2,1)}, bf16[1280,128]{1,0:T(8,128)(2,1)}, bf16[3840,128]{1,0:T(8,128)(2,1)}, bf16[512,256]{1,0:T(8,128)(2,1)}) custom-call(bf16[40,3840]{1,0:T(8,128)(2,1)} %refs_0_.1, bf16[40,128]{1,0:T(8,128)(2,1)} %refs_1_.1, bf16[120,128]{1,0:T(8,128)(2,1)} %bitcast.28, bf16[16,256]{1,0:T(8,128)(2,1)} %pad.57.refs_3_), custom_call_target="tpu_custom_call" | custom-call | bytes 182452224 | tf_op jit(solution)/shard_map/collect/pallas_call | solution.py:283
  103.9 0.9 copy-done.1
  105.7 0.6 slice.38.b1_ref
  106.3 0.8 copy.38
  107.2 0.8 copy.39
  108.7 1.4 fusion.2.table_ref
  110.1 0.7 maximum_bitcast_fusion.table_ref
  110.8 0.6 fusion.3
  111.5 1.1 copy-done.8
  112.5 95.9 %front.1 = (bf16[3,16,1024,128]{3,2,1,0:T(8,128)(2,1)}, bf16[1024,128]{1,0:T(8,128)(2,1)}, bf16[512,1280]{1,0:T(8,128)(2,1)}, f32[16,1,512]{2,1,0:T(1,128)}, bf1...) custom-call(f32[1,1280]{1,0:T(1,128)} %get-tuple-element.111.gain_re, ...), custom_call_target="tpu_custom_call" | custom-call | flops 18656264192 | bytes 30801920 | tf_op jit(solution)/shard_map/front/pallas_call | solution.py:460
  208.6 1.5 constant_dynamic-slice_fusion.mid_ref
  210.1 20.1 %before.1 = (f32[512,1280]{1,0:T(8,128)}, bf16[512,1280]{1,0:T(8,128)(2,1)}, bf16[512,128]{1,0:T(8,128)(2,1)}, bf16[512,128]{1,0:T(8,128)(2,1)}, bf16[512,128]{1,0:T(8,128)(2,1)}, /*index=5*/f32[512,5120]{1,0:T(8,128)}) custom-call(bf16[512,1280]{1,0:T(8,128)(2,1)} %get-tuple-element.62.att_ref.refs_2_, bf16[512,1280]{1,0:T(8,128)(2,1)} %bitcast.22, ...), custom_call_target="tpu_custom_call" | custom-call | flops 8388608000 | bytes 34078720 | tf_op jit(solution)/shard_map/before/pallas_call | solution.py:762
  230.2 19.0 %all-gather.5.cloned.1.call-done.w1_ref = bf16[1280,5120]{1,0:T(8,128)(2,1)} async-done(((bf16[40,5120]{1,0:T(8,128)(2,1)}), bf16[1280,5120]{1,0:T(8,128)(2,1)}) %all-gather.5.cloned.1.call-update) | async-done | bytes 13107216 | tf_op jit(solution)/shard_map/all_gather | solution.py:1246
  249.2 49.3 %feed.1 = (bf16[512,1280]{1,0:T(8,128)(2,1)}, f32[512,1280]{1,0:T(8,128)}, bf16[512,1280]{1,0:T(8,128)(2,1)}, f32[16,1,512]{2,1,0:T(1,128)}, bf16[16,1280]{1,0:T...) custom-call(bf16[512,1280]{1,0:T(8,128)(2,1)} %get-tuple-element.69., ...), custom_call_target="tpu_custom_call" | custom-call | flops 20132659200 | bytes 52428800 | tf_op jit(solution)/shard_map/feed/pallas_call | solution.py:902
  298.5 1.3 collective-permute-start.3
  300.0 28.9 %back_own.1 = (bf16[512,1280]{1,0:T(8,128)(2,1)}, f32[16,512,128]{2,1,0:T(8,128)}, f32[16,512,128]{2,1,0:T(8,128)}) custom-call(s32[1]{0:T(128)} %bitcast.9.place_ref, bf16[3,16,1024,128]{3,2,1,0:T(8,128)(2,1)} %get-tuple-element.77.q_ref.k_ref.v_ref, bf16[16,1024,128]{2,1,0:T(8,128)(2,1)} %get-tuple-element.78.aux_ref, ...), custom_call_target="tpu_custom_call" | custom-call | flops 17179869184 | bytes 25165824 | tf_op jit(solution)/shard_map/back_own/pallas_call | solution.py:561
  328.9 0.8 collective-permute-done.1
  329.8 1.1 copy-done.5
  330.8 14.8 %back_other.1 = (bf16[512,1280]{1,0:T(8,128)(2,1)}, bf16[512,1280]{1,0:T(8,128)(2,1)}) custom-call(s32[1]{0:T(128)} %bitcast.9.place_ref, bf16[3,16,1024,128]{3,2,1,0:T(8,128)(2,1)} %get-tuple-element.77.q_ref.k_ref.v_ref, bf16[16,1024,128]{2,1,0:T(8,128)(2,1)} %get-tuple-element.78.aux_ref, bf16[3,16,1024,128]{3,2,1,0:T(8,128)(2,1)} %get-tuple-element.77.q_ref.k_ref.v_ref, ...), custom_call_target="tpu_custom_call" | custom-call | flops 4294967296 | bytes 25165824 | tf_op jit(solution)/shard_map/back_other/pallas_call | solution.py:667
  345.6 28.6 %close.1 = (f32[512,1280]{1,0:T(8,128)}, bf16[512,640]{1,0:T(8,128)(2,1)}) custom-call(bf16[512,1280]{1,0:T(8,128)(2,1)} %get-tuple-element.82.dq_ref, bf16[512,1280]{1,0:T(8,128)(2,1)} %get-tuple-element.85.dk_ref, bf16[512,1280]{1,0:T(8,128)(2,1)} %get-tuple-element.86.dv_ref, bf16[1280,3840]{1,0:T(8,128)(2,1)} %get-tuple-element.59.weight_ref, ...), custom_call_target="tpu_custom_call" | custom-call | flops 5033164800 | bytes 22937600 | tf_op jit(solution)/shard_map/close/pallas_call | solution.py:1082
  374.3 1.1 copy-done.3
  375.4 6.2 %last.1 = (f32[512,1280]{1,0:T(8,128)}, f32[40,128]{1,0:T(8,128)}, f32[40,128]{1,0:T(8,128)}, f32[40,128]{1,0:T(8,128)}, f32[160,128]{1,0:T(8,128)}, /*index=5*/...) custom-call(f32[512,1280]{1,0:T(8,128)} %get-tuple-element.94.upstream_ref, ...), custom_call_target="tpu_custom_call" | custom-call | tf_op jit(solution)/shard_map/last/pallas_call | solution.py:1138
  (42 shorter events, 4.7 us)
Async XLA Ops:
  7.2 203.0 %all-gather.3.cloned.1.call-start = ((), (), s32[]{:S(2)}) async-start(), calls=%async_computation | async-start | bytes 13516800 | tf_op jit(solution)/shard_map/all_gather | solution.py:1245
  7.9 241.3 %all-gather.5.cloned.1.call-start = ((), (), s32[]{:S(2)}) async-start(), calls=%async_computation.1 | async-start | bytes 13516800 | tf_op jit(solution)/shard_map/all_gather | solution.py:1246
  8.7 102.8 %collective-permute-start = (bf16[512,1280]{1,0:T(8,128)(2,1)}, bf16[512,1280]{1,0:T(8,128)(2,1)S(1)}, u32[]{:S(2)}, u32[]{:S(2)}) collective-permute-start(bf16[512,1280]{1,0:T(8,128)(2,1)} %bitcast.20), channel_id=1, source_target_pairs={{0,1},{1,0},{2,3},{3,2},{4,5},{5,4},{6,7},{7,6},{8,9},{9,8},{10,11... | collective-permute-start | bytes 3932168 | tf_op jit(solution)/shard_map/ppermute | solution.py:1248
  103.9 1.0 copy-start.1
  111.4 1.1 copy-start.8
  208.4 120.4 %collective-permute-start.2 = (f32[16,1,512]{2,1,0:T(1,128)}, f32[16,1,512]{2,1,0:T(1,128)S(1)}, u32[]{:S(2)}, u32[]{:S(2)}) collective-permute-start(f32[16,1,512]{2,1,0:T(1,128)} %get-tuple-element.80.lse_ref), channel_id=1, source_target_pairs={{0,1},{1,0},{2,3},{3,2},{4,5},{5,4},{6,7},{7,6},{8,9},{9,8},{10,11... | collective-permute-start | bytes 98312 | tf_op jit(solution)/shard_map/ppermute | solution.py:1274
  298.5 30.4 %collective-permute-start.3 = (f32[16,1,512]{2,1,0:T(1,128)}, f32[16,1,512]{2,1,0:T(1,128)S(1)}, u32[]{:S(2)}, u32[]{:S(2)}) collective-permute-start(f32[16,1,512]{2,1,0:T(1,128)} %get-tuple-element.81.inner_ref), channel_id=1, source_target_pairs={{0,1},{1,0},{2,3},{3,2},{4,5},{5,4},{6,7},{7,6},{8,9},{9,8},{10,11... | collective-permute-start | bytes 98312 | tf_op jit(solution)/shard_map/ppermute | solution.py:1274
  299.7 30.0 %collective-permute-start.1 = (bf16[512,1280]{1,0:T(8,128)(2,1)}, bf16[512,1280]{1,0:T(8,128)(2,1)S(1)}, u32[]{:S(2)}, u32[]{:S(2)}) collective-permute-start(bf16[512,1280]{1,0:T(8,128)(2,1)} %get-tuple-element.79.grad_ref), channel_id=1, source_target_pairs={{0,1},{1,0},{2,3},{3,2},{4,5},{5,4},{6,7},{7,6},{8,9},{9,8},{10,11... | collective-permute-start | bytes 3932168 | tf_op jit(solution)/shard_map/ppermute | solution.py:1274
  328.9 0.9 copy-start.6
  328.9 0.9 copy-start.7
  329.8 1.1 copy-start.5
  345.6 28.7 %copy-start = (bf16[1,512,1280]{2,1,0:T(8,128)(2,1)S(1)}, bf16[1,512,1280]{2,1,0:T(8,128)(2,1)}, u32[]{:S(2)}) copy-start(bf16[1,512,1280]{2,1,0:T(8,128)(2,1)} %param.28) | copy-start | bytes 3932164
  345.6 28.7 %copy-start.2 = (bf16[512,256]{1,0:T(8,128)(2,1)S(1)}, bf16[512,256]{1,0:T(8,128)(2,1)}, u32[]{:S(2)}) copy-start(bf16[512,256]{1,0:T(8,128)(2,1)} %get-tuple-element.58.source.packs_ref) | copy-start | bytes 786436
  345.6 28.7 %copy-start.4 = (f32[1,1280]{1,0:T(1,128)S(1)}, f32[1,1280]{1,0:T(1,128)}, u32[]{:S(2)}) copy-start(f32[1,1280]{1,0:T(1,128)} %get-tuple-element.111.gain_ref) | copy-start | bytes 15364
  374.3 1.1 copy-start.3
Sparse Core Ops, SparseCore 0:
  10.9 123.9 all-gather.2
  137.7 111.4 all-gather.4
